TPU v7x, 512 devices: a whole 4x8x8 slice. The times are simulated.
512 devices in a mesh: sec: 2 (over z_lo), gy: 16 (over x, z_hi), gx: 16 (over y, core).
Axes of the slice: x: 4, y: 8, z: 8 (z_hi: 4, z_lo: 2; z = z_hi * 2 + z_lo), core: 2. Of those that a mesh axis runs over, the one named last changes fastest.
Arguments:
- fields: float32 [2, 4, 1, 3072, 6144], P('sec', None, None, 'gy', 'gx'), may hold values from -6 to 6
- forcing: bfloat16 [2, 4, 1, 3072, 6144], P('sec', None, None, 'gy', 'gx'), may hold values from -4 to 4
- courant: float32 [2, 1], replicated, may hold values from -0.18 to 0.18
- diffusion: float32 [4], replicated, may hold values from 0.03 to 0.08
- nest_patch: int32 [16, 16], replicated, may hold values from 0 to 143, as said below
Outputs:
- fields_out: float32 [2, 4, 1, 3072, 6144], P('sec', None, None, 'gy', 'gx')
Inputs may be any that keep to these rules, and one draw needn't show every extreme that they name: Entry [i, j] names a patch of the parent device in row nest_patch[i, j] // 9 of device column j: patch row (nest_patch[i, j] % 9) // 3 and patch column nest_patch[i, j] % 3 of its 3 x 3 patches. That device row differs from i by at most one. Nests of one column lie on distinct patches; in every column some parent device lies under exactly three nests, and none under more.
All inputs are finite; a program needn't handle non-finite values.
Results may differ from a plain program's by a relative error of at most 0.0003.
Values sent between devices are 32-bit elements; how exact they have to be, the bound alone decides.
No kernel may reach another device: no remote copies, remote signals or barrier semaphores. Data moves between devices by JAX's collectives and lax.ppermute only.
A program may use at most 128 MiB of HBM per device.

v0:
```python
import functools

import jax
import jax.numpy as jnp
from jax import lax
from jax.experimental import pallas as pl
from jax.experimental.pallas import tpu as pltpu
from jax.sharding import PartitionSpec as P


F32 = jnp.float32
BF16 = jnp.bfloat16
V, H, W = 4, 192, 384
PH, PW = H // 3, W // 3
CHUNK = 16
OFF = 160


def beside(n):
    inner = (n - 1, n, 2 * n - 1, 2 * n)
    return inner, (0, 1, n - 2, n - 1, n, n + 1, 2 * n - 2, 2 * n - 1, 2 * n, 2 * n + 1, 3 * n - 2, 3 * n - 1)


IN_ROWS, BANK_ROWS = beside(PH)
IN_COLS, BANK_COLS = beside(PW)
FORCE_COLS = (0, *IN_COLS, W - 1)
AXES = ("sec", "gy", "gx")
SMEM = pl.BlockSpec(memory_space=pltpu.SMEM)
VMEM = pl.BlockSpec(memory_space=pltpu.VMEM)
ANY = pl.BlockSpec(memory_space=pl.ANY)


def iota(shape, dim):
    return lax.broadcasted_iota(jnp.int32, shape, dim)


def split3(a):
    high = a.astype(BF16)
    rest = a - high.astype(F32)
    middle = rest.astype(BF16)
    low = (rest - middle.astype(F32)).astype(BF16)
    return high, middle, low


def dot_right(a, m):
    return sum(jnp.dot(part, m, preferred_element_type=F32) for part in split3(a))


def dot_nt(m, a):
    dims = (((1,), (1,)), ((), ()))
    return sum(lax.dot_general(m, part, dims, preferred_element_type=F32) for part in split3(a))


def dot_left(m, a):
    return sum(jnp.dot(m, part, preferred_element_type=F32) for part in split3(a))


def select_rows(picks, width):
    row, lane = iota((16, width), 0), iota((16, width), 1)
    wanted = jnp.full((16, width), -1, jnp.int32)
    for i, pick in enumerate(picks):
        wanted = jnp.where(row == i, pick, wanted)
    return jnp.where(lane == wanted, 1.0, 0.0).astype(BF16)


def weights(k, courant):
    half_x = 0.5 * courant[0]
    half_y = 0.5 * courant[1]
    return 1.0 - 4.0 * k, k - half_x, k + half_x, k - half_y, k + half_y


def per_field(diffusion, scale, shape, dim, groups):
    index = iota(shape, dim)
    out = jnp.zeros(shape, F32)
    for g in range(groups):
        for f in range(V):
            out = jnp.where(index == g * V + f, scale * diffusion[f], out)
    return out


def near(*values):
    return [pltpu.with_memory_space_constraint(v, pltpu.VMEM) for v in values]


def position():
    return [lax.axis_index(axis) for axis in AXES]


def edge_kernel(x, drive, down, up, x_top, x_bottom, d_top, d_bottom, sems):
    copies = [
        pltpu.make_async_copy(x.at[:, 0:8, :], x_top, sems.at[0]),
        pltpu.make_async_copy(x.at[:, H - 8 : H, :], x_bottom, sems.at[1]),
        pltpu.make_async_copy(drive.at[:, 0:16, :], d_top, sems.at[2]),
        pltpu.make_async_copy(drive.at[:, H - 16 : H, :], d_bottom, sems.at[3]),
    ]
    for copy in copies:
        copy.start()
    for copy in copies:
        copy.wait()
    for f in range(V):
        down[0, f : f + 1] = x_bottom[f, 7:8, :]
        down[1, f : f + 1] = x_bottom[f, 6:7, :]
        down[2, f : f + 1] = d_bottom[f].astype(F32)[15:16]
        up[0, f : f + 1] = x_top[f, 0:1, :]
        up[1, f : f + 1] = x_top[f, 1:2, :]
        up[2, f : f + 1] = d_top[f].astype(F32)[0:1]


def edge(x, drive):
    shape = pltpu.VMEM((3, V, W), F32)
    return pl.pallas_call(
        edge_kernel,
        in_specs=[ANY, ANY],
        out_specs=[VMEM, VMEM],
        out_shape=[shape, shape],
        scratch_shapes=[
            pltpu.VMEM((V, 8, W), F32),
            pltpu.VMEM((V, 8, W), F32),
            pltpu.VMEM((V, 16, W), BF16),
            pltpu.VMEM((V, 16, W), BF16),
            pltpu.SemaphoreType.DMA((4,)),
        ],
        name="edge",
    )(x, drive)


def first_kernel(
    courant, diffusion, x, drive, y, mean, rows, cols, one, two, source, force, thirds, sems
):
    parent = position()[0] == 0
    scale = jnp.where(parent, 1.0, 3.0)
    lane = iota((1, W), 1)

    def load(f):
        return (
            pltpu.make_async_copy(x.at[f], one.at[f, 8 : 8 + H, :], sems.at[0, f]),
            pltpu.make_async_copy(drive.at[f], source.at[f], sems.at[1, f]),
        )

    for f in range(V):
        for copy in load(f):
            copy.start()
    for f in range(V):
        one[f, 0:8, :] = jnp.zeros((8, W), F32)
        one[f, H + 8 : H + 16, :] = jnp.zeros((8, W), F32)
    two[0:8, :] = jnp.zeros((8, W), F32)
    two[H + 8 : H + 16, :] = jnp.zeros((8, W), F32)

    def field(f, steps):
        a0, ae, aw, as_, an = weights(diffusion[f] * scale, courant)
        east = jnp.where(lane == W - 1, 0.0, ae)
        west = jnp.where(lane == 0, 0.0, aw)

        def step(old, new, at):
            for r in range(0, H, CHUNK):
                centre = old[8 + r : 8 + r + CHUNK, :]
                north = old[7 + r : 7 + r + CHUNK, :]
                south = old[9 + r : 9 + r + CHUNK, :]
                new[at + r : at + r + CHUNK, :] = (
                    a0 * centre
                    + east * pltpu.roll(centre, W - 1, 1)
                    + west * pltpu.roll(centre, 1, 1)
                    + as_ * south
                    + an * north
                    + force[r : r + CHUNK, :]
                )

        force[...] = source[f].astype(F32) * jnp.where(parent, 1.0, 1.0 / 3.0)
        mine = one.at[f]
        if steps == 3:
            step(mine, two, 8)
            step(two, mine, 8)
        step(mine, y.at[f], 0)

    @pl.when(parent)
    def _():
        cols[...] = jnp.zeros(cols.shape, F32)
        picks, force_picks = select_rows(BANK_COLS, W), select_rows(FORCE_COLS, W)
        dims = (((1,), (1,)), ((), ()))
        for f in range(V):
            for copy in load(f):
                copy.wait()
            for i, r in enumerate(BANK_ROWS):
                rows[i, f : f + 1] = one[f, 8 + r : 9 + r, :]
            for i, r in enumerate(IN_ROWS):
                band = source[f, r // 16 * 16 : r // 16 * 16 + 16, :].astype(F32)
                rows[12 + i, f : f + 1] = band[r % 16 : r % 16 + 1]
            from_x = dot_nt(picks, one[f, 8 : 8 + H, :])
            from_drive = lax.dot_general(
                force_picks, source[f], dims, preferred_element_type=F32
            )
            for i in range(12):
                cols[i, f : f + 1, 0:H] = from_x[i : i + 1]
            for i in range(6):
                cols[12 + i, f : f + 1, 0:H] = from_drive[i : i + 1]

        @pl.loop(0, V)
        def _(f):
            field(f, 1)

    @pl.when(jnp.logical_not(parent))
    def _():
        blocks = mean_matrix()

        @pl.loop(0, V)
        def _(f):
            for copy in load(f):
                copy.wait()
            field(f, 3)
            thirds[...] = dot_right(y[f], blocks)
            total = (
                thirds[pl.ds(0, PH, stride=3), :]
                + thirds[pl.ds(1, PH, stride=3), :]
                + thirds[pl.ds(2, PH, stride=3), :]
            )
            mean[f] = total * (1.0 / 9.0)


def mean_matrix():
    gap = iota((W, PW), 0) - 3 * iota((W, PW), 1)
    return jnp.where((gap >= 0) & (gap <= 2), 1.0, 0.0).astype(BF16)


def first(courant, diffusion, x, drive):
    return pl.pallas_call(
        first_kernel,
        in_specs=[SMEM, SMEM, ANY, ANY],
        out_specs=[VMEM] * 4,
        out_shape=[
            pltpu.VMEM((V, H, W), F32),
            pltpu.VMEM((V, PH, PW), F32),
            pltpu.VMEM((16, V, W), F32),
            pltpu.VMEM((18, V, 256), F32),
        ],
        scratch_shapes=[
            pltpu.VMEM((V, H + 16, W), F32),
            pltpu.VMEM((H + 16, W), F32),
            pltpu.VMEM((V, H, W), BF16),
            pltpu.VMEM((H, W), F32),
            pltpu.VMEM((H, PW), F32),
            pltpu.SemaphoreType.DMA((2, V)),
        ],
        cost_estimate=pl.CostEstimate(flops=40_000_000, transcendentals=0, bytes_accessed=20_000_000),
        name="first",
    )(courant, diffusion, x, drive)


def pack_kernel(cols, north, south, to_west, to_east):
    for out, picks, lo in ((to_west, (0, 1, 12), 0), (to_east, (11, 10, 17), W - 128)):
        for i, pick in enumerate(picks):
            out[i] = cols[pick]
        out[3, :, 0:128] = north[0, :, lo : lo + 128]
        out[3, :, 128:256] = north[1, :, lo : lo + 128]
        out[4, :, 0:128] = north[2, :, lo : lo + 128]
        out[4, :, 128:256] = south[2, :, lo : lo + 128]
        out[5, :, 0:128] = south[0, :, lo : lo + 128]
        out[5, :, 128:256] = south[1, :, lo : lo + 128]


def pack(cols, north, south):
    shape = pltpu.VMEM((6, V, 256), F32)
    return pl.pallas_call(
        pack_kernel,
        in_specs=[VMEM] * 3,
        out_specs=[VMEM] * 2,
        out_shape=[shape, shape],
        name="pack",
    )(*near(cols, north, south))


def role_slot(nest_patch, row, column, member, count):
    nest = jnp.clip(row + member - 1, 0, count - 1)
    return nest_patch[nest, column]


def rims_kernel(
    courant, diffusion, nest_patch, rows, cols, north, south, west, east, *out_bank_side
):
    *out, bank, side = out_bank_side
    section, row, column = position()
    count, columns = nest_patch.shape

    @pl.when(section == 0)
    def _():
        k = per_field(diffusion, 1.0, (V, 1), 0, 1)
        a0, ae, aw, as_, an = weights(k, courant)
        has_n = jnp.where(row > 0, 1.0, 0.0)
        has_s = jnp.where(row < count - 1, 1.0, 0.0)
        has_w = jnp.where(column > 0, 1.0, 0.0)
        has_e = jnp.where(column < columns - 1, 1.0, 0.0)
        lane128 = iota((V, 128), 1)
        lane256 = iota((V, 256), 1)
        wide = W + 256
        lane_wide = iota((V, wide), 1)
        keep = jnp.where(lane_wide < 128, has_w, jnp.where(lane_wide >= 128 + W, has_e, 1.0))
        near_w, near_e = west[0], east[0]

        def join(before, middle, after):
            return jnp.concatenate([before, middle, after], axis=1)

        def with_sides(middle, left, right):
            return join(
                jnp.where(lane128 == 127, left, 0.0), middle, jnp.where(lane128 == 0, right, 0.0)
            )

        def lanes(value, at):
            return value[:, at : at + 1]

        def halo_row(near, far, force, inner, a_far, a_inner, exists):
            value = (
                a0 * near
                + ae * pltpu.roll(near, wide - 1, 1)
                + aw * pltpu.roll(near, 1, 1)
                + a_far * far
                + a_inner * inner
                + force
            )
            return value * keep * exists

        north_1 = join(west[3, :, 0:128], north[0], east[3, :, 0:128])
        north_2 = join(west[3, :, 128:256], north[1], east[3, :, 128:256])
        north_f = join(west[4, :, 0:128], north[2], east[4, :, 0:128])
        south_1 = join(west[5, :, 0:128], south[0], east[5, :, 0:128])
        south_2 = join(west[5, :, 128:256], south[1], east[5, :, 128:256])
        south_f = join(west[4, :, 128:256], south[2], east[4, :, 128:256])
        top = with_sides(rows[0], lanes(near_w, 0), lanes(near_e, 0))
        bottom = with_sides(rows[11], lanes(near_w, H - 1), lanes(near_e, H - 1))
        new_north = halo_row(north_1, north_2, north_f, top, an, as_, has_n)
        new_south = halo_row(south_1, south_2, south_f, bottom, as_, an, has_s)

        def with_ends(column_values, before, after):
            return jnp.where(
                lane256 == 255, before, jnp.where(lane256 == H, after, column_values)
            )

        def halo_column(near, far, force, inner, a_far, a_inner, exists, at):
            full = with_ends(near, lanes(north_1, at), lanes(south_1, at))
            value = (
                a0 * full
                + as_ * pltpu.roll(full, 255, 1)
                + an * pltpu.roll(full, 1, 1)
                + a_far * far
                + a_inner * inner
                + force
            )
            new = with_ends(value * exists, lanes(new_north, at), lanes(new_south, at))
            return full, new

        at_w, at_e = 127, 128 + W
        old_west, new_west = halo_column(near_w, west[1], west[2], cols[0], aw, ae, has_w, at_w)
        old_east, new_east = halo_column(near_e, east[1], east[2], cols[11], ae, aw, has_e, at_e)

        bank[0, 0] = north_1
        bank[1, 0] = new_north
        bank[0, 5] = south_1
        bank[1, 5] = new_south
        blank = jnp.zeros((V, 128), F32)
        for i, r in enumerate(IN_ROWS):
            place, at = (1, 3, 2, 4)[i], BANK_ROWS.index(r)
            old = with_sides(rows[at], lanes(near_w, r), lanes(near_e, r))
            bank[0, place] = old
            new = (
                a0 * old
                + ae * pltpu.roll(old, wide - 1, 1)
                + aw * pltpu.roll(old, 1, 1)
                + join(blank, an * rows[at - 1] + as_ * rows[at + 1] + rows[12 + i], blank)
            )
            bank[1, place] = jnp.where(
                lane_wide == 127,
                lanes(new_west, r),
                jnp.where(lane_wide == 128 + W, lanes(new_east, r), new),
            )
        side[0, 0] = old_west
        side[1, 0] = new_west
        side[0, 5] = old_east
        side[1, 5] = new_east
        for i, c in enumerate(IN_COLS):
            place, at = (1, 3, 2, 4)[i], BANK_COLS.index(c)
            old, new = halo_column(
                cols[at], cols[at - 1], cols[12 + FORCE_COLS.index(c)], cols[at + 1], aw, ae, 1.0, 128 + c
            )
            side[0, place] = old
            side[1, place] = new

        for member in range(3):
            slot = lax.rem(role_slot(nest_patch, row, column, member, count), 9)
            patch_row, patch_col = lax.div(slot, 3), lax.rem(slot, 3)
            start = pl.multiple_of(patch_col * PW, PW)
            shift = OFF + 1 - PH * patch_row
            for time in range(2):
                for half in range(2):
                    rim = bank[time, patch_row + 3 * half, :, pl.ds(start, 384)]
                    rim = pltpu.roll(rim, 384 - 127, 1)[:, 0:256]
                    flank = pltpu.roll(side[time, patch_col + 3 * half], shift, 1)
                    flank = jnp.where((lane256 >= OFF) & (lane256 < OFF + PH + 2), flank, 0.0)
                    place = (2 * time + half) * V
                    out[member][place : place + V, :] = jnp.where(lane256 < PW + 2, rim, flank)


def rims(courant, diffusion, nest_patch, rows, cols, north, south, west, east):
    return pl.pallas_call(
        rims_kernel,
        in_specs=[SMEM] * 3 + [VMEM] * 6,
        out_specs=[VMEM] * 3,
        out_shape=[pltpu.VMEM((4 * V, 256), F32)] * 3,
        scratch_shapes=[pltpu.VMEM((2, 6, V, W + 256), F32), pltpu.VMEM((2, 6, V, 256), F32)],
        name="rims",
    )(courant, diffusion, nest_patch, *near(rows, cols, north, south, west, east))


def edge_effect(u, courant, diffusion):
    k_row = per_field(diffusion, 3.0, (2 * V, 1), 0, 2)
    a0, ae, aw, as_, an = weights(k_row, courant)
    upper = iota((2 * V, 1), 0) < V
    outer, inner = jnp.where(upper, an, as_), jnp.where(upper, as_, an)
    lane = iota((2 * V, W), 1)
    east = jnp.where(lane == W - 1, 0.0, ae)
    west = jnp.where(lane == 0, 0.0, aw)
    tent = jnp.maximum(3 - jnp.abs(iota((256, W), 1) - 3 * iota((256, W), 0) + 2), 0)
    edges = dot_right(u, tent.astype(F32).astype(BF16)) * (1.0 / 3.0)
    old, new = edges[0 : 2 * V], edges[2 * V : 4 * V]

    def along_row(v):
        return a0 * v + east * pltpu.roll(v, W - 1, 1) + west * pltpu.roll(v, 1, 1)

    row_effect = depths(old, new, outer, inner, along_row)

    k_col = per_field(diffusion, 3.0, (1, 2 * V), 1, 2)
    a0, ae, aw, as_, an = weights(k_col, courant)
    left = iota((1, 2 * V), 1) < V
    outer, inner = jnp.where(left, aw, ae), jnp.where(left, ae, aw)
    down = iota((H, 2 * V), 0)
    south = jnp.where(down == H - 1, 0.0, as_)
    north = jnp.where(down == 0, 0.0, an)
    tent = jnp.maximum(3 - jnp.abs(iota((H, 256), 0) - 3 * (iota((H, 256), 1) - OFF) + 2), 0)
    tent = tent.astype(F32).astype(BF16)
    old = dot_nt(tent, u[0 : 2 * V]) * (1.0 / 3.0)
    new = dot_nt(tent, u[2 * V : 4 * V]) * (1.0 / 3.0)

    def along_column(v):
        return a0_col * v + south * pltpu.roll(v, H - 1, 0) + north * pltpu.roll(v, 1, 0)

    a0_col = a0
    return row_effect, depths(old, new, outer, inner, along_column)


def depths(old, new, outer, inner, along):
    third = (new - old) * (1.0 / 3.0)
    first_0 = outer * old
    second_0 = along(first_0) + outer * (old + third)
    second_1 = outer * first_0
    third_0 = along(second_0) + inner * second_1 + outer * (old + 2.0 * third)
    third_1 = along(second_1) + outer * second_0
    third_2 = outer * second_1
    return third_0, third_1, third_2


def spread(values, depth):
    block, lane = iota((2 * V, 2 * V * 128), 0), iota((2 * V, 2 * V * 128), 1)
    target = block * 128 + jnp.where(block < V, depth, 127 - depth)
    return dot_right(values, jnp.where(lane == target, 1.0, 0.0).astype(BF16))


def last_kernel(
    courant, diffusion, nest_patch, y, north, south, west, east,
    sent_0, sent_1, sent_2, got_0, got_1, got_2, mean_0, mean_1, mean_2, out, tile, sems,
):
    section, row, column = position()
    count = nest_patch.shape[0]
    parent = section == 0
    sent, got, means = (sent_0, sent_1, sent_2), (got_0, got_1, got_2), (mean_0, mean_1, mean_2)

    def sides(f, both):
        tile[f, :, 0:128] = y[f, :, 0:128] + both[:, f * 128 : (f + 1) * 128]
        tile[f, :, 128 : W - 128] = y[f, :, 128 : W - 128]
        right = (V + f) * 128
        tile[f, :, W - 128 : W] = y[f, :, W - 128 : W] + both[:, right : right + 128]

    def send(f):
        return pltpu.make_async_copy(tile.at[f], out.at[f], sems.at[f])

    @pl.when(parent)
    def _():
        _, ae, aw, _, _ = weights(per_field(diffusion, 1.0, (1, 2 * V), 1, 2), courant)
        eye = jnp.where(iota((H, H), 0) == iota((H, H), 1), 1.0, 0.0).astype(BF16)
        beyond = jnp.concatenate([west[0, :, 0:H], east[0, :, 0:H]], axis=0)
        outer = jnp.where(iota((1, 2 * V), 1) < V, aw, ae)
        both = spread(dot_nt(eye, beyond) * outer, 0)
        for f in range(V):
            _, _, _, as_, an = weights(diffusion[f], courant)
            sides(f, both)
            tile[f, 0:1, :] = tile[f, 0:1, :] + an * north[0, f : f + 1, :]
            tile[f, H - 1 : H, :] = tile[f, H - 1 : H, :] + as_ * south[0, f : f + 1, :]
        thirds = iota((PH, H), 1) - 3 * iota((PH, H), 0)
        thirds = jnp.where((thirds >= 0) & (thirds <= 2), 1.0, 0.0).astype(BF16)
        line = iota((PH, PW), 0)
        for member in range(3):
            nest = row + member - 1
            entry = role_slot(nest_patch, row, column, member, count)
            slot = lax.rem(entry, 9)

            @pl.when((nest >= 0) & (nest < count) & (lax.div(entry, 9) == row))
            def _(member=member, slot=slot):
                at_row = pl.multiple_of(lax.div(slot, 3) * PH, PH)
                at_col = pl.multiple_of(lax.rem(slot, 3) * PW, PW)
                row_effect, col_effect = edge_effect(sent[member][...], courant, diffusion)
                by_row = dot_right(sum(row_effect), mean_matrix()) * (1.0 / 9.0)
                by_col = spread(dot_left(thirds, sum(col_effect)) * (1.0 / 9.0), 0)
                for f in range(V):
                    right = (V + f) * 128
                    tile[f, pl.ds(at_row, PH), pl.ds(at_col, PW)] = (
                        means[member][f]
                        + jnp.where(line == 0, by_row[f : f + 1], 0.0)
                        + jnp.where(line == PH - 1, by_row[V + f : V + f + 1], 0.0)
                        + by_col[:, f * 128 : (f + 1) * 128]
                        + by_col[:, right : right + 128]
                    )

        for f in range(V):
            send(f).start()

    @pl.when(jnp.logical_not(parent))
    def _():
        member = row - lax.div(nest_patch[row, column], 9) + 1
        u = jnp.where(member == 0, got[0][...], jnp.where(member == 1, got[1][...], got[2][...]))
        row_effect, col_effect = edge_effect(u, courant, diffusion)
        both = sum(spread(col_effect[depth], depth) for depth in range(3))
        for f in range(V):
            sides(f, both)
            for depth in range(3):
                bottom = H - 1 - depth
                tile[f, depth : depth + 1, :] = (
                    tile[f, depth : depth + 1, :] + row_effect[depth][f : f + 1]
                )
                tile[f, bottom : bottom + 1, :] = (
                    tile[f, bottom : bottom + 1, :] + row_effect[depth][V + f : V + f + 1]
                )
            send(f).start()

    for f in range(V):
        send(f).wait()


def last(courant, diffusion, nest_patch, y, north, south, west, east, sent, got, means):
    return pl.pallas_call(
        last_kernel,
        in_specs=[SMEM] * 3 + [VMEM] * 14,
        out_specs=ANY,
        out_shape=jax.ShapeDtypeStruct((V, H, W), F32),
        scratch_shapes=[pltpu.VMEM((V, H, W), F32), pltpu.SemaphoreType.DMA((V,))],
        name="last",
    )(
        courant, diffusion, nest_patch,
        *near(y, north, south, west, east, *sent, *got, *means),
    )


def routes(sizes, source, move):
    _, n_rows, n_cols = sizes
    out = []
    for r in range(n_rows):
        for c in range(n_cols):
            to_sec, to_r, to_c = move(r, c)
            if 0 <= to_r < n_rows and 0 <= to_c < n_cols:
                out.append(
                    (
                        (source * n_rows + r) * n_cols + c,
                        (to_sec * n_rows + to_r) * n_cols + to_c,
                    )
                )
    return out


def on_device(sizes, *arrays):
    return compute(sizes, *arrays)


def compute(sizes, fields, forcing, courant, diffusion, nest_patch):
    x = fields.reshape(V, H, W)
    drive = forcing.reshape(V, H, W)
    courant = courant.reshape(2)

    def shift(value, source, move):
        return lax.ppermute(value, AXES, routes(sizes, source, move))

    downward, upward = edge(x, drive)
    north = shift(downward, 0, lambda r, c: (0, r + 1, c))
    south = shift(upward, 0, lambda r, c: (0, r - 1, c))
    y, mean, rows, cols = first(courant, diffusion, x, drive)
    to_west, to_east = pack(cols, north, south)
    west = shift(to_east, 0, lambda r, c: (0, r, c + 1))
    east = shift(to_west, 0, lambda r, c: (0, r, c - 1))
    means = [shift(mean, 1, lambda r, c, m=m: (0, r + 1 - m, c)) for m in range(3)]
    sent = rims(courant, diffusion, nest_patch, rows, cols, north, south, west, east)
    got = [shift(sent[m], 0, lambda r, c, m=m: (1, r + m - 1, c)) for m in range(3)]
    out = last(courant, diffusion, nest_patch, y, north, south, west, east, sent, got, means)
    return out.reshape(fields.shape)


def solution(mesh):
    sizes = tuple(mesh.shape[axis] for axis in AXES)
    spec = P("sec", None, None, "gy", "gx")
    return jax.shard_map(
        functools.partial(on_device, sizes),
        mesh=mesh,
        in_specs=(spec, spec, P(), P(), P()),
        out_specs=spec,
        check_vma=False,
    )
```

profile of v0, /device:TPU:95, one launch (start us, length us, event | category | flops | bytes accessed | tf_op | source)
XLA Modules:
  0.0 53.4 jit_solution(13085401379425161257)
XLA Ops:
  0.0 5.4 %first.1 = (f32[4,192,384]{2,1,0:T(8,128)S(1)}, f32[4,64,128]{2,1,0:T(8,128)S(1)}, f32[16,4,384]{2,1,0:T(4,128)S(1)}, f32[18,4,256]{2,1,0:T(4,128)S(1)}) custom-call(f32[2]{0:T(128)} %bitcast.10, f32[4]{0:T(128)} %diffusion.5, f32[4,192,384]{2,1,0:T(8,128)} %bitcast.6, bf16[4,192,384]{2,1,0:T(8,128)(2,1)} %bitcast.8), custom_call_target="tpu_custom_call" | custom-call | flops 40000000 | bytes 20000000 | tf_op jit(solution)/shard_map/first/pallas_call | solution.py:225
  5.4 9.1 %collective-permute-start.9 = (f32[4,64,128]{2,1,0:T(8,128)S(1)}, f32[4,64,128]{2,1,0:T(8,128)S(1)}, u32[]{:S(2)}, u32[]{:S(2)}) collective-permute-start(f32[4,64,128]{2,1,0:T(8,128)S(1)} %get-tuple-element.26), channel_id=1, source_target_pairs={{272,0},{273,1},{274,2},{275,3},{276,4},{277,5},{278,6},{279,7},{2... | collective-permute-start | bytes 393224 | tf_op jit(solution)/shard_map/ppermute | solution.py:584
  14.5 1.3 %collective-permute-start.8 = (f32[4,64,128]{2,1,0:T(8,128)S(1)}, f32[4,64,128]{2,1,0:T(8,128)S(1)}, u32[]{:S(2)}, u32[]{:S(2)}) collective-permute-start(f32[4,64,128]{2,1,0:T(8,128)S(1)} %get-tuple-element.26), channel_id=1, source_target_pairs={{256,0},{257,1},{258,2},{259,3},{260,4},{261,5},{262,6},{263,7},{2... | collective-permute-start | bytes 393224 | tf_op jit(solution)/shard_map/ppermute | solution.py:584
  15.8 1.3 %collective-permute-start.7 = (f32[4,64,128]{2,1,0:T(8,128)S(1)}, f32[4,64,128]{2,1,0:T(8,128)S(1)}, u32[]{:S(2)}, u32[]{:S(2)}) collective-permute-start(f32[4,64,128]{2,1,0:T(8,128)S(1)} %get-tuple-element.26), channel_id=1, source_target_pairs={{256,16},{257,17},{258,18},{259,19},{260,20},{261,21},{262,22},{26... | collective-permute-start | bytes 393224 | tf_op jit(solution)/shard_map/ppermute | solution.py:584
  17.1 0.9 %edge.1 = (f32[3,4,384]{2,1,0:T(4,128)S(1)}, f32[3,4,384]{2,1,0:T(4,128)S(1)}) custom-call(f32[4,192,384]{2,1,0:T(8,128)} %bitcast.7, bf16[4,192,384]{2,1,0:T(8,128)(2,1)} %bitcast.9), custom_call_target="tpu_custom_call" | custom-call | tf_op jit(solution)/shard_map/edge/pallas_call | solution.py:111
  18.1 0.7 %collective-permute-start = (f32[3,4,384]{2,1,0:T(4,128)S(1)}, f32[3,4,384]{2,1,0:T(4,128)S(1)}, u32[]{:S(2)}, u32[]{:S(2)}) collective-permute-start(f32[3,4,384]{2,1,0:T(4,128)S(1)} %get-tuple-element.17), channel_id=1, source_target_pairs={{0,16},{1,17},{2,18},{3,19},{4,20},{5,21},{6,22},{7,23},{8,24},{9,... | collective-permute-start | bytes 55304 | tf_op jit(solution)/shard_map/ppermute | solution.py:584
  18.7 0.7 %collective-permute-start.1 = (f32[3,4,384]{2,1,0:T(4,128)S(1)}, f32[3,4,384]{2,1,0:T(4,128)S(1)}, u32[]{:S(2)}, u32[]{:S(2)}) collective-permute-start(f32[3,4,384]{2,1,0:T(4,128)S(1)} %get-tuple-element.18), channel_id=1, source_target_pairs={{16,0},{17,1},{18,2},{19,3},{20,4},{21,5},{22,6},{23,7},{24,8},{25... | collective-permute-start | bytes 55304 | tf_op jit(solution)/shard_map/ppermute | solution.py:584
  19.4 0.0 collective-permute-done.north
  19.4 0.0 collective-permute-done.1.south
  19.5 0.7 %collective-permute-start.2 = (f32[6,4,256]{2,1,0:T(4,128)S(1)}, f32[6,4,256]{2,1,0:T(4,128)S(1)}, u32[]{:S(2)}, u32[]{:S(2)}) collective-permute-start(f32[6,4,256]{2,1,0:T(4,128)S(1)} %get-tuple-element.20), channel_id=1, source_target_pairs={{0,1},{1,2},{2,3},{3,4},{4,5},{5,6},{6,7},{7,8},{8,9},{9,10},{10,1... | collective-permute-start | bytes 73736 | tf_op jit(solution)/shard_map/ppermute | solution.py:584
  20.1 0.7 %collective-permute-start.3 = (f32[6,4,256]{2,1,0:T(4,128)S(1)}, f32[6,4,256]{2,1,0:T(4,128)S(1)}, u32[]{:S(2)}, u32[]{:S(2)}) collective-permute-start(f32[6,4,256]{2,1,0:T(4,128)S(1)} %get-tuple-element.21), channel_id=1, source_target_pairs={{1,0},{2,1},{3,2},{4,3},{5,4},{6,5},{7,6},{8,7},{9,8},{10,9},{11,1... | collective-permute-start | bytes 73736 | tf_op jit(solution)/shard_map/ppermute | solution.py:584
  20.8 0.0 collective-permute-done.2.west
  20.8 0.0 collective-permute-done.3.east
  20.8 0.8 %rims.1 = (f32[16,256]{1,0:T(8,128)S(1)}, f32[16,256]{1,0:T(8,128)S(1)}, f32[16,256]{1,0:T(8,128)S(1)}) custom-call(f32[2]{0:T(128)} %bitcast.11, f32[4]{0:T(128)} %diffusion.5, s32[16,16]{1,0:T(8,128)} %nest_patch.3, f32[16,4,384]{2,1,0:T(4,128)S(1)} %get-tuple-element.22.rows, f32[18,4,256]{2,1,0:T(4,128)S(1)} %get-tuple-element.19.cols, ...), custom_call_target="tpu_custom_call" | custom-call | tf_op jit(solution)/shard_map/rims/pallas_call | solution.py:401
  21.7 1.3 %collective-permute-start.4 = (f32[16,256]{1,0:T(8,128)S(1)}, f32[16,256]{1,0:T(8,128)S(1)}, u32[]{:S(2)}, u32[]{:S(2)}) collective-permute-start(f32[16,256]{1,0:T(8,128)S(1)} %get-tuple-element.23.sent_0), channel_id=1, source_target_pairs={{16,256},{17,257},{18,258},{19,259},{20,260},{21,261},{22,262},{23... | collective-permute-start | bytes 49160 | tf_op jit(solution)/shard_map/ppermute | solution.py:584
  23.0 1.3 %collective-permute-start.5 = (f32[16,256]{1,0:T(8,128)S(1)}, f32[16,256]{1,0:T(8,128)S(1)}, u32[]{:S(2)}, u32[]{:S(2)}) collective-permute-start(f32[16,256]{1,0:T(8,128)S(1)} %get-tuple-element.24.sent_1), channel_id=1, source_target_pairs={{0,256},{1,257},{2,258},{3,259},{4,260},{5,261},{6,262},{7,263},{8... | collective-permute-start | bytes 49160 | tf_op jit(solution)/shard_map/ppermute | solution.py:584
  24.3 17.3 %collective-permute-done.4.got_0 = f32[16,256]{1,0:T(8,128)S(1)} collective-permute-done((f32[16,256]{1,0:T(8,128)S(1)}, f32[16,256]{1,0:T(8,128)S(1)}, u32[]{:S(2)}, u32[]{:S(2)}) %collective-permute-start.4) | collective-permute-done | bytes 16416 | tf_op jit(solution)/shard_map/ppermute | solution.py:584
  41.6 1.3 %collective-permute-start.6 = (f32[16,256]{1,0:T(8,128)S(1)}, f32[16,256]{1,0:T(8,128)S(1)}, u32[]{:S(2)}, u32[]{:S(2)}) collective-permute-start(f32[16,256]{1,0:T(8,128)S(1)} %get-tuple-element.25.sent_2), channel_id=1, source_target_pairs={{0,272},{1,273},{2,274},{3,275},{4,276},{5,277},{6,278},{7,279},{8... | collective-permute-start | bytes 49160 | tf_op jit(solution)/shard_map/ppermute | solution.py:584
  42.8 0.0 collective-permute-done.5.got_1
  42.9 7.1 %collective-permute-done.6.got_2 = f32[16,256]{1,0:T(8,128)S(1)} collective-permute-done((f32[16,256]{1,0:T(8,128)S(1)}, f32[16,256]{1,0:T(8,128)S(1)}, u32[]{:S(2)}, u32[]{:S(2)}) %collective-permute-start.6) | collective-permute-done | bytes 16416 | tf_op jit(solution)/shard_map/ppermute | solution.py:584
  49.9 0.0 collective-permute-done.9.mean_2
  49.9 0.0 collective-permute-done.8.mean_1
  49.9 0.0 collective-permute-done.7.mean_0
  49.9 3.5 %last.1 = f32[4,192,384]{2,1,0:T(8,128)} custom-call(f32[2]{0:T(128)} %bitcast.12, f32[4]{0:T(128)} %diffusion.5, s32[16,16]{1,0:T(8,128)} %nest_patch.3, f32[4,192,384]{2,1,0:T(8,128)S(1)} %get-tuple-element.16.y, f32[3,4,384]{2,1,0:T(4,128)S(1)} %collective-permute-done.north, f32[3,4,384]{2,1,0:T(4,128)S(1)} %collective-permute-done.1.south, ...), custom_call_target="tpu_custom_call" | custom-call | tf_op jit(solution)/shard_map/last/pallas_call | solution.py:545
  (1 shorter events, 0.0 us)
Async XLA Ops:
  5.4 44.6 %collective-permute-start.9 = (f32[4,64,128]{2,1,0:T(8,128)S(1)}, f32[4,64,128]{2,1,0:T(8,128)S(1)}, u32[]{:S(2)}, u32[]{:S(2)}) collective-permute-start(f32[4,64,128]{2,1,0:T(8,128)S(1)} %get-tuple-element.26), channel_id=1, source_target_pairs={{272,0},{273,1},{274,2},{275,3},{276,4},{277,5},{278,6},{279,7},{2... | collective-permute-start | bytes 393224 | tf_op jit(solution)/shard_map/ppermute | solution.py:584
  14.5 35.4 %collective-permute-start.8 = (f32[4,64,128]{2,1,0:T(8,128)S(1)}, f32[4,64,128]{2,1,0:T(8,128)S(1)}, u32[]{:S(2)}, u32[]{:S(2)}) collective-permute-start(f32[4,64,128]{2,1,0:T(8,128)S(1)} %get-tuple-element.26), channel_id=1, source_target_pairs={{256,0},{257,1},{258,2},{259,3},{260,4},{261,5},{262,6},{263,7},{2... | collective-permute-start | bytes 393224 | tf_op jit(solution)/shard_map/ppermute | solution.py:584
  15.8 34.1 %collective-permute-start.7 = (f32[4,64,128]{2,1,0:T(8,128)S(1)}, f32[4,64,128]{2,1,0:T(8,128)S(1)}, u32[]{:S(2)}, u32[]{:S(2)}) collective-permute-start(f32[4,64,128]{2,1,0:T(8,128)S(1)} %get-tuple-element.26), channel_id=1, source_target_pairs={{256,16},{257,17},{258,18},{259,19},{260,20},{261,21},{262,22},{26... | collective-permute-start | bytes 393224 | tf_op jit(solution)/shard_map/ppermute | solution.py:584
  18.1 1.3 %collective-permute-start = (f32[3,4,384]{2,1,0:T(4,128)S(1)}, f32[3,4,384]{2,1,0:T(4,128)S(1)}, u32[]{:S(2)}, u32[]{:S(2)}) collective-permute-start(f32[3,4,384]{2,1,0:T(4,128)S(1)} %get-tuple-element.17), channel_id=1, source_target_pairs={{0,16},{1,17},{2,18},{3,19},{4,20},{5,21},{6,22},{7,23},{8,24},{9,... | collective-permute-start | bytes 55304 | tf_op jit(solution)/shard_map/ppermute | solution.py:584
  18.7 0.7 %collective-permute-start.1 = (f32[3,4,384]{2,1,0:T(4,128)S(1)}, f32[3,4,384]{2,1,0:T(4,128)S(1)}, u32[]{:S(2)}, u32[]{:S(2)}) collective-permute-start(f32[3,4,384]{2,1,0:T(4,128)S(1)} %get-tuple-element.18), channel_id=1, source_target_pairs={{16,0},{17,1},{18,2},{19,3},{20,4},{21,5},{22,6},{23,7},{24,8},{25... | collective-permute-start | bytes 55304 | tf_op jit(solution)/shard_map/ppermute | solution.py:584
  19.5 1.3 %collective-permute-start.2 = (f32[6,4,256]{2,1,0:T(4,128)S(1)}, f32[6,4,256]{2,1,0:T(4,128)S(1)}, u32[]{:S(2)}, u32[]{:S(2)}) collective-permute-start(f32[6,4,256]{2,1,0:T(4,128)S(1)} %get-tuple-element.20), channel_id=1, source_target_pairs={{0,1},{1,2},{2,3},{3,4},{4,5},{5,6},{6,7},{7,8},{8,9},{9,10},{10,1... | collective-permute-start | bytes 73736 | tf_op jit(solution)/shard_map/ppermute | solution.py:584
  20.1 0.7 %collective-permute-start.3 = (f32[6,4,256]{2,1,0:T(4,128)S(1)}, f32[6,4,256]{2,1,0:T(4,128)S(1)}, u32[]{:S(2)}, u32[]{:S(2)}) collective-permute-start(f32[6,4,256]{2,1,0:T(4,128)S(1)} %get-tuple-element.21), channel_id=1, source_target_pairs={{1,0},{2,1},{3,2},{4,3},{5,4},{6,5},{7,6},{8,7},{9,8},{10,9},{11,1... | collective-permute-start | bytes 73736 | tf_op jit(solution)/shard_map/ppermute | solution.py:584
  21.7 19.9 %collective-permute-start.4 = (f32[16,256]{1,0:T(8,128)S(1)}, f32[16,256]{1,0:T(8,128)S(1)}, u32[]{:S(2)}, u32[]{:S(2)}) collective-permute-start(f32[16,256]{1,0:T(8,128)S(1)} %get-tuple-element.23.sent_0), channel_id=1, source_target_pairs={{16,256},{17,257},{18,258},{19,259},{20,260},{21,261},{22,262},{23... | collective-permute-start | bytes 49160 | tf_op jit(solution)/shard_map/ppermute | solution.py:584
  23.0 19.9 %collective-permute-start.5 = (f32[16,256]{1,0:T(8,128)S(1)}, f32[16,256]{1,0:T(8,128)S(1)}, u32[]{:S(2)}, u32[]{:S(2)}) collective-permute-start(f32[16,256]{1,0:T(8,128)S(1)} %get-tuple-element.24.sent_1), channel_id=1, source_target_pairs={{0,256},{1,257},{2,258},{3,259},{4,260},{5,261},{6,262},{7,263},{8... | collective-permute-start | bytes 49160 | tf_op jit(solution)/shard_map/ppermute | solution.py:584
  41.6 8.4 %collective-permute-start.6 = (f32[16,256]{1,0:T(8,128)S(1)}, f32[16,256]{1,0:T(8,128)S(1)}, u32[]{:S(2)}, u32[]{:S(2)}) collective-permute-start(f32[16,256]{1,0:T(8,128)S(1)} %get-tuple-element.25.sent_2), channel_id=1, source_target_pairs={{0,272},{1,273},{2,274},{3,275},{4,276},{5,277},{6,278},{7,279},{8... | collective-permute-start | bytes 49160 | tf_op jit(solution)/shard_map/ppermute | solution.py:584
where the time goes:
time: 53.9 us; the launch traced here: 53.4 us
  waiting for transfers between devices  24.4 us (45%)
  starting transfers between devices  18.3 us (34%)
  Pallas kernels  10.6 us (20%)
    ppermute x10, waiting for transfers between devices, shift(): return lax.ppermute(value, AXES, routes(sizes, source, move))  24.4 us
    ppermute x10, starting transfers between devices, shift(): return lax.ppermute(value, AXES, routes(sizes, source, move))  18.3 us
    pallas_call x1, Pallas kernels, first(): pl.pallas_call(first_kernel, in_specs=[SMEM, SMEM, ANY, ANY], out_specs=[...  5.37 us
    pallas_call x1, Pallas kernels, last(): pl.pallas_call(last_kernel, in_specs=[SMEM] * 3 + [VMEM] * 14, out_specs=...  3.49 us
  transfers between devices with their start and end apart: 10, of which 2 were waited for; matrix products, arithmetic and copies ran while one was open for 0% of the time, Pallas kernels for 3%

commit v1 on v0

--- a/solution.py
+++ b/solution.py
@@ -28,31 +28,29 @@
 SMEM = pl.BlockSpec(memory_space=pltpu.SMEM)
 VMEM = pl.BlockSpec(memory_space=pltpu.VMEM)
 ANY = pl.BlockSpec(memory_space=pl.ANY)
+SMALL = pltpu.CompilerParams(vmem_limit_bytes=16 << 20)
 
 
 def iota(shape, dim):
     return lax.broadcasted_iota(jnp.int32, shape, dim)
 
 
-def split3(a):
+def split2(a):
     high = a.astype(BF16)
-    rest = a - high.astype(F32)
-    middle = rest.astype(BF16)
-    low = (rest - middle.astype(F32)).astype(BF16)
-    return high, middle, low
+    return high, (a - high.astype(F32)).astype(BF16)
 
 
 def dot_right(a, m):
-    return sum(jnp.dot(part, m, preferred_element_type=F32) for part in split3(a))
+    return sum(jnp.dot(part, m, preferred_element_type=F32) for part in split2(a))
 
 
 def dot_nt(m, a):
     dims = (((1,), (1,)), ((), ()))
-    return sum(lax.dot_general(m, part, dims, preferred_element_type=F32) for part in split3(a))
+    return sum(lax.dot_general(m, part, dims, preferred_element_type=F32) for part in split2(a))
 
 
 def dot_left(m, a):
-    return sum(jnp.dot(m, part, preferred_element_type=F32) for part in split3(a))
+    return sum(jnp.dot(m, part, preferred_element_type=F32) for part in split2(a))
 
 
 def select_rows(picks, width):
@@ -69,13 +67,31 @@
     return 1.0 - 4.0 * k, k - half_x, k + half_x, k - half_y, k + half_y
 
 
-def per_field(diffusion, scale, shape, dim, groups):
-    index = iota(shape, dim)
-    out = jnp.zeros(shape, F32)
-    for g in range(groups):
-        for f in range(V):
-            out = jnp.where(index == g * V + f, scale * diffusion[f], out)
+def per_field(diffusion, scale, shape, dim):
+    index = iota(shape, dim) & (V - 1)
+    out = jnp.full(shape, scale * diffusion[0], F32)
+    for f in range(1, V):
+        out = jnp.where(index == f, scale * diffusion[f], out)
     return out
+
+
+def step_rows(old, r, coefs, force):
+    a0, east, west, south, north = coefs
+    centre = old[8 + r : 8 + r + CHUNK, :]
+    return (
+        a0 * centre
+        + east * pltpu.roll(centre, W - 1, 1)
+        + west * pltpu.roll(centre, 1, 1)
+        + south * old[9 + r : 9 + r + CHUNK, :]
+        + north * old[7 + r : 7 + r + CHUNK, :]
+        + force
+    )
+
+
+def closed(k, courant):
+    a0, east, west, south, north = weights(k, courant)
+    lane = iota((1, W), 1)
+    return a0, jnp.where(lane == W - 1, 0.0, east), jnp.where(lane == 0, 0.0, west), south, north
 
 
 def near(*values):
@@ -120,16 +136,15 @@
             pltpu.VMEM((V, 16, W), BF16),
             pltpu.SemaphoreType.DMA((4,)),
         ],
+        compiler_params=SMALL,
         name="edge",
     )(x, drive)
 
 
 def first_kernel(
-    courant, diffusion, x, drive, y, mean, rows, cols, one, two, source, force, thirds, sems
+    courant, diffusion, x, drive, one, source, y, mean, rows, cols, two, force, thirds, sems
 ):
     parent = position()[0] == 0
-    scale = jnp.where(parent, 1.0, 3.0)
-    lane = iota((1, W), 1)
 
     def load(f):
         return (
@@ -143,34 +158,6 @@
     for f in range(V):
         one[f, 0:8, :] = jnp.zeros((8, W), F32)
         one[f, H + 8 : H + 16, :] = jnp.zeros((8, W), F32)
-    two[0:8, :] = jnp.zeros((8, W), F32)
-    two[H + 8 : H + 16, :] = jnp.zeros((8, W), F32)
-
-    def field(f, steps):
-        a0, ae, aw, as_, an = weights(diffusion[f] * scale, courant)
-        east = jnp.where(lane == W - 1, 0.0, ae)
-        west = jnp.where(lane == 0, 0.0, aw)
-
-        def step(old, new, at):
-            for r in range(0, H, CHUNK):
-                centre = old[8 + r : 8 + r + CHUNK, :]
-                north = old[7 + r : 7 + r + CHUNK, :]
-                south = old[9 + r : 9 + r + CHUNK, :]
-                new[at + r : at + r + CHUNK, :] = (
-                    a0 * centre
-                    + east * pltpu.roll(centre, W - 1, 1)
-                    + west * pltpu.roll(centre, 1, 1)
-                    + as_ * south
-                    + an * north
-                    + force[r : r + CHUNK, :]
-                )
-
-        force[...] = source[f].astype(F32) * jnp.where(parent, 1.0, 1.0 / 3.0)
-        mine = one.at[f]
-        if steps == 3:
-            step(mine, two, 8)
-            step(two, mine, 8)
-        step(mine, y.at[f], 0)
 
     @pl.when(parent)
     def _():
@@ -194,19 +181,29 @@
             for i in range(6):
                 cols[12 + i, f : f + 1, 0:H] = from_drive[i : i + 1]
 
-        @pl.loop(0, V)
-        def _(f):
-            field(f, 1)
-
     @pl.when(jnp.logical_not(parent))
     def _():
+        two[0:8, :] = jnp.zeros((8, W), F32)
+        two[H + 8 : H + 16, :] = jnp.zeros((8, W), F32)
         blocks = mean_matrix()
 
         @pl.loop(0, V)
         def _(f):
             for copy in load(f):
                 copy.wait()
-            field(f, 3)
+            coefs = closed(diffusion[f] * 3.0, courant)
+            mine = one.at[f]
+
+            def step(old, new, at):
+                for r in range(0, H, CHUNK):
+                    new[at + r : at + r + CHUNK, :] = step_rows(
+                        old, r, coefs, force[r : r + CHUNK, :]
+                    )
+
+            force[...] = source[f].astype(F32) * (1.0 / 3.0)
+            step(mine, two, 8)
+            step(two, mine, 8)
+            step(mine, y.at[f], 0)
             thirds[...] = dot_right(y[f], blocks)
             total = (
                 thirds[pl.ds(0, PH, stride=3), :]
@@ -225,22 +222,23 @@
     return pl.pallas_call(
         first_kernel,
         in_specs=[SMEM, SMEM, ANY, ANY],
-        out_specs=[VMEM] * 4,
+        out_specs=[VMEM] * 6,
         out_shape=[
+            pltpu.VMEM((V, H + 16, W), F32),
+            pltpu.VMEM((V, H, W), BF16),
             pltpu.VMEM((V, H, W), F32),
             pltpu.VMEM((V, PH, PW), F32),
             pltpu.VMEM((16, V, W), F32),
             pltpu.VMEM((18, V, 256), F32),
         ],
         scratch_shapes=[
-            pltpu.VMEM((V, H + 16, W), F32),
             pltpu.VMEM((H + 16, W), F32),
-            pltpu.VMEM((V, H, W), BF16),
             pltpu.VMEM((H, W), F32),
             pltpu.VMEM((H, PW), F32),
             pltpu.SemaphoreType.DMA((2, V)),
         ],
         cost_estimate=pl.CostEstimate(flops=40_000_000, transcendentals=0, bytes_accessed=20_000_000),
+        compiler_params=SMALL,
         name="first",
     )(courant, diffusion, x, drive)
 
@@ -264,6 +262,7 @@
         in_specs=[VMEM] * 3,
         out_specs=[VMEM] * 2,
         out_shape=[shape, shape],
+        compiler_params=SMALL,
         name="pack",
     )(*near(cols, north, south))
 
@@ -282,7 +281,7 @@
 
     @pl.when(section == 0)
     def _():
-        k = per_field(diffusion, 1.0, (V, 1), 0, 1)
+        k = per_field(diffusion, 1.0, (V, 1), 0)
         a0, ae, aw, as_, an = weights(k, courant)
         has_n = jnp.where(row > 0, 1.0, 0.0)
         has_s = jnp.where(row < count - 1, 1.0, 0.0)
@@ -404,44 +403,47 @@
         out_specs=[VMEM] * 3,
         out_shape=[pltpu.VMEM((4 * V, 256), F32)] * 3,
         scratch_shapes=[pltpu.VMEM((2, 6, V, W + 256), F32), pltpu.VMEM((2, 6, V, 256), F32)],
+        compiler_params=SMALL,
         name="rims",
     )(courant, diffusion, nest_patch, *near(rows, cols, north, south, west, east))
 
 
-def edge_effect(u, courant, diffusion):
-    k_row = per_field(diffusion, 3.0, (2 * V, 1), 0, 2)
-    a0, ae, aw, as_, an = weights(k_row, courant)
-    upper = iota((2 * V, 1), 0) < V
+def edge_effect(old, new, courant, diffusion):
+    n = old.shape[0]
+    k_row = per_field(diffusion, 3.0, (n, 1), 0)
+    a0_row, ae, aw, as_, an = weights(k_row, courant)
+    upper = (iota((n, 1), 0) & V) == 0
     outer, inner = jnp.where(upper, an, as_), jnp.where(upper, as_, an)
-    lane = iota((2 * V, W), 1)
+    lane = iota((n, W), 1)
     east = jnp.where(lane == W - 1, 0.0, ae)
     west = jnp.where(lane == 0, 0.0, aw)
     tent = jnp.maximum(3 - jnp.abs(iota((256, W), 1) - 3 * iota((256, W), 0) + 2), 0)
-    edges = dot_right(u, tent.astype(F32).astype(BF16)) * (1.0 / 3.0)
-    old, new = edges[0 : 2 * V], edges[2 * V : 4 * V]
+    tent = tent.astype(F32).astype(BF16)
 
     def along_row(v):
-        return a0 * v + east * pltpu.roll(v, W - 1, 1) + west * pltpu.roll(v, 1, 1)
-
-    row_effect = depths(old, new, outer, inner, along_row)
-
-    k_col = per_field(diffusion, 3.0, (1, 2 * V), 1, 2)
-    a0, ae, aw, as_, an = weights(k_col, courant)
-    left = iota((1, 2 * V), 1) < V
+        return a0_row * v + east * pltpu.roll(v, W - 1, 1) + west * pltpu.roll(v, 1, 1)
+
+    row_effect = depths(
+        dot_right(old, tent) * (1.0 / 3.0), dot_right(new, tent) * (1.0 / 3.0), outer, inner, along_row
+    )
+
+    k_col = per_field(diffusion, 3.0, (1, n), 1)
+    a0_col, ae, aw, as_, an = weights(k_col, courant)
+    left = (iota((1, n), 1) & V) == 0
     outer, inner = jnp.where(left, aw, ae), jnp.where(left, ae, aw)
-    down = iota((H, 2 * V), 0)
+    down = iota((H, n), 0)
     south = jnp.where(down == H - 1, 0.0, as_)
     north = jnp.where(down == 0, 0.0, an)
     tent = jnp.maximum(3 - jnp.abs(iota((H, 256), 0) - 3 * (iota((H, 256), 1) - OFF) + 2), 0)
     tent = tent.astype(F32).astype(BF16)
-    old = dot_nt(tent, u[0 : 2 * V]) * (1.0 / 3.0)
-    new = dot_nt(tent, u[2 * V : 4 * V]) * (1.0 / 3.0)
 
     def along_column(v):
         return a0_col * v + south * pltpu.roll(v, H - 1, 0) + north * pltpu.roll(v, 1, 0)
 
-    a0_col = a0
-    return row_effect, depths(old, new, outer, inner, along_column)
+    col_effect = depths(
+        dot_nt(tent, old) * (1.0 / 3.0), dot_nt(tent, new) * (1.0 / 3.0), outer, inner, along_column
+    )
+    return row_effect, col_effect
 
 
 def depths(old, new, outer, inner, along):
@@ -455,44 +457,53 @@
     return third_0, third_1, third_2
 
 
-def spread(values, depth):
-    block, lane = iota((2 * V, 2 * V * 128), 0), iota((2 * V, 2 * V * 128), 1)
+def spread(values, depth, first=0):
+    shape = (values.shape[1], 2 * V * 128)
+    block, lane = iota(shape, 0) - first, iota(shape, 1)
     target = block * 128 + jnp.where(block < V, depth, 127 - depth)
     return dot_right(values, jnp.where(lane == target, 1.0, 0.0).astype(BF16))
 
 
 def last_kernel(
-    courant, diffusion, nest_patch, y, north, south, west, east,
+    courant, diffusion, nest_patch, one, source, y, north, south, west, east,
     sent_0, sent_1, sent_2, got_0, got_1, got_2, mean_0, mean_1, mean_2, out, tile, sems,
 ):
     section, row, column = position()
     count = nest_patch.shape[0]
     parent = section == 0
     sent, got, means = (sent_0, sent_1, sent_2), (got_0, got_1, got_2), (mean_0, mean_1, mean_2)
-
-    def sides(f, both):
-        tile[f, :, 0:128] = y[f, :, 0:128] + both[:, f * 128 : (f + 1) * 128]
-        tile[f, :, 128 : W - 128] = y[f, :, 128 : W - 128]
-        right = (V + f) * 128
-        tile[f, :, W - 128 : W] = y[f, :, W - 128 : W] + both[:, right : right + 128]
+    n = 2 * V
 
     def send(f):
         return pltpu.make_async_copy(tile.at[f], out.at[f], sems.at[f])
 
     @pl.when(parent)
     def _():
-        _, ae, aw, _, _ = weights(per_field(diffusion, 1.0, (1, 2 * V), 1, 2), courant)
+        _, ae, aw, _, _ = weights(per_field(diffusion, 1.0, (1, n), 1), courant)
         eye = jnp.where(iota((H, H), 0) == iota((H, H), 1), 1.0, 0.0).astype(BF16)
         beyond = jnp.concatenate([west[0, :, 0:H], east[0, :, 0:H]], axis=0)
-        outer = jnp.where(iota((1, 2 * V), 1) < V, aw, ae)
+        outer = jnp.where(iota((1, n), 1) < V, aw, ae)
         both = spread(dot_nt(eye, beyond) * outer, 0)
         for f in range(V):
-            _, _, _, as_, an = weights(diffusion[f], courant)
-            sides(f, both)
-            tile[f, 0:1, :] = tile[f, 0:1, :] + an * north[0, f : f + 1, :]
-            tile[f, H - 1 : H, :] = tile[f, H - 1 : H, :] + as_ * south[0, f : f + 1, :]
+            coefs = closed(diffusion[f], courant)
+            left, right = f * 128, (V + f) * 128
+            for r in range(0, H, CHUNK):
+                end = r + CHUNK
+                value = step_rows(one.at[f], r, coefs, source[f, r:end, :].astype(F32))
+                tile[f, r:end, 0:128] = value[:, 0:128] + both[r:end, left : left + 128]
+                tile[f, r:end, 128 : W - 128] = value[:, 128 : W - 128]
+                tile[f, r:end, W - 128 : W] = (
+                    value[:, W - 128 : W] + both[r:end, right : right + 128]
+                )
+            tile[f, 0:1, :] = tile[f, 0:1, :] + coefs[4] * north[0, f : f + 1, :]
+            tile[f, H - 1 : H, :] = tile[f, H - 1 : H, :] + coefs[3] * south[0, f : f + 1, :]
+        old = jnp.concatenate([s[0:n, :] for s in sent], axis=0)
+        new = jnp.concatenate([s[n : 2 * n, :] for s in sent], axis=0)
+        row_effect, col_effect = edge_effect(old, new, courant, diffusion)
+        by_row = dot_right(sum(row_effect), mean_matrix()) * (1.0 / 9.0)
         thirds = iota((PH, H), 1) - 3 * iota((PH, H), 0)
         thirds = jnp.where((thirds >= 0) & (thirds <= 2), 1.0, 0.0).astype(BF16)
+        by_col = dot_left(thirds, sum(col_effect)) * (1.0 / 9.0)
         line = iota((PH, PW), 0)
         for member in range(3):
             nest = row + member - 1
@@ -503,17 +514,15 @@
             def _(member=member, slot=slot):
                 at_row = pl.multiple_of(lax.div(slot, 3) * PH, PH)
                 at_col = pl.multiple_of(lax.rem(slot, 3) * PW, PW)
-                row_effect, col_effect = edge_effect(sent[member][...], courant, diffusion)
-                by_row = dot_right(sum(row_effect), mean_matrix()) * (1.0 / 9.0)
-                by_col = spread(dot_left(thirds, sum(col_effect)) * (1.0 / 9.0), 0)
+                beside = spread(by_col, 0, member * n)
                 for f in range(V):
-                    right = (V + f) * 128
+                    left, right, up = f * 128, (V + f) * 128, member * n + f
                     tile[f, pl.ds(at_row, PH), pl.ds(at_col, PW)] = (
                         means[member][f]
-                        + jnp.where(line == 0, by_row[f : f + 1], 0.0)
-                        + jnp.where(line == PH - 1, by_row[V + f : V + f + 1], 0.0)
-                        + by_col[:, f * 128 : (f + 1) * 128]
-                        + by_col[:, right : right + 128]
+                        + jnp.where(line == 0, by_row[up : up + 1], 0.0)
+                        + jnp.where(line == PH - 1, by_row[up + V : up + V + 1], 0.0)
+                        + beside[:, left : left + 128]
+                        + beside[:, right : right + 128]
                     )
 
         for f in range(V):
@@ -523,10 +532,13 @@
     def _():
         member = row - lax.div(nest_patch[row, column], 9) + 1
         u = jnp.where(member == 0, got[0][...], jnp.where(member == 1, got[1][...], got[2][...]))
-        row_effect, col_effect = edge_effect(u, courant, diffusion)
+        row_effect, col_effect = edge_effect(u[0:n], u[n : 2 * n], courant, diffusion)
         both = sum(spread(col_effect[depth], depth) for depth in range(3))
         for f in range(V):
-            sides(f, both)
+            left, right = f * 128, (V + f) * 128
+            tile[f, :, 0:128] = y[f, :, 0:128] + both[:, left : left + 128]
+            tile[f, :, 128 : W - 128] = y[f, :, 128 : W - 128]
+            tile[f, :, W - 128 : W] = y[f, :, W - 128 : W] + both[:, right : right + 128]
             for depth in range(3):
                 bottom = H - 1 - depth
                 tile[f, depth : depth + 1, :] = (
@@ -541,18 +553,16 @@
         send(f).wait()
 
 
-def last(courant, diffusion, nest_patch, y, north, south, west, east, sent, got, means):
+def last(courant, diffusion, nest_patch, *arrays):
     return pl.pallas_call(
         last_kernel,
-        in_specs=[SMEM] * 3 + [VMEM] * 14,
+        in_specs=[SMEM] * 3 + [VMEM] * 16,
         out_specs=ANY,
         out_shape=jax.ShapeDtypeStruct((V, H, W), F32),
         scratch_shapes=[pltpu.VMEM((V, H, W), F32), pltpu.SemaphoreType.DMA((V,))],
+        compiler_params=SMALL,
         name="last",
-    )(
-        courant, diffusion, nest_patch,
-        *near(y, north, south, west, east, *sent, *got, *means),
-    )
+    )(courant, diffusion, nest_patch, *near(*arrays))
 
 
 def routes(sizes, source, move):
@@ -586,14 +596,16 @@
     downward, upward = edge(x, drive)
     north = shift(downward, 0, lambda r, c: (0, r + 1, c))
     south = shift(upward, 0, lambda r, c: (0, r - 1, c))
-    y, mean, rows, cols = first(courant, diffusion, x, drive)
+    one, source, y, mean, rows, cols = first(courant, diffusion, x, drive)
+    means = [shift(mean, 1, lambda r, c, m=m: (0, r + 1 - m, c)) for m in range(3)]
     to_west, to_east = pack(cols, north, south)
     west = shift(to_east, 0, lambda r, c: (0, r, c + 1))
     east = shift(to_west, 0, lambda r, c: (0, r, c - 1))
-    means = [shift(mean, 1, lambda r, c, m=m: (0, r + 1 - m, c)) for m in range(3)]
     sent = rims(courant, diffusion, nest_patch, rows, cols, north, south, west, east)
     got = [shift(sent[m], 0, lambda r, c, m=m: (1, r + m - 1, c)) for m in range(3)]
-    out = last(courant, diffusion, nest_patch, y, north, south, west, east, sent, got, means)
+    out = last(
+        courant, diffusion, nest_patch, one, source, y, north, south, west, east, *sent, *got, *means
+    )
     return out.reshape(fields.shape)
 
 

time: 53.9 us -> 54.6 us (1.013)
  the two profiles are of different devices: /device:TPU:95 before, /device:TPU:91 now
where the time goes in v1:
time: 54.6 us; the launch traced here: 54.2 us
  waiting for transfers between devices  24.7 us (45%)
  starting transfers between devices  16.9 us (31%)
  Pallas kernels  8.77 us (16%)
  local copies, waits for them, and re-layouts  3.66 us (7%)
    ppermute x10, waiting for transfers between devices, shift(): return lax.ppermute(value, AXES, routes(sizes, source, move))  24.7 us
    ppermute x10, starting transfers between devices, shift(): return lax.ppermute(value, AXES, routes(sizes, source, move))  16.9 us
    pallas_call x1, Pallas kernels, first(): pl.pallas_call(first_kernel, in_specs=[SMEM, SMEM, ANY, ANY], out_specs=[...  4.96 us
    unnamed x14, local copies, waits for them, and re-layouts  3.66 us
    pallas_call x1, Pallas kernels, last(): pl.pallas_call(last_kernel, in_specs=[SMEM] * 3 + [VMEM] * 16, out_specs=...  2.99 us
  transfers between devices with their start and end apart: 10, of which 2 were waited for; matrix products, arithmetic and copies ran while one was open for 0% of the time, Pallas kernels for 2%

profile of v1, /device:TPU:91, one launch (start us, length us, event | category | flops | bytes accessed | tf_op | source)
XLA Modules:
  0.0 54.2 jit_solution(2558571297770640139)
XLA Ops:
  0.0 1.3 %copy-done = f32[1,4,1,192,384]{4,3,2,1,0:T(8,128)S(1)} copy-done((f32[1,4,1,192,384]{4,3,2,1,0:T(8,128)S(1)}, f32[1,4,1,192,384]{4,3,2,1,0:T(8,128)}, u32[]{:S(2)}) %copy-start) | copy-done | bytes 1179672
  1.3 1.1 %copy-done.2 = bf16[1,4,1,192,384]{4,3,2,1,0:T(8,128)(2,1)S(1)} copy-done((bf16[1,4,1,192,384]{4,3,2,1,0:T(8,128)(2,1)S(1)}, bf16[1,4,1,192,384]{4,3,2,1,0:T(8,128)(2,1)}, u32[]{:S(2)}) %copy-start.2) | copy-done | bytes 589848
  2.3 0.7 %copy-done.5 = f32[2,1]{0,1:T(1,128)S(1)} copy-done((f32[2,1]{0,1:T(1,128)S(1)}, f32[2,1]{0,1:T(1,128)}, u32[]{:S(2)}) %copy-start.5) | copy-done | bytes 32
  3.0 0.7 %copy-done.6 = f32[4]{0:T(128)S(1)} copy-done((f32[4]{0:T(128)S(1)}, f32[4]{0:T(128)}, u32[]{:S(2)}) %copy-start.6) | copy-done | bytes 40
  3.7 5.0 %first.1 = (f32[4,208,384]{2,1,0:T(8,128)S(1)}, bf16[4,192,384]{2,1,0:T(8,128)(2,1)S(1)}, f32[4,192,384]{2,1,0:T(8,128)S(1)}, f32[4,64,128]{2,1,0:T(8,128)S(1)},...) custom-call(f32[2]{0:T(128)S(1)} %bitcast.10, f32[4]{0:T(128)S(1)} %copy-done.6, f32[4,192,384]{2,1,0:T(8,128)S(1)} %bitcast.6, ...), custom_call_target="tpu_custom_call" | custom-call | flops 40000000 | bytes 20000000 | tf_op jit(solution)/shard_map/first/pallas_call | solution.py:222
  8.6 0.0 copy-start.4
  8.6 7.8 %collective-permute-start.9 = (f32[4,64,128]{2,1,0:T(8,128)S(1)}, f32[4,64,128]{2,1,0:T(8,128)S(1)}, u32[]{:S(2)}, u32[]{:S(2)}) collective-permute-start(f32[4,64,128]{2,1,0:T(8,128)S(1)} %get-tuple-element.30), channel_id=1, source_target_pairs={{272,0},{273,1},{274,2},{275,3},{276,4},{277,5},{278,6},{279,7},{2... | collective-permute-start | bytes 393224 | tf_op jit(solution)/shard_map/ppermute | solution.py:594
  16.4 1.3 %collective-permute-start.8 = (f32[4,64,128]{2,1,0:T(8,128)S(1)}, f32[4,64,128]{2,1,0:T(8,128)S(1)}, u32[]{:S(2)}, u32[]{:S(2)}) collective-permute-start(f32[4,64,128]{2,1,0:T(8,128)S(1)} %get-tuple-element.30), channel_id=1, source_target_pairs={{256,0},{257,1},{258,2},{259,3},{260,4},{261,5},{262,6},{263,7},{2... | collective-permute-start | bytes 393224 | tf_op jit(solution)/shard_map/ppermute | solution.py:594
  17.7 1.3 %collective-permute-start.7 = (f32[4,64,128]{2,1,0:T(8,128)S(1)}, f32[4,64,128]{2,1,0:T(8,128)S(1)}, u32[]{:S(2)}, u32[]{:S(2)}) collective-permute-start(f32[4,64,128]{2,1,0:T(8,128)S(1)} %get-tuple-element.30), channel_id=1, source_target_pairs={{256,16},{257,17},{258,18},{259,19},{260,20},{261,21},{262,22},{26... | collective-permute-start | bytes 393224 | tf_op jit(solution)/shard_map/ppermute | solution.py:594
  19.0 0.0 copy-done.1
  19.0 0.0 copy-done.3
  19.0 0.1 edge.1
  19.2 0.7 %collective-permute-start = (f32[3,4,384]{2,1,0:T(4,128)S(1)}, f32[3,4,384]{2,1,0:T(4,128)S(1)}, u32[]{:S(2)}, u32[]{:S(2)}) collective-permute-start(f32[3,4,384]{2,1,0:T(4,128)S(1)} %get-tuple-element.21), channel_id=1, source_target_pairs={{0,16},{1,17},{2,18},{3,19},{4,20},{5,21},{6,22},{7,23},{8,24},{9,... | collective-permute-start | bytes 55304 | tf_op jit(solution)/shard_map/ppermute | solution.py:594
  19.8 0.7 %collective-permute-start.1 = (f32[3,4,384]{2,1,0:T(4,128)S(1)}, f32[3,4,384]{2,1,0:T(4,128)S(1)}, u32[]{:S(2)}, u32[]{:S(2)}) collective-permute-start(f32[3,4,384]{2,1,0:T(4,128)S(1)} %get-tuple-element.22), channel_id=1, source_target_pairs={{16,0},{17,1},{18,2},{19,3},{20,4},{21,5},{22,6},{23,7},{24,8},{25... | collective-permute-start | bytes 55304 | tf_op jit(solution)/shard_map/ppermute | solution.py:594
  20.5 0.0 collective-permute-done.north
  20.5 0.0 collective-permute-done.1.south
  20.5 0.7 %collective-permute-start.2 = (f32[6,4,256]{2,1,0:T(4,128)S(1)}, f32[6,4,256]{2,1,0:T(4,128)S(1)}, u32[]{:S(2)}, u32[]{:S(2)}) collective-permute-start(f32[6,4,256]{2,1,0:T(4,128)S(1)} %get-tuple-element.24), channel_id=1, source_target_pairs={{0,1},{1,2},{2,3},{3,4},{4,5},{5,6},{6,7},{7,8},{8,9},{9,10},{10,1... | collective-permute-start | bytes 73736 | tf_op jit(solution)/shard_map/ppermute | solution.py:594
  21.2 0.7 %collective-permute-start.3 = (f32[6,4,256]{2,1,0:T(4,128)S(1)}, f32[6,4,256]{2,1,0:T(4,128)S(1)}, u32[]{:S(2)}, u32[]{:S(2)}) collective-permute-start(f32[6,4,256]{2,1,0:T(4,128)S(1)} %get-tuple-element.25), channel_id=1, source_target_pairs={{1,0},{2,1},{3,2},{4,3},{5,4},{6,5},{7,6},{8,7},{9,8},{10,9},{11,1... | collective-permute-start | bytes 73736 | tf_op jit(solution)/shard_map/ppermute | solution.py:594
  21.9 0.0 collective-permute-done.2.west
  21.9 0.0 collective-permute-done.3.east
  21.9 0.0 copy-done.4
  21.9 0.7 %rims.1 = (f32[16,256]{1,0:T(8,128)S(1)}, f32[16,256]{1,0:T(8,128)S(1)}, f32[16,256]{1,0:T(8,128)S(1)}) custom-call(f32[2]{0:T(128)S(1)} %bitcast.11, f32[4]{0:T(128)S(1)} %copy-done.6, s32[16,16]{1,0:T(8,128)S(1)} %copy-done.4, f32[16,4,384]{2,1,0:T(4,128)S(1)} %get-tuple-element.26.rows, f32[18,4,256]{2,1,0:T(4,128)S(1)} %get-tuple-element.23.cols, ...), custom_call_target="tpu_custom_call" | custom-call | tf_op jit(solution)/shard_map/rims/pallas_call | solution.py:400
  22.6 1.3 %collective-permute-start.4 = (f32[16,256]{1,0:T(8,128)S(1)}, f32[16,256]{1,0:T(8,128)S(1)}, u32[]{:S(2)}, u32[]{:S(2)}) collective-permute-start(f32[16,256]{1,0:T(8,128)S(1)} %get-tuple-element.27.sent_0), channel_id=1, source_target_pairs={{16,256},{17,257},{18,258},{19,259},{20,260},{21,261},{22,262},{23... | collective-permute-start | bytes 49160 | tf_op jit(solution)/shard_map/ppermute | solution.py:594
  23.9 1.3 %collective-permute-start.5 = (f32[16,256]{1,0:T(8,128)S(1)}, f32[16,256]{1,0:T(8,128)S(1)}, u32[]{:S(2)}, u32[]{:S(2)}) collective-permute-start(f32[16,256]{1,0:T(8,128)S(1)} %get-tuple-element.28.sent_1), channel_id=1, source_target_pairs={{0,256},{1,257},{2,258},{3,259},{4,260},{5,261},{6,262},{7,263},{8... | collective-permute-start | bytes 49160 | tf_op jit(solution)/shard_map/ppermute | solution.py:594
  25.2 17.6 %collective-permute-done.4.got_0 = f32[16,256]{1,0:T(8,128)S(1)} collective-permute-done((f32[16,256]{1,0:T(8,128)S(1)}, f32[16,256]{1,0:T(8,128)S(1)}, u32[]{:S(2)}, u32[]{:S(2)}) %collective-permute-start.4) | collective-permute-done | bytes 16416 | tf_op jit(solution)/shard_map/ppermute | solution.py:594
  42.8 1.3 %collective-permute-start.6 = (f32[16,256]{1,0:T(8,128)S(1)}, f32[16,256]{1,0:T(8,128)S(1)}, u32[]{:S(2)}, u32[]{:S(2)}) collective-permute-start(f32[16,256]{1,0:T(8,128)S(1)} %get-tuple-element.29.sent_2), channel_id=1, source_target_pairs={{0,272},{1,273},{2,274},{3,275},{4,276},{5,277},{6,278},{7,279},{8... | collective-permute-start | bytes 49160 | tf_op jit(solution)/shard_map/ppermute | solution.py:594
  44.1 0.0 collective-permute-done.5.got_1
  44.1 7.1 %collective-permute-done.6.got_2 = f32[16,256]{1,0:T(8,128)S(1)} collective-permute-done((f32[16,256]{1,0:T(8,128)S(1)}, f32[16,256]{1,0:T(8,128)S(1)}, u32[]{:S(2)}, u32[]{:S(2)}) %collective-permute-start.6) | collective-permute-done | bytes 16416 | tf_op jit(solution)/shard_map/ppermute | solution.py:594
  51.2 0.0 collective-permute-done.9.mean_2
  51.2 0.0 collective-permute-done.8.mean_1
  51.2 0.0 collective-permute-done.7.mean_0
  51.2 3.0 %last.1 = f32[4,192,384]{2,1,0:T(8,128)} custom-call(f32[2]{0:T(128)S(1)} %bitcast.12, f32[4]{0:T(128)S(1)} %copy-done.6, s32[16,16]{1,0:T(8,128)S(1)} %copy-done.4, f32[4,208,384]{2,1,0:T(8,128)S(1)} %get-tuple-element.18.one, bf16[4,192,384]{2,1,0:T(8,128)(2,1)S(1)} %get-tuple-element.19.source, f32[4,192,384]{2,1,0:T(8,128)S(1)} %get-tuple-element.20.y, ...), custom_call_target="tpu_custom_call" | custom-call | tf_op jit(solution)/shard_map/last/pallas_call | solution.py:557
  (7 shorter events, 0.0 us)
Async XLA Ops:
  0.0 1.3 %copy-start = (f32[1,4,1,192,384]{4,3,2,1,0:T(8,128)S(1)}, f32[1,4,1,192,384]{4,3,2,1,0:T(8,128)}, u32[]{:S(2)}) copy-start(f32[1,4,1,192,384]{4,3,2,1,0:T(8,128)} %param.5) | copy-start | bytes 3538948
  1.3 1.1 %copy-start.2 = (bf16[1,4,1,192,384]{4,3,2,1,0:T(8,128)(2,1)S(1)}, bf16[1,4,1,192,384]{4,3,2,1,0:T(8,128)(2,1)}, u32[]{:S(2)}) copy-start(bf16[1,4,1,192,384]{4,3,2,1,0:T(8,128)(2,1)} %param.6) | copy-start | bytes 1769476
  2.3 0.7 %copy-start.5 = (f32[2,1]{0,1:T(1,128)S(1)}, f32[2,1]{0,1:T(1,128)}, u32[]{:S(2)}) copy-start(f32[2,1]{0,1:T(1,128)} %param.7) | copy-start | bytes 28
  3.0 0.7 %copy-start.6 = (f32[4]{0:T(128)S(1)}, f32[4]{0:T(128)}, u32[]{:S(2)}) copy-start(f32[4]{0:T(128)} %diffusion.5) | copy-start | bytes 52
  3.6 15.4 %copy-start.1 = (f32[1,4,1,192,384]{4,3,2,1,0:T(8,128)S(1)}, f32[1,4,1,192,384]{4,3,2,1,0:T(8,128)}, u32[]{:S(2)}) copy-start(f32[1,4,1,192,384]{4,3,2,1,0:T(8,128)} %param.5) | copy-start | bytes 3538948
  3.6 15.4 %copy-start.3 = (bf16[1,4,1,192,384]{4,3,2,1,0:T(8,128)(2,1)S(1)}, bf16[1,4,1,192,384]{4,3,2,1,0:T(8,128)(2,1)}, u32[]{:S(2)}) copy-start(bf16[1,4,1,192,384]{4,3,2,1,0:T(8,128)(2,1)} %param.6) | copy-start | bytes 1769476
  8.6 13.3 %copy-start.4 = (s32[16,16]{1,0:T(8,128)S(1)}, s32[16,16]{1,0:T(8,128)}, u32[]{:S(2)}) copy-start(s32[16,16]{1,0:T(8,128)} %nest_patch.3) | copy-start | bytes 3076
  8.6 42.6 %collective-permute-start.9 = (f32[4,64,128]{2,1,0:T(8,128)S(1)}, f32[4,64,128]{2,1,0:T(8,128)S(1)}, u32[]{:S(2)}, u32[]{:S(2)}) collective-permute-start(f32[4,64,128]{2,1,0:T(8,128)S(1)} %get-tuple-element.30), channel_id=1, source_target_pairs={{272,0},{273,1},{274,2},{275,3},{276,4},{277,5},{278,6},{279,7},{2... | collective-permute-start | bytes 393224 | tf_op jit(solution)/shard_map/ppermute | solution.py:594
  16.4 34.8 %collective-permute-start.8 = (f32[4,64,128]{2,1,0:T(8,128)S(1)}, f32[4,64,128]{2,1,0:T(8,128)S(1)}, u32[]{:S(2)}, u32[]{:S(2)}) collective-permute-start(f32[4,64,128]{2,1,0:T(8,128)S(1)} %get-tuple-element.30), channel_id=1, source_target_pairs={{256,0},{257,1},{258,2},{259,3},{260,4},{261,5},{262,6},{263,7},{2... | collective-permute-start | bytes 393224 | tf_op jit(solution)/shard_map/ppermute | solution.py:594
  17.7 33.5 %collective-permute-start.7 = (f32[4,64,128]{2,1,0:T(8,128)S(1)}, f32[4,64,128]{2,1,0:T(8,128)S(1)}, u32[]{:S(2)}, u32[]{:S(2)}) collective-permute-start(f32[4,64,128]{2,1,0:T(8,128)S(1)} %get-tuple-element.30), channel_id=1, source_target_pairs={{256,16},{257,17},{258,18},{259,19},{260,20},{261,21},{262,22},{26... | collective-permute-start | bytes 393224 | tf_op jit(solution)/shard_map/ppermute | solution.py:594
  19.2 1.3 %collective-permute-start = (f32[3,4,384]{2,1,0:T(4,128)S(1)}, f32[3,4,384]{2,1,0:T(4,128)S(1)}, u32[]{:S(2)}, u32[]{:S(2)}) collective-permute-start(f32[3,4,384]{2,1,0:T(4,128)S(1)} %get-tuple-element.21), channel_id=1, source_target_pairs={{0,16},{1,17},{2,18},{3,19},{4,20},{5,21},{6,22},{7,23},{8,24},{9,... | collective-permute-start | bytes 55304 | tf_op jit(solution)/shard_map/ppermute | solution.py:594
  19.8 0.7 %collective-permute-start.1 = (f32[3,4,384]{2,1,0:T(4,128)S(1)}, f32[3,4,384]{2,1,0:T(4,128)S(1)}, u32[]{:S(2)}, u32[]{:S(2)}) collective-permute-start(f32[3,4,384]{2,1,0:T(4,128)S(1)} %get-tuple-element.22), channel_id=1, source_target_pairs={{16,0},{17,1},{18,2},{19,3},{20,4},{21,5},{22,6},{23,7},{24,8},{25... | collective-permute-start | bytes 55304 | tf_op jit(solution)/shard_map/ppermute | solution.py:594
  20.5 1.3 %collective-permute-start.2 = (f32[6,4,256]{2,1,0:T(4,128)S(1)}, f32[6,4,256]{2,1,0:T(4,128)S(1)}, u32[]{:S(2)}, u32[]{:S(2)}) collective-permute-start(f32[6,4,256]{2,1,0:T(4,128)S(1)} %get-tuple-element.24), channel_id=1, source_target_pairs={{0,1},{1,2},{2,3},{3,4},{4,5},{5,6},{6,7},{7,8},{8,9},{9,10},{10,1... | collective-permute-start | bytes 73736 | tf_op jit(solution)/shard_map/ppermute | solution.py:594
  21.2 0.7 %collective-permute-start.3 = (f32[6,4,256]{2,1,0:T(4,128)S(1)}, f32[6,4,256]{2,1,0:T(4,128)S(1)}, u32[]{:S(2)}, u32[]{:S(2)}) collective-permute-start(f32[6,4,256]{2,1,0:T(4,128)S(1)} %get-tuple-element.25), channel_id=1, source_target_pairs={{1,0},{2,1},{3,2},{4,3},{5,4},{6,5},{7,6},{8,7},{9,8},{10,9},{11,1... | collective-permute-start | bytes 73736 | tf_op jit(solution)/shard_map/ppermute | solution.py:594
  22.6 20.2 %collective-permute-start.4 = (f32[16,256]{1,0:T(8,128)S(1)}, f32[16,256]{1,0:T(8,128)S(1)}, u32[]{:S(2)}, u32[]{:S(2)}) collective-permute-start(f32[16,256]{1,0:T(8,128)S(1)} %get-tuple-element.27.sent_0), channel_id=1, source_target_pairs={{16,256},{17,257},{18,258},{19,259},{20,260},{21,261},{22,262},{23... | collective-permute-start | bytes 49160 | tf_op jit(solution)/shard_map/ppermute | solution.py:594
  23.9 20.2 %collective-permute-start.5 = (f32[16,256]{1,0:T(8,128)S(1)}, f32[16,256]{1,0:T(8,128)S(1)}, u32[]{:S(2)}, u32[]{:S(2)}) collective-permute-start(f32[16,256]{1,0:T(8,128)S(1)} %get-tuple-element.28.sent_1), channel_id=1, source_target_pairs={{0,256},{1,257},{2,258},{3,259},{4,260},{5,261},{6,262},{7,263},{8... | collective-permute-start | bytes 49160 | tf_op jit(solution)/shard_map/ppermute | solution.py:594
  42.8 8.4 %collective-permute-start.6 = (f32[16,256]{1,0:T(8,128)S(1)}, f32[16,256]{1,0:T(8,128)S(1)}, u32[]{:S(2)}, u32[]{:S(2)}) collective-permute-start(f32[16,256]{1,0:T(8,128)S(1)} %get-tuple-element.29.sent_2), channel_id=1, source_target_pairs={{0,272},{1,273},{2,274},{3,275},{4,276},{5,277},{6,278},{7,279},{8... | collective-permute-start | bytes 49160 | tf_op jit(solution)/shard_map/ppermute | solution.py:594

commit v2 on v1

v2 whole, which is shorter than its diff:
```python
import functools

import jax
import jax.numpy as jnp
from jax import lax
from jax.experimental import pallas as pl
from jax.experimental.pallas import tpu as pltpu
from jax.sharding import PartitionSpec as P


F32 = jnp.float32
BF16 = jnp.bfloat16
V, H, W = 4, 192, 384
PH, PW = H // 3, W // 3
CHUNK = 16
OFF = 160


def inner(n):
    lines = (n - 1, n, 2 * n - 1, 2 * n)
    return lines, (n - 2, n - 1, n, n + 1, 2 * n - 2, 2 * n - 1, 2 * n, 2 * n + 1)


IN_ROWS, BANK_ROWS = inner(PH)
IN_COLS, BANK_COLS = inner(PW)
WIDE = W + 256
COURANT, PATCH_ROW, PATCH_COL, MEMBER = V, V + 2, V + 5, V + 8
AXES = ("sec", "gy", "gx")
VMEM = pl.BlockSpec(memory_space=pltpu.VMEM)
ANY = pl.BlockSpec(memory_space=pl.ANY)
SMALL = pltpu.CompilerParams(vmem_limit_bytes=16 << 20)


def iota(shape, dim):
    return lax.broadcasted_iota(jnp.int32, shape, dim)


def split2(a):
    high = a.astype(BF16)
    return high, (a - high.astype(F32)).astype(BF16)


def dot_right(a, m):
    return sum(jnp.dot(part, m, preferred_element_type=F32) for part in split2(a))


def dot_nt(m, a):
    dims = (((1,), (1,)), ((), ()))
    return sum(lax.dot_general(m, part, dims, preferred_element_type=F32) for part in split2(a))


def dot_left(m, a):
    return sum(jnp.dot(m, part, preferred_element_type=F32) for part in split2(a))


def select_rows(picks, width):
    row, lane = iota((16, width), 0), iota((16, width), 1)
    wanted = jnp.full((16, width), -1, jnp.int32)
    for i, pick in enumerate(picks):
        wanted = jnp.where(row == i, pick, wanted)
    return jnp.where(lane == wanted, 1.0, 0.0).astype(BF16)


def weights(k, params):
    width = k.shape[1]
    half_x = 0.5 * params[COURANT : COURANT + 1, 0:width]
    half_y = 0.5 * params[COURANT + 1 : COURANT + 2, 0:width]
    return 1.0 - 4.0 * k, k - half_x, k + half_x, k - half_y, k + half_y


def per_field(params, shape, dim):
    index = iota(shape, dim) & (V - 1)
    out = jnp.broadcast_to(params[0:1, 0:1], shape)
    for f in range(1, V):
        out = jnp.where(index == f, params[f : f + 1, 0:1], out)
    return out


def weights_of(k, params):
    half_x = 0.5 * params[COURANT : COURANT + 1, 0:1]
    half_y = 0.5 * params[COURANT + 1 : COURANT + 2, 0:1]
    return 1.0 - 4.0 * k, k - half_x, k + half_x, k - half_y, k + half_y


def closed(k, params):
    a0, east, west, south, north = weights(k, params)
    lane = iota((1, W), 1)
    return a0, jnp.where(lane == W - 1, 0.0, east), jnp.where(lane == 0, 0.0, west), south, north


def step_rows(get, r, coefs, force):
    a0, east, west, south, north = coefs
    centre = get(r)
    return (
        a0 * centre
        + east * pltpu.roll(centre, W - 1, 1)
        + west * pltpu.roll(centre, 1, 1)
        + south * get(r + 1)
        + north * get(r - 1)
        + force
    )


def padded(ref):
    return lambda r: ref[8 + r : 8 + r + CHUNK, :]


def between(before, ref, after):
    def get(r):
        if r < 0:
            return jnp.concatenate([before, ref[0 : CHUNK - 1, :]], axis=0)
        if r + CHUNK > H:
            return jnp.concatenate([ref[r:H, :], after], axis=0)
        return ref[r : r + CHUNK, :]

    return get


def near(*values):
    return [pltpu.with_memory_space_constraint(v, pltpu.VMEM) for v in values]


def far(*values):
    return [pltpu.with_memory_space_constraint(v, pltpu.HBM) for v in values]


def position():
    return [lax.axis_index(axis) for axis in AXES]


def edge_kernel(
    x, drive, courant, diffusion, nest_patch, down, up, params,
    x_top, x_bottom, d_top, d_bottom, c_now, k_now, entries, sems,
):
    copies = [
        pltpu.make_async_copy(source, target, sems.at[i])
        for i, (source, target) in enumerate(
            (
                (x.at[:, 0:8, :], x_top),
                (x.at[:, H - 8 : H, :], x_bottom),
                (drive.at[:, 0:16, :], d_top),
                (drive.at[:, H - 16 : H, :], d_bottom),
                (courant, c_now),
                (diffusion, k_now),
                (nest_patch, entries),
            )
        )
    ]
    for copy in copies:
        copy.start()
    for copy in copies:
        copy.wait()
    for f in range(V):
        down[0, f : f + 1] = x_bottom[f, 7:8, :]
        down[1, f : f + 1] = x_bottom[f, 6:7, :]
        down[2, f : f + 1] = d_bottom[f].astype(F32)[15:16]
        up[0, f : f + 1] = x_top[f, 0:1, :]
        up[1, f : f + 1] = x_top[f, 1:2, :]
        up[2, f : f + 1] = d_top[f].astype(F32)[0:1]

    def put(at, value):
        params[at : at + 1, :] = jnp.full((1, WIDE), value, F32)

    for f in range(V):
        put(f, k_now[f])
    put(COURANT, c_now[0])
    put(COURANT + 1, c_now[1])
    _, row, column = position()
    count = nest_patch.shape[0]
    for member in range(3):
        slot = lax.rem(role_entry(entries, row, column, member, count), 9)
        put(PATCH_ROW + member, lax.div(slot, 3).astype(F32))
        put(PATCH_COL + member, lax.rem(slot, 3).astype(F32))
    put(MEMBER, (row - lax.div(entries[row, column], 9) + 1).astype(F32))


def edge(x, drive, courant, diffusion, nest_patch):
    return pl.pallas_call(
        edge_kernel,
        in_specs=[ANY] * 5,
        out_specs=[VMEM] * 3,
        out_shape=[
            pltpu.VMEM((3, V, W), F32),
            pltpu.VMEM((3, V, W), F32),
            pltpu.VMEM((16, WIDE), F32),
        ],
        scratch_shapes=[
            pltpu.VMEM((V, 8, W), F32),
            pltpu.VMEM((V, 8, W), F32),
            pltpu.VMEM((V, 16, W), BF16),
            pltpu.VMEM((V, 16, W), BF16),
            pltpu.SMEM((2,), F32),
            pltpu.SMEM((V,), F32),
            pltpu.SMEM(nest_patch.shape, jnp.int32),
            pltpu.SemaphoreType.DMA((7,)),
        ],
        compiler_params=SMALL,
        name="edge",
    )(*far(x, drive, courant, diffusion, nest_patch))


def role_entry(entries, row, column, member, count):
    nest = jnp.clip(row + member - 1, 0, count - 1)
    return entries[nest, column]


NT = (((1,), (1,)), ((), ()))


def nests_kernel(
    params, x, drive, y, mean, ends, tent_row, tent_col, two, three, force, thirds
):
    parent = position()[0] == 0

    @pl.when(parent)
    def _():
        ends[...] = jnp.zeros(ends.shape, F32)
        none = -1
        x_west, x_east = select_rows((0, 1), 128), select_rows((none, none, none, 127, 126), 128)
        d_west = select_rows((none, none, 0), 128)
        d_east = select_rows((none, none, none, none, none, 127), 128)
        for f in range(V):
            values = dot_nt(x_west, x[f, :, 0:128]) + dot_nt(x_east, x[f, :, W - 128 : W])
            values = values + lax.dot_general(
                d_west, drive[f, :, 0:128], NT, preferred_element_type=F32
            )
            values = values + lax.dot_general(
                d_east, drive[f, :, W - 128 : W], NT, preferred_element_type=F32
            )
            for i in range(6):
                ends[i, f : f + 1, 0:H] = values[i : i + 1]

    @pl.when(jnp.logical_not(parent))
    def _():
        for buffer in (two, three):
            buffer[0:8, :] = jnp.zeros((8, W), F32)
            buffer[H + 8 : H + 16, :] = jnp.zeros((8, W), F32)
        blocks = mean_matrix()
        zero = jnp.zeros((1, W), F32)
        tent_row[...] = row_tent()
        tent_col[...] = col_tent()

        @pl.loop(0, V)
        def _(f):
            coefs = closed(3.0 * params[pl.ds(f, 1), :][:, 0:W], params)

            def step(get, new, at):
                for r in range(0, H, CHUNK):
                    new[at + r : at + r + CHUNK, :] = step_rows(
                        get, r, coefs, force[r : r + CHUNK, :]
                    )

            force[...] = drive[f].astype(F32) * (1.0 / 3.0)
            step(between(zero, x.at[f], zero), two, 8)
            step(padded(two), three, 8)
            step(padded(three), y.at[f], 0)
            thirds[...] = dot_right(y[f], blocks)
            total = (
                thirds[pl.ds(0, PH, stride=3), :]
                + thirds[pl.ds(1, PH, stride=3), :]
                + thirds[pl.ds(2, PH, stride=3), :]
            )
            mean[f] = total * (1.0 / 9.0)


def mean_matrix():
    gap = iota((W, PW), 0) - 3 * iota((W, PW), 1)
    return jnp.where((gap >= 0) & (gap <= 2), 1.0, 0.0).astype(BF16)


def row_tent():
    tent = jnp.maximum(3 - jnp.abs(iota((256, W), 1) - 3 * iota((256, W), 0) + 2), 0)
    return tent.astype(F32).astype(BF16)


def col_tent():
    tent = jnp.maximum(3 - jnp.abs(iota((H, 256), 0) - 3 * (iota((H, 256), 1) - OFF) + 2), 0)
    return tent.astype(F32).astype(BF16)


def nests(params, x, drive):
    return pl.pallas_call(
        nests_kernel,
        in_specs=[VMEM] * 3,
        out_specs=[VMEM] * 5,
        out_shape=[
            pltpu.VMEM((V, H, W), F32),
            pltpu.VMEM((V, PH, PW), F32),
            pltpu.VMEM((6, V, 256), F32),
            pltpu.VMEM((256, W), BF16),
            pltpu.VMEM((H, 256), BF16),
        ],
        scratch_shapes=[
            pltpu.VMEM((H + 16, W), F32),
            pltpu.VMEM((H + 16, W), F32),
            pltpu.VMEM((H, W), F32),
            pltpu.VMEM((H, PW), F32),
        ],
        compiler_params=SMALL,
        name="nests",
    )(*near(params, x, drive))


def bank_kernel(x, drive, rows, cols):
    @pl.when(position()[0] == 0)
    def _():
        cols[...] = jnp.zeros(cols.shape, F32)
        picks, force_picks = select_rows(BANK_COLS, W), select_rows(IN_COLS, W)
        for f in range(V):
            for i, r in enumerate((0, *BANK_ROWS, H - 1)):
                rows[i, f : f + 1] = x[f, r : r + 1, :]
            for i, r in enumerate(IN_ROWS):
                band = drive[f, r // 16 * 16 : r // 16 * 16 + 16, :].astype(F32)
                rows[10 + i, f : f + 1] = band[r % 16 : r % 16 + 1]
            from_x = dot_nt(picks, x[f])
            from_drive = lax.dot_general(force_picks, drive[f], NT, preferred_element_type=F32)
            for i in range(8):
                cols[i, f : f + 1, 0:H] = from_x[i : i + 1]
            for i in range(4):
                cols[8 + i, f : f + 1, 0:H] = from_drive[i : i + 1]


def banks(x, drive):
    return pl.pallas_call(
        bank_kernel,
        in_specs=[VMEM] * 2,
        out_specs=[VMEM] * 2,
        out_shape=[pltpu.VMEM((14, V, W), F32), pltpu.VMEM((12, V, 256), F32)],
        compiler_params=SMALL,
        name="banks",
    )(*near(x, drive))


def pack_kernel(ends, north, south, to_west, to_east):
    for out, at, lo in ((to_west, 0, 0), (to_east, 3, W - 128)):
        out[0:3] = ends[at : at + 3]
        out[3, :, 0:128] = north[0, :, lo : lo + 128]
        out[3, :, 128:256] = north[1, :, lo : lo + 128]
        out[4, :, 0:128] = north[2, :, lo : lo + 128]
        out[4, :, 128:256] = south[2, :, lo : lo + 128]
        out[5, :, 0:128] = south[0, :, lo : lo + 128]
        out[5, :, 128:256] = south[1, :, lo : lo + 128]


def pack(ends, north, south):
    shape = pltpu.VMEM((6, V, 256), F32)
    return pl.pallas_call(
        pack_kernel,
        in_specs=[VMEM] * 3,
        out_specs=[VMEM] * 2,
        out_shape=[shape, shape],
        compiler_params=SMALL,
        name="pack",
    )(*near(ends, north, south))


def rims_kernel(
    params, shape, rows, cols, ends, north, south, west, east, *out
):
    section, row, column = position()
    count, columns = shape

    @pl.when(section == 0)
    def _():
        k = per_field(params, (V, 1), 0)
        a0, ae, aw, as_, an = weights_of(k, params)
        has_n = jnp.where(row > 0, 1.0, 0.0)
        has_s = jnp.where(row < count - 1, 1.0, 0.0)
        has_w = jnp.where(column > 0, 1.0, 0.0)
        has_e = jnp.where(column < columns - 1, 1.0, 0.0)
        lane128 = iota((V, 128), 1)
        lane256 = iota((V, 256), 1)
        wide = WIDE
        lane_wide = iota((V, wide), 1)
        keep = jnp.where(lane_wide < 128, has_w, jnp.where(lane_wide >= 128 + W, has_e, 1.0))
        near_w, near_e = west[0], east[0]

        def join(before, middle, after):
            return jnp.concatenate([before, middle, after], axis=1)

        def with_sides(middle, left, right):
            return join(
                jnp.where(lane128 == 127, left, 0.0), middle, jnp.where(lane128 == 0, right, 0.0)
            )

        def lanes(value, at):
            return value[:, at : at + 1]

        def halo_row(near, far, force, inner, a_far, a_inner, exists):
            value = (
                a0 * near
                + ae * pltpu.roll(near, wide - 1, 1)
                + aw * pltpu.roll(near, 1, 1)
                + a_far * far
                + a_inner * inner
                + force
            )
            return value * keep * exists

        north_1 = join(west[3, :, 0:128], north[0], east[3, :, 0:128])
        north_2 = join(west[3, :, 128:256], north[1], east[3, :, 128:256])
        north_f = join(west[4, :, 0:128], north[2], east[4, :, 0:128])
        south_1 = join(west[5, :, 0:128], south[0], east[5, :, 0:128])
        south_2 = join(west[5, :, 128:256], south[1], east[5, :, 128:256])
        south_f = join(west[4, :, 128:256], south[2], east[4, :, 128:256])
        top = with_sides(rows[0], lanes(near_w, 0), lanes(near_e, 0))
        bottom = with_sides(rows[9], lanes(near_w, H - 1), lanes(near_e, H - 1))
        new_north = halo_row(north_1, north_2, north_f, top, an, as_, has_n)
        new_south = halo_row(south_1, south_2, south_f, bottom, as_, an, has_s)

        def with_ends(column_values, before, after):
            return jnp.where(
                lane256 == 255, before, jnp.where(lane256 == H, after, column_values)
            )

        def halo_column(near, far, force, inner, a_far, a_inner, exists, at):
            full = with_ends(near, lanes(north_1, at), lanes(south_1, at))
            value = (
                a0 * full
                + as_ * pltpu.roll(full, 255, 1)
                + an * pltpu.roll(full, 1, 1)
                + a_far * far
                + a_inner * inner
                + force
            )
            new = with_ends(value * exists, lanes(new_north, at), lanes(new_south, at))
            return full, new

        at_w, at_e = 127, 128 + W
        old_west, new_west = halo_column(near_w, west[1], west[2], ends[0], aw, ae, has_w, at_w)
        old_east, new_east = halo_column(near_e, east[1], east[2], ends[3], ae, aw, has_e, at_e)

        bank = {(0, 0): north_1, (1, 0): new_north, (0, 5): south_1, (1, 5): new_south}
        side = {(0, 0): old_west, (1, 0): new_west, (0, 5): old_east, (1, 5): new_east}
        blank = jnp.zeros((V, 128), F32)
        for i, r in enumerate(IN_ROWS):
            place, at = (1, 3, 2, 4)[i], 1 + BANK_ROWS.index(r)
            old = with_sides(rows[at], lanes(near_w, r), lanes(near_e, r))
            bank[0, place] = old
            new = (
                a0 * old
                + ae * pltpu.roll(old, wide - 1, 1)
                + aw * pltpu.roll(old, 1, 1)
                + join(blank, an * rows[at - 1] + as_ * rows[at + 1] + rows[10 + i], blank)
            )
            bank[1, place] = jnp.where(
                lane_wide == 127,
                lanes(new_west, r),
                jnp.where(lane_wide == 128 + W, lanes(new_east, r), new),
            )
        for i, c in enumerate(IN_COLS):
            place, at = (1, 3, 2, 4)[i], BANK_COLS.index(c)
            old, new = halo_column(
                cols[at], cols[at - 1], cols[8 + i], cols[at + 1], aw, ae, 1.0, 128 + c
            )
            side[0, place] = old
            side[1, place] = new

        def choose(which, candidates):
            return jnp.where(
                which == 0.0, candidates[0], jnp.where(which == 1.0, candidates[1], candidates[2])
            )

        for member in range(3):
            at = PATCH_ROW + member
            patch_row = params[at : at + 1, :]
            at = PATCH_COL + member
            patch_col = params[at : at + 1, :]
            for time in range(2):
                for half in range(2):
                    line = choose(patch_row, [bank[time, 3 * half + i] for i in range(3)])
                    rim = choose(
                        patch_col[:, 0:W], [line[:, i * PW : i * PW + W] for i in range(3)]
                    )
                    rim = pltpu.roll(rim, W - 127, 1)[:, 0:256]
                    flank = choose(
                        patch_col[:, 0:256], [side[time, 3 * half + i] for i in range(3)]
                    )
                    flank = choose(
                        patch_row[:, 0:256],
                        [pltpu.roll(flank, OFF + 1 - PH * i, 1) for i in range(3)],
                    )
                    flank = jnp.where((lane256 >= OFF) & (lane256 < OFF + PH + 2), flank, 0.0)
                    place = (2 * time + half) * V
                    out[member][place : place + V, :] = jnp.where(lane256 < PW + 2, rim, flank)


def rims(shape, *arrays):
    def kernel(params, *refs):
        rims_kernel(params, shape, *refs)

    return pl.pallas_call(
        kernel,
        in_specs=[VMEM] * 8,
        out_specs=[VMEM] * 3,
        out_shape=[pltpu.VMEM((4 * V, 256), F32)] * 3,
        compiler_params=SMALL,
        name="rims",
    )(*near(*arrays))


def edge_effect(old, new, params, tent_row, tent_col):
    n = old.shape[0]
    k_row = 3.0 * per_field(params, (n, 1), 0)
    a0_row, ae, aw, as_, an = weights_of(k_row, params)
    upper = (iota((n, 1), 0) & V) == 0
    outer, inner = jnp.where(upper, an, as_), jnp.where(upper, as_, an)
    lane = iota((n, W), 1)
    east = jnp.where(lane == W - 1, 0.0, ae)
    west = jnp.where(lane == 0, 0.0, aw)

    def along_row(v):
        return a0_row * v + east * pltpu.roll(v, W - 1, 1) + west * pltpu.roll(v, 1, 1)

    row_effect = depths(
        dot_right(old, tent_row) * (1.0 / 3.0), dot_right(new, tent_row) * (1.0 / 3.0), outer, inner, along_row
    )

    k_col = 3.0 * per_field(params, (1, n), 1)
    a0_col, ae, aw, as_, an = weights_of(k_col, params)
    left = (iota((1, n), 1) & V) == 0
    outer, inner = jnp.where(left, aw, ae), jnp.where(left, ae, aw)
    down = iota((H, n), 0)
    south = jnp.where(down == H - 1, 0.0, as_)
    north = jnp.where(down == 0, 0.0, an)

    def along_column(v):
        return a0_col * v + south * pltpu.roll(v, H - 1, 0) + north * pltpu.roll(v, 1, 0)

    col_effect = depths(
        dot_nt(tent_col, old) * (1.0 / 3.0), dot_nt(tent_col, new) * (1.0 / 3.0), outer, inner, along_column
    )
    return row_effect, col_effect


def depths(old, new, outer, inner, along):
    third = (new - old) * (1.0 / 3.0)
    first_0 = outer * old
    second_0 = along(first_0) + outer * (old + third)
    second_1 = outer * first_0
    third_0 = along(second_0) + inner * second_1 + outer * (old + 2.0 * third)
    third_1 = along(second_1) + outer * second_0
    third_2 = outer * second_1
    return third_0, third_1, third_2


def spread(values, depth, first=0):
    shape = (values.shape[1], 2 * V * 128)
    block, lane = iota(shape, 0) - first, iota(shape, 1)
    target = block * 128 + jnp.where(block < V, depth, 127 - depth)
    return dot_right(values, jnp.where(lane == target, 1.0, 0.0).astype(BF16))


def last_kernel(
    nest_patch, params, x, drive, y, tent_row, tent_col, north, south, west, east,
    sent_0, sent_1, sent_2, got_0, got_1, got_2, mean_0, mean_1, mean_2, out, tile, entries, sems,
):
    section, row, column = position()
    count = nest_patch.shape[0]
    parent = section == 0
    sent, got, means = (sent_0, sent_1, sent_2), (got_0, got_1, got_2), (mean_0, mean_1, mean_2)
    n = 2 * V

    def send(f):
        return pltpu.make_async_copy(tile.at[f], out.at[f], sems.at[f])

    @pl.when(parent)
    def _():
        fetch = pltpu.make_async_copy(nest_patch, entries, sems.at[V])
        fetch.start()
        _, ae, aw, _, _ = weights_of(per_field(params, (1, n), 1), params)
        eye = jnp.where(iota((H, H), 0) == iota((H, H), 1), 1.0, 0.0).astype(BF16)
        beyond = jnp.concatenate([west[0, :, 0:H], east[0, :, 0:H]], axis=0)
        outer = jnp.where(iota((1, n), 1) < V, aw, ae)
        both = spread(dot_nt(eye, beyond) * outer, 0)
        for f in range(V):
            coefs = closed(params[f : f + 1, 0:W], params)
            get = between(north[0, f : f + 1, :], x.at[f], south[0, f : f + 1, :])
            left, right = f * 128, (V + f) * 128
            for r in range(0, H, CHUNK):
                end = r + CHUNK
                value = step_rows(get, r, coefs, drive[f, r:end, :].astype(F32))
                tile[f, r:end, 0:128] = value[:, 0:128] + both[r:end, left : left + 128]
                tile[f, r:end, 128 : W - 128] = value[:, 128 : W - 128]
                tile[f, r:end, W - 128 : W] = (
                    value[:, W - 128 : W] + both[r:end, right : right + 128]
                )
        old = jnp.concatenate([s[0:n, :] for s in sent], axis=0)
        new = jnp.concatenate([s[n : 2 * n, :] for s in sent], axis=0)
        row_effect, col_effect = edge_effect(old, new, params, row_tent(), col_tent())
        by_row = dot_right(sum(row_effect), mean_matrix()) * (1.0 / 9.0)
        thirds = iota((PH, H), 1) - 3 * iota((PH, H), 0)
        thirds = jnp.where((thirds >= 0) & (thirds <= 2), 1.0, 0.0).astype(BF16)
        by_col = dot_left(thirds, sum(col_effect)) * (1.0 / 9.0)
        line = iota((PH, PW), 0)
        fetch.wait()
        for member in range(3):
            nest = row + member - 1
            entry = role_entry(entries, row, column, member, count)
            slot = lax.rem(entry, 9)

            @pl.when((nest >= 0) & (nest < count) & (lax.div(entry, 9) == row))
            def _(member=member, slot=slot):
                at_row = pl.multiple_of(lax.div(slot, 3) * PH, PH)
                at_col = pl.multiple_of(lax.rem(slot, 3) * PW, PW)
                beside = spread(by_col, 0, member * n)
                for f in range(V):
                    left, right, up = f * 128, (V + f) * 128, member * n + f
                    tile[f, pl.ds(at_row, PH), pl.ds(at_col, PW)] = (
                        means[member][f]
                        + jnp.where(line == 0, by_row[up : up + 1], 0.0)
                        + jnp.where(line == PH - 1, by_row[up + V : up + V + 1], 0.0)
                        + beside[:, left : left + 128]
                        + beside[:, right : right + 128]
                    )

        for f in range(V):
            send(f).start()

    @pl.when(jnp.logical_not(parent))
    def _():
        member = params[MEMBER : MEMBER + 1, 0:256]
        u = jnp.where(
            member == 0.0, got[0][...], jnp.where(member == 1.0, got[1][...], got[2][...])
        )
        row_effect, col_effect = edge_effect(
            u[0:n], u[n : 2 * n], params, tent_row[...], tent_col[...]
        )
        both = sum(spread(col_effect[depth], depth) for depth in range(3))
        for f in range(V):
            left, right = f * 128, (V + f) * 128
            tile[f, :, 0:128] = y[f, :, 0:128] + both[:, left : left + 128]
            tile[f, :, 128 : W - 128] = y[f, :, 128 : W - 128]
            tile[f, :, W - 128 : W] = y[f, :, W - 128 : W] + both[:, right : right + 128]
            for depth in range(3):
                bottom = H - 1 - depth
                tile[f, depth : depth + 1, :] = (
                    tile[f, depth : depth + 1, :] + row_effect[depth][f : f + 1]
                )
                tile[f, bottom : bottom + 1, :] = (
                    tile[f, bottom : bottom + 1, :] + row_effect[depth][V + f : V + f + 1]
                )
            send(f).start()

    for f in range(V):
        send(f).wait()


def last(nest_patch, *arrays):
    return pl.pallas_call(
        last_kernel,
        in_specs=[ANY] + [VMEM] * 19,
        out_specs=ANY,
        out_shape=jax.ShapeDtypeStruct((V, H, W), F32),
        scratch_shapes=[
            pltpu.VMEM((V, H, W), F32),
            pltpu.SMEM(nest_patch.shape, jnp.int32),
            pltpu.SemaphoreType.DMA((V + 1,)),
        ],
        compiler_params=SMALL,
        name="last",
    )(*far(nest_patch), *near(*arrays))


def routes(sizes, source, move):
    _, n_rows, n_cols = sizes
    out = []
    for r in range(n_rows):
        for c in range(n_cols):
            to_sec, to_r, to_c = move(r, c)
            if 0 <= to_r < n_rows and 0 <= to_c < n_cols:
                out.append(
                    (
                        (source * n_rows + r) * n_cols + c,
                        (to_sec * n_rows + to_r) * n_cols + to_c,
                    )
                )
    return out


def on_device(sizes, *arrays):
    return compute(sizes, *arrays)


def compute(sizes, fields, forcing, courant, diffusion, nest_patch):
    x = fields.reshape(V, H, W)
    drive = forcing.reshape(V, H, W)
    courant = courant.reshape(2)

    def shift(value, source, move):
        return lax.ppermute(value, AXES, routes(sizes, source, move))

    downward, upward, params = edge(x, drive, courant, diffusion, nest_patch)
    north = shift(downward, 0, lambda r, c: (0, r + 1, c))
    south = shift(upward, 0, lambda r, c: (0, r - 1, c))
    y, mean, ends, *tents = nests(params, x, drive)
    means = [shift(mean, 1, lambda r, c, m=m: (0, r + 1 - m, c)) for m in range(3)]
    to_west, to_east = pack(ends, north, south)
    west = shift(to_east, 0, lambda r, c: (0, r, c + 1))
    east = shift(to_west, 0, lambda r, c: (0, r, c - 1))
    rows, cols = banks(x, drive)
    halos = north, south, west, east
    sent = rims(sizes[1:], params, rows, cols, ends, *halos)
    got = [shift(sent[m], 0, lambda r, c, m=m: (1, r + m - 1, c)) for m in range(3)]
    out = last(nest_patch, params, x, drive, y, *tents, *halos, *sent, *got, *means)
    return out.reshape(fields.shape)


def solution(mesh):
    sizes = tuple(mesh.shape[axis] for axis in AXES)
    spec = P("sec", None, None, "gy", "gx")
    return jax.shard_map(
        functools.partial(on_device, sizes),
        mesh=mesh,
        in_specs=(spec, spec, P(), P(), P()),
        out_specs=spec,
        check_vma=False,
    )
```

time: 54.6 us -> 48.6 us (0.89)
  the two profiles are of different devices: /device:TPU:91 before, /device:TPU:93 now
where the time goes in v2:
time: 48.6 us; the launch traced here: 48.3 us
  waiting for transfers between devices  24.8 us (51%)
  starting transfers between devices  16.1 us (33%)
  Pallas kernels  6.84 us (14%)
    ppermute x10, waiting for transfers between devices, shift(): return lax.ppermute(value, AXES, routes(sizes, source, move))  24.8 us
    ppermute x10, starting transfers between devices, shift(): return lax.ppermute(value, AXES, routes(sizes, source, move))  16.1 us
    pallas_call x1, Pallas kernels, nests(): pl.pallas_call(nests_kernel, in_specs=[VMEM] * 3, out_specs=[VMEM] * 5, o...  3.42 us
    pallas_call x1, Pallas kernels, last(): pl.pallas_call(last_kernel, in_specs=[ANY] + [VMEM] * 19, out_specs=ANY,...  2.22 us
    pallas_call x1, Pallas kernels, edge(): pl.pallas_call(edge_kernel, in_specs=[ANY] * 5, out_specs=[VMEM] * 3, out...  1.15 us
  transfers between devices with their start and end apart: 10, of which 2 were waited for; matrix products, arithmetic and copies ran while one was open for 0% of the time, Pallas kernels for 0%

profile of v2, /device:TPU:93, one launch (start us, length us, event | category | flops | bytes accessed | tf_op | source)
XLA Modules:
  0.0 48.3 jit_solution(12226325036823651370)
XLA Ops:
  0.0 0.0 copy-start.1
  0.0 0.0 copy-start
  0.0 1.1 %edge.1 = (f32[3,4,384]{2,1,0:T(4,128)S(1)}, f32[3,4,384]{2,1,0:T(4,128)S(1)}, f32[16,640]{1,0:T(8,128)S(1)}) custom-call(f32[4,192,384]{2,1,0:T(8,128)} %bitcast.6, bf16[4,192,384]{2,1,0:T(8,128)(2,1)} %bitcast.10, f32[2]{0:T(128)} %bitcast.14, f32[4]{0:T(128)} %diffusion.1, s32[16,16]{1,0:T(8,128)} %nest_patch.3), custom_call_target="tpu_custom_call" | custom-call | tf_op jit(solution)/shard_map/edge/pallas_call | solution.py:178
  1.2 0.0 copy-done.1
  1.2 0.4 copy-done
  1.6 3.4 %nests.1 = (f32[4,192,384]{2,1,0:T(8,128)S(1)}, f32[4,64,128]{2,1,0:T(8,128)S(1)}, f32[6,4,256]{2,1,0:T(4,128)S(1)}, bf16[256,384]{1,0:T(8,128)(2,1)S(1)}, bf16[192,256]{1,0:T(8,128)(2,1)S(1)}) custom-call(f32[16,640]{1,0:T(8,128)S(1)} %get-tuple-element.20.params, f32[4,192,384]{2,1,0:T(8,128)S(1)} %bitcast.7, bf16[4,192,384]{2,1,0:T(8,128)(2,1)S(1)} %bitcast.11), custom_call_target="tpu_custom_call" | custom-call | tf_op jit(solution)/shard_map/nests/pallas_call | solution.py:282
  5.0 7.0 %collective-permute-start.9 = (f32[4,64,128]{2,1,0:T(8,128)S(1)}, f32[4,64,128]{2,1,0:T(8,128)S(1)}, u32[]{:S(2)}, u32[]{:S(2)}) collective-permute-start(f32[4,64,128]{2,1,0:T(8,128)S(1)} %get-tuple-element.34), channel_id=1, source_target_pairs={{272,0},{273,1},{274,2},{275,3},{276,4},{277,5},{278,6},{279,7},{2... | collective-permute-start | bytes 393224 | tf_op jit(solution)/shard_map/ppermute | solution.py:691
  12.0 1.3 %collective-permute-start.8 = (f32[4,64,128]{2,1,0:T(8,128)S(1)}, f32[4,64,128]{2,1,0:T(8,128)S(1)}, u32[]{:S(2)}, u32[]{:S(2)}) collective-permute-start(f32[4,64,128]{2,1,0:T(8,128)S(1)} %get-tuple-element.34), channel_id=1, source_target_pairs={{256,0},{257,1},{258,2},{259,3},{260,4},{261,5},{262,6},{263,7},{2... | collective-permute-start | bytes 393224 | tf_op jit(solution)/shard_map/ppermute | solution.py:691
  13.3 1.3 %collective-permute-start.7 = (f32[4,64,128]{2,1,0:T(8,128)S(1)}, f32[4,64,128]{2,1,0:T(8,128)S(1)}, u32[]{:S(2)}, u32[]{:S(2)}) collective-permute-start(f32[4,64,128]{2,1,0:T(8,128)S(1)} %get-tuple-element.34), channel_id=1, source_target_pairs={{256,16},{257,17},{258,18},{259,19},{260,20},{261,21},{262,22},{26... | collective-permute-start | bytes 393224 | tf_op jit(solution)/shard_map/ppermute | solution.py:691
  14.6 0.7 %collective-permute-start = (f32[3,4,384]{2,1,0:T(4,128)S(1)}, f32[3,4,384]{2,1,0:T(4,128)S(1)}, u32[]{:S(2)}, u32[]{:S(2)}) collective-permute-start(f32[3,4,384]{2,1,0:T(4,128)S(1)} %get-tuple-element.24), channel_id=1, source_target_pairs={{0,16},{1,17},{2,18},{3,19},{4,20},{5,21},{6,22},{7,23},{8,24},{9,... | collective-permute-start | bytes 55304 | tf_op jit(solution)/shard_map/ppermute | solution.py:691
  15.3 0.7 %collective-permute-start.1 = (f32[3,4,384]{2,1,0:T(4,128)S(1)}, f32[3,4,384]{2,1,0:T(4,128)S(1)}, u32[]{:S(2)}, u32[]{:S(2)}) collective-permute-start(f32[3,4,384]{2,1,0:T(4,128)S(1)} %get-tuple-element.25), channel_id=1, source_target_pairs={{16,0},{17,1},{18,2},{19,3},{20,4},{21,5},{22,6},{23,7},{24,8},{25... | collective-permute-start | bytes 55304 | tf_op jit(solution)/shard_map/ppermute | solution.py:691
  16.0 0.0 collective-permute-done.north.refs_3_
  16.0 0.0 collective-permute-done.1.south.refs_4_
  16.0 0.7 %collective-permute-start.2 = (f32[6,4,256]{2,1,0:T(4,128)S(1)}, f32[6,4,256]{2,1,0:T(4,128)S(1)}, u32[]{:S(2)}, u32[]{:S(2)}) collective-permute-start(f32[6,4,256]{2,1,0:T(4,128)S(1)} %get-tuple-element.27), channel_id=1, source_target_pairs={{0,1},{1,2},{2,3},{3,4},{4,5},{5,6},{6,7},{7,8},{8,9},{9,10},{10,1... | collective-permute-start | bytes 73736 | tf_op jit(solution)/shard_map/ppermute | solution.py:691
  16.7 0.7 %collective-permute-start.3 = (f32[6,4,256]{2,1,0:T(4,128)S(1)}, f32[6,4,256]{2,1,0:T(4,128)S(1)}, u32[]{:S(2)}, u32[]{:S(2)}) collective-permute-start(f32[6,4,256]{2,1,0:T(4,128)S(1)} %get-tuple-element.28), channel_id=1, source_target_pairs={{1,0},{2,1},{3,2},{4,3},{5,4},{6,5},{7,6},{8,7},{9,8},{10,9},{11,1... | collective-permute-start | bytes 73736 | tf_op jit(solution)/shard_map/ppermute | solution.py:691
  17.4 0.0 collective-permute-done.2.refs_5_.west
  17.4 0.0 collective-permute-done.3.refs_6_.east
  17.4 1.3 %collective-permute-start.4 = (f32[16,256]{1,0:T(8,128)S(1)}, f32[16,256]{1,0:T(8,128)S(1)}, u32[]{:S(2)}, u32[]{:S(2)}) collective-permute-start(f32[16,256]{1,0:T(8,128)S(1)} %get-tuple-element.31.sent_0), channel_id=1, source_target_pairs={{16,256},{17,257},{18,258},{19,259},{20,260},{21,261},{22,262},{23... | collective-permute-start | bytes 49160 | tf_op jit(solution)/shard_map/ppermute | solution.py:691
  18.7 1.3 %collective-permute-start.5 = (f32[16,256]{1,0:T(8,128)S(1)}, f32[16,256]{1,0:T(8,128)S(1)}, u32[]{:S(2)}, u32[]{:S(2)}) collective-permute-start(f32[16,256]{1,0:T(8,128)S(1)} %get-tuple-element.32.sent_1), channel_id=1, source_target_pairs={{0,256},{1,257},{2,258},{3,259},{4,260},{5,261},{6,262},{7,263},{8... | collective-permute-start | bytes 49160 | tf_op jit(solution)/shard_map/ppermute | solution.py:691
  20.0 17.7 %collective-permute-done.4.got_0 = f32[16,256]{1,0:T(8,128)S(1)} collective-permute-done((f32[16,256]{1,0:T(8,128)S(1)}, f32[16,256]{1,0:T(8,128)S(1)}, u32[]{:S(2)}, u32[]{:S(2)}) %collective-permute-start.4) | collective-permute-done | bytes 16416 | tf_op jit(solution)/shard_map/ppermute | solution.py:691
  37.7 1.3 %collective-permute-start.6 = (f32[16,256]{1,0:T(8,128)S(1)}, f32[16,256]{1,0:T(8,128)S(1)}, u32[]{:S(2)}, u32[]{:S(2)}) collective-permute-start(f32[16,256]{1,0:T(8,128)S(1)} %get-tuple-element.33.sent_2), channel_id=1, source_target_pairs={{0,272},{1,273},{2,274},{3,275},{4,276},{5,277},{6,278},{7,279},{8... | collective-permute-start | bytes 49160 | tf_op jit(solution)/shard_map/ppermute | solution.py:691
  39.0 0.0 collective-permute-done.5.got_1
  39.0 7.1 %collective-permute-done.6.got_2 = f32[16,256]{1,0:T(8,128)S(1)} collective-permute-done((f32[16,256]{1,0:T(8,128)S(1)}, f32[16,256]{1,0:T(8,128)S(1)}, u32[]{:S(2)}, u32[]{:S(2)}) %collective-permute-start.6) | collective-permute-done | bytes 16416 | tf_op jit(solution)/shard_map/ppermute | solution.py:691
  46.1 0.0 collective-permute-done.9.mean_2
  46.1 0.0 collective-permute-done.8.mean_1
  46.1 0.0 collective-permute-done.7.mean_0
  46.1 2.2 %last.1 = f32[4,192,384]{2,1,0:T(8,128)} custom-call(s32[16,16]{1,0:T(8,128)} %nest_patch.3, f32[16,640]{1,0:T(8,128)S(1)} %get-tuple-element.20.params, f32[4,192,384]{2,1,0:T(8,128)S(1)} %bitcast.9, bf16[4,192,384]{2,1,0:T(8,128)(2,1)S(1)} %bitcast.13, f32[4,192,384]{2,1,0:T(8,128)S(1)} %get-tuple-element.21.y, ...), custom_call_target="tpu_custom_call" | custom-call | tf_op jit(solution)/shard_map/last/pallas_call | solution.py:650
  (3 shorter events, 0.0 us)
Async XLA Ops:
  0.0 1.2 %copy-start.1 = (bf16[1,4,1,192,384]{4,3,2,1,0:T(8,128)(2,1)S(1)}, bf16[1,4,1,192,384]{4,3,2,1,0:T(8,128)(2,1)}, u32[]{:S(2)}) copy-start(bf16[1,4,1,192,384]{4,3,2,1,0:T(8,128)(2,1)} %param.6) | copy-start | bytes 1769476
  0.0 1.5 %copy-start = (f32[1,4,1,192,384]{4,3,2,1,0:T(8,128)S(1)}, f32[1,4,1,192,384]{4,3,2,1,0:T(8,128)}, u32[]{:S(2)}) copy-start(f32[1,4,1,192,384]{4,3,2,1,0:T(8,128)} %param.5) | copy-start | bytes 3538948
  5.0 41.1 %collective-permute-start.9 = (f32[4,64,128]{2,1,0:T(8,128)S(1)}, f32[4,64,128]{2,1,0:T(8,128)S(1)}, u32[]{:S(2)}, u32[]{:S(2)}) collective-permute-start(f32[4,64,128]{2,1,0:T(8,128)S(1)} %get-tuple-element.34), channel_id=1, source_target_pairs={{272,0},{273,1},{274,2},{275,3},{276,4},{277,5},{278,6},{279,7},{2... | collective-permute-start | bytes 393224 | tf_op jit(solution)/shard_map/ppermute | solution.py:691
  12.0 34.1 %collective-permute-start.8 = (f32[4,64,128]{2,1,0:T(8,128)S(1)}, f32[4,64,128]{2,1,0:T(8,128)S(1)}, u32[]{:S(2)}, u32[]{:S(2)}) collective-permute-start(f32[4,64,128]{2,1,0:T(8,128)S(1)} %get-tuple-element.34), channel_id=1, source_target_pairs={{256,0},{257,1},{258,2},{259,3},{260,4},{261,5},{262,6},{263,7},{2... | collective-permute-start | bytes 393224 | tf_op jit(solution)/shard_map/ppermute | solution.py:691
  13.3 32.8 %collective-permute-start.7 = (f32[4,64,128]{2,1,0:T(8,128)S(1)}, f32[4,64,128]{2,1,0:T(8,128)S(1)}, u32[]{:S(2)}, u32[]{:S(2)}) collective-permute-start(f32[4,64,128]{2,1,0:T(8,128)S(1)} %get-tuple-element.34), channel_id=1, source_target_pairs={{256,16},{257,17},{258,18},{259,19},{260,20},{261,21},{262,22},{26... | collective-permute-start | bytes 393224 | tf_op jit(solution)/shard_map/ppermute | solution.py:691
  14.6 1.3 %collective-permute-start = (f32[3,4,384]{2,1,0:T(4,128)S(1)}, f32[3,4,384]{2,1,0:T(4,128)S(1)}, u32[]{:S(2)}, u32[]{:S(2)}) collective-permute-start(f32[3,4,384]{2,1,0:T(4,128)S(1)} %get-tuple-element.24), channel_id=1, source_target_pairs={{0,16},{1,17},{2,18},{3,19},{4,20},{5,21},{6,22},{7,23},{8,24},{9,... | collective-permute-start | bytes 55304 | tf_op jit(solution)/shard_map/ppermute | solution.py:691
  15.3 0.7 %collective-permute-start.1 = (f32[3,4,384]{2,1,0:T(4,128)S(1)}, f32[3,4,384]{2,1,0:T(4,128)S(1)}, u32[]{:S(2)}, u32[]{:S(2)}) collective-permute-start(f32[3,4,384]{2,1,0:T(4,128)S(1)} %get-tuple-element.25), channel_id=1, source_target_pairs={{16,0},{17,1},{18,2},{19,3},{20,4},{21,5},{22,6},{23,7},{24,8},{25... | collective-permute-start | bytes 55304 | tf_op jit(solution)/shard_map/ppermute | solution.py:691
  16.0 1.4 %collective-permute-start.2 = (f32[6,4,256]{2,1,0:T(4,128)S(1)}, f32[6,4,256]{2,1,0:T(4,128)S(1)}, u32[]{:S(2)}, u32[]{:S(2)}) collective-permute-start(f32[6,4,256]{2,1,0:T(4,128)S(1)} %get-tuple-element.27), channel_id=1, source_target_pairs={{0,1},{1,2},{2,3},{3,4},{4,5},{5,6},{6,7},{7,8},{8,9},{9,10},{10,1... | collective-permute-start | bytes 73736 | tf_op jit(solution)/shard_map/ppermute | solution.py:691
  16.7 0.7 %collective-permute-start.3 = (f32[6,4,256]{2,1,0:T(4,128)S(1)}, f32[6,4,256]{2,1,0:T(4,128)S(1)}, u32[]{:S(2)}, u32[]{:S(2)}) collective-permute-start(f32[6,4,256]{2,1,0:T(4,128)S(1)} %get-tuple-element.28), channel_id=1, source_target_pairs={{1,0},{2,1},{3,2},{4,3},{5,4},{6,5},{7,6},{8,7},{9,8},{10,9},{11,1... | collective-permute-start | bytes 73736 | tf_op jit(solution)/shard_map/ppermute | solution.py:691
  17.4 20.3 %collective-permute-start.4 = (f32[16,256]{1,0:T(8,128)S(1)}, f32[16,256]{1,0:T(8,128)S(1)}, u32[]{:S(2)}, u32[]{:S(2)}) collective-permute-start(f32[16,256]{1,0:T(8,128)S(1)} %get-tuple-element.31.sent_0), channel_id=1, source_target_pairs={{16,256},{17,257},{18,258},{19,259},{20,260},{21,261},{22,262},{23... | collective-permute-start | bytes 49160 | tf_op jit(solution)/shard_map/ppermute | solution.py:691
  18.7 20.3 %collective-permute-start.5 = (f32[16,256]{1,0:T(8,128)S(1)}, f32[16,256]{1,0:T(8,128)S(1)}, u32[]{:S(2)}, u32[]{:S(2)}) collective-permute-start(f32[16,256]{1,0:T(8,128)S(1)} %get-tuple-element.32.sent_1), channel_id=1, source_target_pairs={{0,256},{1,257},{2,258},{3,259},{4,260},{5,261},{6,262},{7,263},{8... | collective-permute-start | bytes 49160 | tf_op jit(solution)/shard_map/ppermute | solution.py:691
  37.7 8.4 %collective-permute-start.6 = (f32[16,256]{1,0:T(8,128)S(1)}, f32[16,256]{1,0:T(8,128)S(1)}, u32[]{:S(2)}, u32[]{:S(2)}) collective-permute-start(f32[16,256]{1,0:T(8,128)S(1)} %get-tuple-element.33.sent_2), channel_id=1, source_target_pairs={{0,272},{1,273},{2,274},{3,275},{4,276},{5,277},{6,278},{7,279},{8... | collective-permute-start | bytes 49160 | tf_op jit(solution)/shard_map/ppermute | solution.py:691

commit v3 on v2

--- a/solution.py
+++ b/solution.py
@@ -516,6 +516,8 @@
         dot_right(old, tent_row) * (1.0 / 3.0), dot_right(new, tent_row) * (1.0 / 3.0), outer, inner, along_row
     )
 
+    if n == 2 * V:
+        old, new, n = jnp.concatenate([old] * 3, axis=0), jnp.concatenate([new] * 3, axis=0), 3 * n
     k_col = 3.0 * per_field(params, (1, n), 1)
     a0_col, ae, aw, as_, an = weights_of(k_col, params)
     left = (iota((1, n), 1) & V) == 0
@@ -544,11 +546,13 @@
     return third_0, third_1, third_2
 
 
-def spread(values, depth, first=0):
+def spread(values, first=0):
     shape = (values.shape[1], 2 * V * 128)
-    block, lane = iota(shape, 0) - first, iota(shape, 1)
+    index, lane = iota(shape, 0) - first, iota(shape, 1)
+    block, depth = index & (2 * V - 1), index >> 3
     target = block * 128 + jnp.where(block < V, depth, 127 - depth)
-    return dot_right(values, jnp.where(lane == target, 1.0, 0.0).astype(BF16))
+    valid = (index >= 0) & (depth < 3)
+    return dot_right(values, jnp.where((lane == target) & valid, 1.0, 0.0).astype(BF16))
 
 
 def last_kernel(
@@ -572,7 +576,7 @@
         eye = jnp.where(iota((H, H), 0) == iota((H, H), 1), 1.0, 0.0).astype(BF16)
         beyond = jnp.concatenate([west[0, :, 0:H], east[0, :, 0:H]], axis=0)
         outer = jnp.where(iota((1, n), 1) < V, aw, ae)
-        both = spread(dot_nt(eye, beyond) * outer, 0)
+        both = spread(dot_nt(eye, beyond) * outer)
         for f in range(V):
             coefs = closed(params[f : f + 1, 0:W], params)
             get = between(north[0, f : f + 1, :], x.at[f], south[0, f : f + 1, :])
@@ -603,7 +607,8 @@
             def _(member=member, slot=slot):
                 at_row = pl.multiple_of(lax.div(slot, 3) * PH, PH)
                 at_col = pl.multiple_of(lax.rem(slot, 3) * PW, PW)
-                beside = spread(by_col, 0, member * n)
+                mine = (iota(by_col.shape, 1) >> 3) == member
+                beside = spread(jnp.where(mine, by_col, 0.0), member * n)
                 for f in range(V):
                     left, right, up = f * 128, (V + f) * 128, member * n + f
                     tile[f, pl.ds(at_row, PH), pl.ds(at_col, PW)] = (
@@ -626,7 +631,12 @@
         row_effect, col_effect = edge_effect(
             u[0:n], u[n : 2 * n], params, tent_row[...], tent_col[...]
         )
-        both = sum(spread(col_effect[depth], depth) for depth in range(3))
+        depth = iota(col_effect[0].shape, 1) >> 3
+        both = spread(
+            jnp.where(
+                depth == 0, col_effect[0], jnp.where(depth == 1, col_effect[1], col_effect[2])
+            )
+        )
         for f in range(V):
             left, right = f * 128, (V + f) * 128
             tile[f, :, 0:128] = y[f, :, 0:128] + both[:, left : left + 128]

time: 48.6 us -> 48.3 us (level)
  the two profiles are of different devices: /device:TPU:93 before, /device:TPU:91 now
where the time goes in v3:
time: 48.3 us; the launch traced here: 47.9 us
  waiting for transfers between devices  24.8 us (51%)
  starting transfers between devices  16.1 us (33%)
  Pallas kernels  6.48 us (13%)
    ppermute x10, waiting for transfers between devices, shift(): return lax.ppermute(value, AXES, routes(sizes, source, move))  24.8 us
    ppermute x10, starting transfers between devices, shift(): return lax.ppermute(value, AXES, routes(sizes, source, move))  16.1 us
    pallas_call x1, Pallas kernels, nests(): pl.pallas_call(nests_kernel, in_specs=[VMEM] * 3, out_specs=[VMEM] * 5, o...  3.42 us
    pallas_call x1, Pallas kernels, last(): pl.pallas_call(last_kernel, in_specs=[ANY] + [VMEM] * 19, out_specs=ANY,...  1.86 us
    pallas_call x1, Pallas kernels, edge(): pl.pallas_call(edge_kernel, in_specs=[ANY] * 5, out_specs=[VMEM] * 3, out...  1.15 us
  transfers between devices with their start and end apart: 10, of which 2 were waited for; matrix products, arithmetic and copies ran while one was open for 0% of the time, Pallas kernels for 0%

profile of v3, /device:TPU:91, one launch (start us, length us, event | category | flops | bytes accessed | tf_op | source)
XLA Modules:
  0.0 47.9 jit_solution(16442423192814509061)
XLA Ops:
  0.0 0.0 copy-start.1
  0.0 0.0 copy-start
  0.0 1.1 %edge.1 = (f32[3,4,384]{2,1,0:T(4,128)S(1)}, f32[3,4,384]{2,1,0:T(4,128)S(1)}, f32[16,640]{1,0:T(8,128)S(1)}) custom-call(f32[4,192,384]{2,1,0:T(8,128)} %bitcast.6, bf16[4,192,384]{2,1,0:T(8,128)(2,1)} %bitcast.10, f32[2]{0:T(128)} %bitcast.14, f32[4]{0:T(128)} %diffusion.1, s32[16,16]{1,0:T(8,128)} %nest_patch.3), custom_call_target="tpu_custom_call" | custom-call | tf_op jit(solution)/shard_map/edge/pallas_call | solution.py:178
  1.2 0.0 copy-done.1
  1.2 0.4 copy-done
  1.6 3.4 %nests.1 = (f32[4,192,384]{2,1,0:T(8,128)S(1)}, f32[4,64,128]{2,1,0:T(8,128)S(1)}, f32[6,4,256]{2,1,0:T(4,128)S(1)}, bf16[256,384]{1,0:T(8,128)(2,1)S(1)}, bf16[192,256]{1,0:T(8,128)(2,1)S(1)}) custom-call(f32[16,640]{1,0:T(8,128)S(1)} %get-tuple-element.20.params, f32[4,192,384]{2,1,0:T(8,128)S(1)} %bitcast.7, bf16[4,192,384]{2,1,0:T(8,128)(2,1)S(1)} %bitcast.11), custom_call_target="tpu_custom_call" | custom-call | tf_op jit(solution)/shard_map/nests/pallas_call | solution.py:282
  5.0 7.0 %collective-permute-start.9 = (f32[4,64,128]{2,1,0:T(8,128)S(1)}, f32[4,64,128]{2,1,0:T(8,128)S(1)}, u32[]{:S(2)}, u32[]{:S(2)}) collective-permute-start(f32[4,64,128]{2,1,0:T(8,128)S(1)} %get-tuple-element.34), channel_id=1, source_target_pairs={{272,0},{273,1},{274,2},{275,3},{276,4},{277,5},{278,6},{279,7},{2... | collective-permute-start | bytes 393224 | tf_op jit(solution)/shard_map/ppermute | solution.py:701
  12.0 1.3 %collective-permute-start.8 = (f32[4,64,128]{2,1,0:T(8,128)S(1)}, f32[4,64,128]{2,1,0:T(8,128)S(1)}, u32[]{:S(2)}, u32[]{:S(2)}) collective-permute-start(f32[4,64,128]{2,1,0:T(8,128)S(1)} %get-tuple-element.34), channel_id=1, source_target_pairs={{256,0},{257,1},{258,2},{259,3},{260,4},{261,5},{262,6},{263,7},{2... | collective-permute-start | bytes 393224 | tf_op jit(solution)/shard_map/ppermute | solution.py:701
  13.3 1.3 %collective-permute-start.7 = (f32[4,64,128]{2,1,0:T(8,128)S(1)}, f32[4,64,128]{2,1,0:T(8,128)S(1)}, u32[]{:S(2)}, u32[]{:S(2)}) collective-permute-start(f32[4,64,128]{2,1,0:T(8,128)S(1)} %get-tuple-element.34), channel_id=1, source_target_pairs={{256,16},{257,17},{258,18},{259,19},{260,20},{261,21},{262,22},{26... | collective-permute-start | bytes 393224 | tf_op jit(solution)/shard_map/ppermute | solution.py:701
  14.6 0.7 %collective-permute-start = (f32[3,4,384]{2,1,0:T(4,128)S(1)}, f32[3,4,384]{2,1,0:T(4,128)S(1)}, u32[]{:S(2)}, u32[]{:S(2)}) collective-permute-start(f32[3,4,384]{2,1,0:T(4,128)S(1)} %get-tuple-element.24), channel_id=1, source_target_pairs={{0,16},{1,17},{2,18},{3,19},{4,20},{5,21},{6,22},{7,23},{8,24},{9,... | collective-permute-start | bytes 55304 | tf_op jit(solution)/shard_map/ppermute | solution.py:701
  15.3 0.7 %collective-permute-start.1 = (f32[3,4,384]{2,1,0:T(4,128)S(1)}, f32[3,4,384]{2,1,0:T(4,128)S(1)}, u32[]{:S(2)}, u32[]{:S(2)}) collective-permute-start(f32[3,4,384]{2,1,0:T(4,128)S(1)} %get-tuple-element.25), channel_id=1, source_target_pairs={{16,0},{17,1},{18,2},{19,3},{20,4},{21,5},{22,6},{23,7},{24,8},{25... | collective-permute-start | bytes 55304 | tf_op jit(solution)/shard_map/ppermute | solution.py:701
  16.0 0.0 collective-permute-done.north.refs_3_
  16.0 0.0 collective-permute-done.1.south.refs_4_
  16.0 0.7 %collective-permute-start.2 = (f32[6,4,256]{2,1,0:T(4,128)S(1)}, f32[6,4,256]{2,1,0:T(4,128)S(1)}, u32[]{:S(2)}, u32[]{:S(2)}) collective-permute-start(f32[6,4,256]{2,1,0:T(4,128)S(1)} %get-tuple-element.27), channel_id=1, source_target_pairs={{0,1},{1,2},{2,3},{3,4},{4,5},{5,6},{6,7},{7,8},{8,9},{9,10},{10,1... | collective-permute-start | bytes 73736 | tf_op jit(solution)/shard_map/ppermute | solution.py:701
  16.7 0.7 %collective-permute-start.3 = (f32[6,4,256]{2,1,0:T(4,128)S(1)}, f32[6,4,256]{2,1,0:T(4,128)S(1)}, u32[]{:S(2)}, u32[]{:S(2)}) collective-permute-start(f32[6,4,256]{2,1,0:T(4,128)S(1)} %get-tuple-element.28), channel_id=1, source_target_pairs={{1,0},{2,1},{3,2},{4,3},{5,4},{6,5},{7,6},{8,7},{9,8},{10,9},{11,1... | collective-permute-start | bytes 73736 | tf_op jit(solution)/shard_map/ppermute | solution.py:701
  17.4 0.0 collective-permute-done.2.refs_5_.west
  17.4 0.0 collective-permute-done.3.refs_6_.east
  17.4 1.3 %collective-permute-start.4 = (f32[16,256]{1,0:T(8,128)S(1)}, f32[16,256]{1,0:T(8,128)S(1)}, u32[]{:S(2)}, u32[]{:S(2)}) collective-permute-start(f32[16,256]{1,0:T(8,128)S(1)} %get-tuple-element.31.sent_0), channel_id=1, source_target_pairs={{16,256},{17,257},{18,258},{19,259},{20,260},{21,261},{22,262},{23... | collective-permute-start | bytes 49160 | tf_op jit(solution)/shard_map/ppermute | solution.py:701
  18.7 1.3 %collective-permute-start.5 = (f32[16,256]{1,0:T(8,128)S(1)}, f32[16,256]{1,0:T(8,128)S(1)}, u32[]{:S(2)}, u32[]{:S(2)}) collective-permute-start(f32[16,256]{1,0:T(8,128)S(1)} %get-tuple-element.32.sent_1), channel_id=1, source_target_pairs={{0,256},{1,257},{2,258},{3,259},{4,260},{5,261},{6,262},{7,263},{8... | collective-permute-start | bytes 49160 | tf_op jit(solution)/shard_map/ppermute | solution.py:701
  20.0 17.7 %collective-permute-done.4.got_0 = f32[16,256]{1,0:T(8,128)S(1)} collective-permute-done((f32[16,256]{1,0:T(8,128)S(1)}, f32[16,256]{1,0:T(8,128)S(1)}, u32[]{:S(2)}, u32[]{:S(2)}) %collective-permute-start.4) | collective-permute-done | bytes 16416 | tf_op jit(solution)/shard_map/ppermute | solution.py:701
  37.7 1.3 %collective-permute-start.6 = (f32[16,256]{1,0:T(8,128)S(1)}, f32[16,256]{1,0:T(8,128)S(1)}, u32[]{:S(2)}, u32[]{:S(2)}) collective-permute-start(f32[16,256]{1,0:T(8,128)S(1)} %get-tuple-element.33.sent_2), channel_id=1, source_target_pairs={{0,272},{1,273},{2,274},{3,275},{4,276},{5,277},{6,278},{7,279},{8... | collective-permute-start | bytes 49160 | tf_op jit(solution)/shard_map/ppermute | solution.py:701
  39.0 0.0 collective-permute-done.5.got_1
  39.0 7.1 %collective-permute-done.6.got_2 = f32[16,256]{1,0:T(8,128)S(1)} collective-permute-done((f32[16,256]{1,0:T(8,128)S(1)}, f32[16,256]{1,0:T(8,128)S(1)}, u32[]{:S(2)}, u32[]{:S(2)}) %collective-permute-start.6) | collective-permute-done | bytes 16416 | tf_op jit(solution)/shard_map/ppermute | solution.py:701
  46.1 0.0 collective-permute-done.9.mean_2
  46.1 0.0 collective-permute-done.8.mean_1
  46.1 0.0 collective-permute-done.7.mean_0
  46.1 1.9 %last.1 = f32[4,192,384]{2,1,0:T(8,128)} custom-call(s32[16,16]{1,0:T(8,128)} %nest_patch.3, f32[16,640]{1,0:T(8,128)S(1)} %get-tuple-element.20.params, f32[4,192,384]{2,1,0:T(8,128)S(1)} %bitcast.9, bf16[4,192,384]{2,1,0:T(8,128)(2,1)S(1)} %bitcast.13, f32[4,192,384]{2,1,0:T(8,128)S(1)} %get-tuple-element.21.y, ...), custom_call_target="tpu_custom_call" | custom-call | tf_op jit(solution)/shard_map/last/pallas_call | solution.py:660
  (3 shorter events, 0.0 us)
Async XLA Ops:
  0.0 1.2 %copy-start.1 = (bf16[1,4,1,192,384]{4,3,2,1,0:T(8,128)(2,1)S(1)}, bf16[1,4,1,192,384]{4,3,2,1,0:T(8,128)(2,1)}, u32[]{:S(2)}) copy-start(bf16[1,4,1,192,384]{4,3,2,1,0:T(8,128)(2,1)} %param.6) | copy-start | bytes 1769476
  0.0 1.5 %copy-start = (f32[1,4,1,192,384]{4,3,2,1,0:T(8,128)S(1)}, f32[1,4,1,192,384]{4,3,2,1,0:T(8,128)}, u32[]{:S(2)}) copy-start(f32[1,4,1,192,384]{4,3,2,1,0:T(8,128)} %param.5) | copy-start | bytes 3538948
  5.0 41.1 %collective-permute-start.9 = (f32[4,64,128]{2,1,0:T(8,128)S(1)}, f32[4,64,128]{2,1,0:T(8,128)S(1)}, u32[]{:S(2)}, u32[]{:S(2)}) collective-permute-start(f32[4,64,128]{2,1,0:T(8,128)S(1)} %get-tuple-element.34), channel_id=1, source_target_pairs={{272,0},{273,1},{274,2},{275,3},{276,4},{277,5},{278,6},{279,7},{2... | collective-permute-start | bytes 393224 | tf_op jit(solution)/shard_map/ppermute | solution.py:701
  12.0 34.1 %collective-permute-start.8 = (f32[4,64,128]{2,1,0:T(8,128)S(1)}, f32[4,64,128]{2,1,0:T(8,128)S(1)}, u32[]{:S(2)}, u32[]{:S(2)}) collective-permute-start(f32[4,64,128]{2,1,0:T(8,128)S(1)} %get-tuple-element.34), channel_id=1, source_target_pairs={{256,0},{257,1},{258,2},{259,3},{260,4},{261,5},{262,6},{263,7},{2... | collective-permute-start | bytes 393224 | tf_op jit(solution)/shard_map/ppermute | solution.py:701
  13.3 32.8 %collective-permute-start.7 = (f32[4,64,128]{2,1,0:T(8,128)S(1)}, f32[4,64,128]{2,1,0:T(8,128)S(1)}, u32[]{:S(2)}, u32[]{:S(2)}) collective-permute-start(f32[4,64,128]{2,1,0:T(8,128)S(1)} %get-tuple-element.34), channel_id=1, source_target_pairs={{256,16},{257,17},{258,18},{259,19},{260,20},{261,21},{262,22},{26... | collective-permute-start | bytes 393224 | tf_op jit(solution)/shard_map/ppermute | solution.py:701
  14.6 1.3 %collective-permute-start = (f32[3,4,384]{2,1,0:T(4,128)S(1)}, f32[3,4,384]{2,1,0:T(4,128)S(1)}, u32[]{:S(2)}, u32[]{:S(2)}) collective-permute-start(f32[3,4,384]{2,1,0:T(4,128)S(1)} %get-tuple-element.24), channel_id=1, source_target_pairs={{0,16},{1,17},{2,18},{3,19},{4,20},{5,21},{6,22},{7,23},{8,24},{9,... | collective-permute-start | bytes 55304 | tf_op jit(solution)/shard_map/ppermute | solution.py:701
  15.3 0.7 %collective-permute-start.1 = (f32[3,4,384]{2,1,0:T(4,128)S(1)}, f32[3,4,384]{2,1,0:T(4,128)S(1)}, u32[]{:S(2)}, u32[]{:S(2)}) collective-permute-start(f32[3,4,384]{2,1,0:T(4,128)S(1)} %get-tuple-element.25), channel_id=1, source_target_pairs={{16,0},{17,1},{18,2},{19,3},{20,4},{21,5},{22,6},{23,7},{24,8},{25... | collective-permute-start | bytes 55304 | tf_op jit(solution)/shard_map/ppermute | solution.py:701
  16.0 1.4 %collective-permute-start.2 = (f32[6,4,256]{2,1,0:T(4,128)S(1)}, f32[6,4,256]{2,1,0:T(4,128)S(1)}, u32[]{:S(2)}, u32[]{:S(2)}) collective-permute-start(f32[6,4,256]{2,1,0:T(4,128)S(1)} %get-tuple-element.27), channel_id=1, source_target_pairs={{0,1},{1,2},{2,3},{3,4},{4,5},{5,6},{6,7},{7,8},{8,9},{9,10},{10,1... | collective-permute-start | bytes 73736 | tf_op jit(solution)/shard_map/ppermute | solution.py:701
  16.7 0.7 %collective-permute-start.3 = (f32[6,4,256]{2,1,0:T(4,128)S(1)}, f32[6,4,256]{2,1,0:T(4,128)S(1)}, u32[]{:S(2)}, u32[]{:S(2)}) collective-permute-start(f32[6,4,256]{2,1,0:T(4,128)S(1)} %get-tuple-element.28), channel_id=1, source_target_pairs={{1,0},{2,1},{3,2},{4,3},{5,4},{6,5},{7,6},{8,7},{9,8},{10,9},{11,1... | collective-permute-start | bytes 73736 | tf_op jit(solution)/shard_map/ppermute | solution.py:701
  17.4 20.3 %collective-permute-start.4 = (f32[16,256]{1,0:T(8,128)S(1)}, f32[16,256]{1,0:T(8,128)S(1)}, u32[]{:S(2)}, u32[]{:S(2)}) collective-permute-start(f32[16,256]{1,0:T(8,128)S(1)} %get-tuple-element.31.sent_0), channel_id=1, source_target_pairs={{16,256},{17,257},{18,258},{19,259},{20,260},{21,261},{22,262},{23... | collective-permute-start | bytes 49160 | tf_op jit(solution)/shard_map/ppermute | solution.py:701
  18.7 20.3 %collective-permute-start.5 = (f32[16,256]{1,0:T(8,128)S(1)}, f32[16,256]{1,0:T(8,128)S(1)}, u32[]{:S(2)}, u32[]{:S(2)}) collective-permute-start(f32[16,256]{1,0:T(8,128)S(1)} %get-tuple-element.32.sent_1), channel_id=1, source_target_pairs={{0,256},{1,257},{2,258},{3,259},{4,260},{5,261},{6,262},{7,263},{8... | collective-permute-start | bytes 49160 | tf_op jit(solution)/shard_map/ppermute | solution.py:701
  37.7 8.4 %collective-permute-start.6 = (f32[16,256]{1,0:T(8,128)S(1)}, f32[16,256]{1,0:T(8,128)S(1)}, u32[]{:S(2)}, u32[]{:S(2)}) collective-permute-start(f32[16,256]{1,0:T(8,128)S(1)} %get-tuple-element.33.sent_2), channel_id=1, source_target_pairs={{0,272},{1,273},{2,274},{3,275},{4,276},{5,277},{6,278},{7,279},{8... | collective-permute-start | bytes 49160 | tf_op jit(solution)/shard_map/ppermute | solution.py:701

commit v4 on v3

--- a/solution.py
+++ b/solution.py
@@ -128,8 +128,13 @@
     return [lax.axis_index(axis) for axis in AXES]
 
 
+def by_parity(index, even, odd):
+    pl.when(lax.rem(index, 2) == 0)(even)
+    pl.when(lax.rem(index, 2) == 1)(odd)
+
+
 def edge_kernel(
-    x, drive, courant, diffusion, nest_patch, down, up, params,
+    x, drive, courant, diffusion, nest_patch, one, two, params,
     x_top, x_bottom, d_top, d_bottom, c_now, k_now, entries, sems,
 ):
     copies = [
@@ -150,13 +155,18 @@
         copy.start()
     for copy in copies:
         copy.wait()
-    for f in range(V):
-        down[0, f : f + 1] = x_bottom[f, 7:8, :]
-        down[1, f : f + 1] = x_bottom[f, 6:7, :]
-        down[2, f : f + 1] = d_bottom[f].astype(F32)[15:16]
-        up[0, f : f + 1] = x_top[f, 0:1, :]
-        up[1, f : f + 1] = x_top[f, 1:2, :]
-        up[2, f : f + 1] = d_top[f].astype(F32)[0:1]
+    _, row, column = position()
+
+    def fill(down, up):
+        for f in range(V):
+            down[0, f : f + 1] = x_bottom[f, 7:8, :]
+            down[1, f : f + 1] = x_bottom[f, 6:7, :]
+            down[2, f : f + 1] = d_bottom[f].astype(F32)[15:16]
+            up[0, f : f + 1] = x_top[f, 0:1, :]
+            up[1, f : f + 1] = x_top[f, 1:2, :]
+            up[2, f : f + 1] = d_top[f].astype(F32)[0:1]
+
+    by_parity(row, lambda: fill(one, two), lambda: fill(two, one))
 
     def put(at, value):
         params[at : at + 1, :] = jnp.full((1, WIDE), value, F32)
@@ -165,7 +175,6 @@
         put(f, k_now[f])
     put(COURANT, c_now[0])
     put(COURANT + 1, c_now[1])
-    _, row, column = position()
     count = nest_patch.shape[0]
     for member in range(3):
         slot = lax.rem(role_entry(entries, row, column, member, count), 9)
@@ -331,37 +340,57 @@
     )(*near(x, drive))
 
 
-def pack_kernel(ends, north, south, to_west, to_east):
-    for out, at, lo in ((to_west, 0, 0), (to_east, 3, W - 128)):
-        out[0:3] = ends[at : at + 3]
-        out[3, :, 0:128] = north[0, :, lo : lo + 128]
-        out[3, :, 128:256] = north[1, :, lo : lo + 128]
-        out[4, :, 0:128] = north[2, :, lo : lo + 128]
-        out[4, :, 128:256] = south[2, :, lo : lo + 128]
-        out[5, :, 0:128] = south[0, :, lo : lo + 128]
-        out[5, :, 128:256] = south[1, :, lo : lo + 128]
-
-
-def pack(ends, north, south):
-    shape = pltpu.VMEM((6, V, 256), F32)
+def pack_kernel(ends, from_one, from_two, one, two, north, south):
+    section, row, column = position()
+
+    def sort(up, down):
+        north[...] = up[...]
+        south[...] = down[...]
+
+    def fill(to_west, to_east):
+        for out, at, lo in ((to_west, 0, 0), (to_east, 3, W - 128)):
+            out[0:3] = ends[at : at + 3]
+            out[3, :, 0:128] = north[0, :, lo : lo + 128]
+            out[3, :, 128:256] = north[1, :, lo : lo + 128]
+            out[4, :, 0:128] = north[2, :, lo : lo + 128]
+            out[4, :, 128:256] = south[2, :, lo : lo + 128]
+            out[5, :, 0:128] = south[0, :, lo : lo + 128]
+            out[5, :, 128:256] = south[1, :, lo : lo + 128]
+
+    @pl.when(section == 0)
+    def _():
+        by_parity(row, lambda: sort(from_two, from_one), lambda: sort(from_one, from_two))
+        by_parity(column, lambda: fill(two, one), lambda: fill(one, two))
+
+
+def pack(ends, from_one, from_two):
+    flank, row = pltpu.VMEM((6, V, 256), F32), pltpu.VMEM((3, V, W), F32)
     return pl.pallas_call(
         pack_kernel,
         in_specs=[VMEM] * 3,
-        out_specs=[VMEM] * 2,
-        out_shape=[shape, shape],
+        out_specs=[VMEM] * 4,
+        out_shape=[flank, flank, row, row],
         compiler_params=SMALL,
         name="pack",
-    )(*near(ends, north, south))
+    )(*near(ends, from_one, from_two))
 
 
 def rims_kernel(
-    params, shape, rows, cols, ends, north, south, west, east, *out
+    params, shape, rows, cols, ends, north, south, from_one, from_two, *out
 ):
+    *out, beyond, west, east = out
     section, row, column = position()
     count, columns = shape
 
+    def sort(left, right):
+        west[...] = left[...]
+        east[...] = right[...]
+
     @pl.when(section == 0)
     def _():
+        by_parity(column, lambda: sort(from_two, from_one), lambda: sort(from_one, from_two))
+        beyond[0:V] = west[0]
+        beyond[V : 2 * V] = east[0]
         k = per_field(params, (V, 1), 0)
         a0, ae, aw, as_, an = weights_of(k, params)
         has_n = jnp.where(row > 0, 1.0, 0.0)
@@ -492,8 +521,9 @@
     return pl.pallas_call(
         kernel,
         in_specs=[VMEM] * 8,
-        out_specs=[VMEM] * 3,
-        out_shape=[pltpu.VMEM((4 * V, 256), F32)] * 3,
+        out_specs=[VMEM] * 4,
+        out_shape=[pltpu.VMEM((4 * V, 256), F32)] * 3 + [pltpu.VMEM((2 * V, 256), F32)],
+        scratch_shapes=[pltpu.VMEM((6, V, 256), F32)] * 2,
         compiler_params=SMALL,
         name="rims",
     )(*near(*arrays))
@@ -556,7 +586,7 @@
 
 
 def last_kernel(
-    nest_patch, params, x, drive, y, tent_row, tent_col, north, south, west, east,
+    nest_patch, params, x, drive, y, tent_row, tent_col, north, south, beyond,
     sent_0, sent_1, sent_2, got_0, got_1, got_2, mean_0, mean_1, mean_2, out, tile, entries, sems,
 ):
     section, row, column = position()
@@ -574,9 +604,8 @@
         fetch.start()
         _, ae, aw, _, _ = weights_of(per_field(params, (1, n), 1), params)
         eye = jnp.where(iota((H, H), 0) == iota((H, H), 1), 1.0, 0.0).astype(BF16)
-        beyond = jnp.concatenate([west[0, :, 0:H], east[0, :, 0:H]], axis=0)
         outer = jnp.where(iota((1, n), 1) < V, aw, ae)
-        both = spread(dot_nt(eye, beyond) * outer)
+        both = spread(dot_nt(eye, beyond[:, 0:H]) * outer)
         for f in range(V):
             coefs = closed(params[f : f + 1, 0:W], params)
             get = between(north[0, f : f + 1, :], x.at[f], south[0, f : f + 1, :])
@@ -659,7 +688,7 @@
 def last(nest_patch, *arrays):
     return pl.pallas_call(
         last_kernel,
-        in_specs=[ANY] + [VMEM] * 19,
+        in_specs=[ANY] + [VMEM] * 18,
         out_specs=ANY,
         out_shape=jax.ShapeDtypeStruct((V, H, W), F32),
         scratch_shapes=[
@@ -700,19 +729,25 @@
     def shift(value, source, move):
         return lax.ppermute(value, AXES, routes(sizes, source, move))
 
-    downward, upward, params = edge(x, drive, courant, diffusion, nest_patch)
-    north = shift(downward, 0, lambda r, c: (0, r + 1, c))
-    south = shift(upward, 0, lambda r, c: (0, r - 1, c))
+    def partner(index, first):
+        return index + 1 if index % 2 == first else index - 1
+
+    rows_one, rows_two, params = edge(x, drive, courant, diffusion, nest_patch)
+    rows_one = shift(rows_one, 0, lambda r, c: (0, partner(r, 0), c))
+    rows_two = shift(rows_two, 0, lambda r, c: (0, partner(r, 1), c))
     y, mean, ends, *tents = nests(params, x, drive)
     means = [shift(mean, 1, lambda r, c, m=m: (0, r + 1 - m, c)) for m in range(3)]
-    to_west, to_east = pack(ends, north, south)
-    west = shift(to_east, 0, lambda r, c: (0, r, c + 1))
-    east = shift(to_west, 0, lambda r, c: (0, r, c - 1))
+    cols_one, cols_two, north, south = pack(ends, rows_one, rows_two)
+    cols_one = shift(cols_one, 0, lambda r, c: (0, r, partner(c, 0)))
+    cols_two = shift(cols_two, 0, lambda r, c: (0, r, partner(c, 1)))
     rows, cols = banks(x, drive)
-    halos = north, south, west, east
-    sent = rims(sizes[1:], params, rows, cols, ends, *halos)
+    *sent, beyond = rims(
+        sizes[1:], params, rows, cols, ends, north, south, cols_one, cols_two
+    )
     got = [shift(sent[m], 0, lambda r, c, m=m: (1, r + m - 1, c)) for m in range(3)]
-    out = last(nest_patch, params, x, drive, y, *tents, *halos, *sent, *got, *means)
+    out = last(
+        nest_patch, params, x, drive, y, *tents, north, south, beyond, *sent, *got, *means
+    )
     return out.reshape(fields.shape)
 
 

time: 48.3 us -> 47.2 us (0.977)
  the two profiles are of different devices: /device:TPU:91 before, /device:TPU:34 now
where the time goes in v4:
time: 47.2 us; the launch traced here: 46.8 us
  starting transfers between devices  32.9 us (70%)
  Pallas kernels  7.02 us (15%)
  waiting for transfers between devices  6.39 us (14%)
    ppermute x10, starting transfers between devices, shift(): return lax.ppermute(value, AXES, routes(sizes, source, move))  32.9 us
    ppermute x10, waiting for transfers between devices, shift(): return lax.ppermute(value, AXES, routes(sizes, source, move))  6.39 us
    pallas_call x1, Pallas kernels, last(): pl.pallas_call(last_kernel, in_specs=[ANY] + [VMEM] * 18, out_specs=ANY,...  3.76 us
    pallas_call x1, Pallas kernels, edge(): pl.pallas_call(edge_kernel, in_specs=[ANY] * 5, out_specs=[VMEM] * 3, out...  1.16 us
  transfers between devices with their start and end apart: 10, of which 4 were waited for; matrix products, arithmetic and copies ran while one was open for 0% of the time, Pallas kernels for 3%

profile of v4, /device:TPU:34, one launch (start us, length us, event | category | flops | bytes accessed | tf_op | source)
XLA Modules:
  0.0 46.8 jit_solution(4521059525412972791)
XLA Ops:
  0.0 0.0 copy-start.1
  0.0 0.0 copy-start
  0.0 1.2 %edge.1 = (f32[3,4,384]{2,1,0:T(4,128)S(1)}, f32[3,4,384]{2,1,0:T(4,128)S(1)}, f32[16,640]{1,0:T(8,128)S(1)}) custom-call(f32[4,192,384]{2,1,0:T(8,128)} %bitcast.6, bf16[4,192,384]{2,1,0:T(8,128)(2,1)} %bitcast.10, f32[2]{0:T(128)} %bitcast.14, f32[4]{0:T(128)} %diffusion.1, s32[16,16]{1,0:T(8,128)} %nest_patch.3), custom_call_target="tpu_custom_call" | custom-call | tf_op jit(solution)/shard_map/edge/pallas_call | solution.py:187
  1.2 0.0 copy-done.1
  1.2 0.4 copy-done
  1.6 0.7 %nests.1 = (f32[4,192,384]{2,1,0:T(8,128)S(1)}, f32[4,64,128]{2,1,0:T(8,128)S(1)}, f32[6,4,256]{2,1,0:T(4,128)S(1)}, bf16[256,384]{1,0:T(8,128)(2,1)S(1)}, bf16[192,256]{1,0:T(8,128)(2,1)S(1)}) custom-call(f32[16,640]{1,0:T(8,128)S(1)} %get-tuple-element.23.params, f32[4,192,384]{2,1,0:T(8,128)S(1)} %bitcast.7, bf16[4,192,384]{2,1,0:T(8,128)(2,1)S(1)} %bitcast.11), custom_call_target="tpu_custom_call" | custom-call | tf_op jit(solution)/shard_map/nests/pallas_call | solution.py:291
  2.3 1.3 %collective-permute-start.9 = (f32[4,64,128]{2,1,0:T(8,128)S(1)}, f32[4,64,128]{2,1,0:T(8,128)S(1)}, u32[]{:S(2)}, u32[]{:S(2)}) collective-permute-start(f32[4,64,128]{2,1,0:T(8,128)S(1)} %get-tuple-element.40), channel_id=1, source_target_pairs={{272,0},{273,1},{274,2},{275,3},{276,4},{277,5},{278,6},{279,7},{2... | collective-permute-start | bytes 393224 | tf_op jit(solution)/shard_map/ppermute | solution.py:730
  3.6 1.3 %collective-permute-start.8 = (f32[4,64,128]{2,1,0:T(8,128)S(1)}, f32[4,64,128]{2,1,0:T(8,128)S(1)}, u32[]{:S(2)}, u32[]{:S(2)}) collective-permute-start(f32[4,64,128]{2,1,0:T(8,128)S(1)} %get-tuple-element.40), channel_id=1, source_target_pairs={{256,0},{257,1},{258,2},{259,3},{260,4},{261,5},{262,6},{263,7},{2... | collective-permute-start | bytes 393224 | tf_op jit(solution)/shard_map/ppermute | solution.py:730
  4.9 1.3 %collective-permute-start.7 = (f32[4,64,128]{2,1,0:T(8,128)S(1)}, f32[4,64,128]{2,1,0:T(8,128)S(1)}, u32[]{:S(2)}, u32[]{:S(2)}) collective-permute-start(f32[4,64,128]{2,1,0:T(8,128)S(1)} %get-tuple-element.40), channel_id=1, source_target_pairs={{256,16},{257,17},{258,18},{259,19},{260,20},{261,21},{262,22},{26... | collective-permute-start | bytes 393224 | tf_op jit(solution)/shard_map/ppermute | solution.py:730
  6.2 6.1 %collective-permute-start = (f32[3,4,384]{2,1,0:T(4,128)S(1)}, f32[3,4,384]{2,1,0:T(4,128)S(1)}, u32[]{:S(2)}, u32[]{:S(2)}) collective-permute-start(f32[3,4,384]{2,1,0:T(4,128)S(1)} %get-tuple-element.28), channel_id=1, source_target_pairs={{0,16},{1,17},{2,18},{3,19},{4,20},{5,21},{6,22},{7,23},{8,24},{9,... | collective-permute-start | bytes 55304 | tf_op jit(solution)/shard_map/ppermute | solution.py:730
  12.3 7.3 %collective-permute-start.1 = (f32[3,4,384]{2,1,0:T(4,128)S(1)}, f32[3,4,384]{2,1,0:T(4,128)S(1)}, u32[]{:S(2)}, u32[]{:S(2)}) collective-permute-start(f32[3,4,384]{2,1,0:T(4,128)S(1)} %get-tuple-element.29), channel_id=1, source_target_pairs={{16,32},{17,33},{18,34},{19,35},{20,36},{21,37},{22,38},{23,39},{2... | collective-permute-start | bytes 55304 | tf_op jit(solution)/shard_map/ppermute | solution.py:730
  19.5 0.0 collective-permute-done.from_one
  19.6 1.7 %collective-permute-done.1.from_two = f32[3,4,384]{2,1,0:T(4,128)S(1)} collective-permute-done((f32[3,4,384]{2,1,0:T(4,128)S(1)}, f32[3,4,384]{2,1,0:T(4,128)S(1)}, u32[]{:S(2)}, u32[]{:S(2)}) %collective-permute-start.1) | collective-permute-done | bytes 18464 | tf_op jit(solution)/shard_map/ppermute | solution.py:730
  21.3 1.9 %collective-permute-start.2 = (f32[6,4,256]{2,1,0:T(4,128)S(1)}, f32[6,4,256]{2,1,0:T(4,128)S(1)}, u32[]{:S(2)}, u32[]{:S(2)}) collective-permute-start(f32[6,4,256]{2,1,0:T(4,128)S(1)} %get-tuple-element.34), channel_id=1, source_target_pairs={{0,1},{1,0},{2,3},{3,2},{4,5},{5,4},{6,7},{7,6},{8,9},{9,8},{10,11... | collective-permute-start | bytes 73736 | tf_op jit(solution)/shard_map/ppermute | solution.py:730
  23.2 2.5 %collective-permute-start.3 = (f32[6,4,256]{2,1,0:T(4,128)S(1)}, f32[6,4,256]{2,1,0:T(4,128)S(1)}, u32[]{:S(2)}, u32[]{:S(2)}) collective-permute-start(f32[6,4,256]{2,1,0:T(4,128)S(1)} %get-tuple-element.35), channel_id=1, source_target_pairs={{1,2},{2,1},{3,4},{4,3},{5,6},{6,5},{7,8},{8,7},{9,10},{10,9},{11,... | collective-permute-start | bytes 73736 | tf_op jit(solution)/shard_map/ppermute | solution.py:730
  25.7 0.8 %banks.1 = (f32[14,4,384]{2,1,0:T(4,128)S(1)}, f32[12,4,256]{2,1,0:T(4,128)S(1)}) custom-call(f32[4,192,384]{2,1,0:T(8,128)S(1)} %bitcast.8, bf16[4,192,384]{2,1,0:T(8,128)(2,1)S(1)} %bitcast.12), custom_call_target="tpu_custom_call" | custom-call | tf_op jit(solution)/shard_map/banks/pallas_call | solution.py:333
  26.5 0.0 collective-permute-done.2.refs_5_
  26.5 3.1 %collective-permute-done.3.refs_6_ = f32[6,4,256]{2,1,0:T(4,128)S(1)} collective-permute-done((f32[6,4,256]{2,1,0:T(4,128)S(1)}, f32[6,4,256]{2,1,0:T(4,128)S(1)}, u32[]{:S(2)}, u32[]{:S(2)}) %collective-permute-start.3) | collective-permute-done | bytes 24608 | tf_op jit(solution)/shard_map/ppermute | solution.py:730
  29.6 0.6 %rims.1 = (f32[16,256]{1,0:T(8,128)S(1)}, f32[16,256]{1,0:T(8,128)S(1)}, f32[16,256]{1,0:T(8,128)S(1)}, f32[8,256]{1,0:T(8,128)S(1)}) custom-call(f32[16,640]{1,0:T(8,128)S(1)} %get-tuple-element.23.params, f32[14,4,384]{2,1,0:T(4,128)S(1)} %get-tuple-element.32.refs_0_, f32[12,4,256]{2,1,0:T(4,128)S(1)} %get-tuple-element.33.refs_1_, ...), custom_call_target="tpu_custom_call" | custom-call | tf_op jit(solution)/shard_map/rims/pallas_call | solution.py:521
  30.2 1.3 %collective-permute-start.4 = (f32[16,256]{1,0:T(8,128)S(1)}, f32[16,256]{1,0:T(8,128)S(1)}, u32[]{:S(2)}, u32[]{:S(2)}) collective-permute-start(f32[16,256]{1,0:T(8,128)S(1)} %get-tuple-element.37.sent_0), channel_id=1, source_target_pairs={{16,256},{17,257},{18,258},{19,259},{20,260},{21,261},{22,262},{23... | collective-permute-start | bytes 49160 | tf_op jit(solution)/shard_map/ppermute | solution.py:730
  31.5 1.3 %collective-permute-start.5 = (f32[16,256]{1,0:T(8,128)S(1)}, f32[16,256]{1,0:T(8,128)S(1)}, u32[]{:S(2)}, u32[]{:S(2)}) collective-permute-start(f32[16,256]{1,0:T(8,128)S(1)} %get-tuple-element.38.sent_1), channel_id=1, source_target_pairs={{0,256},{1,257},{2,258},{3,259},{4,260},{5,261},{6,262},{7,263},{8... | collective-permute-start | bytes 49160 | tf_op jit(solution)/shard_map/ppermute | solution.py:730
  32.8 0.1 collective-permute-done.4.got_0
  32.9 8.7 %collective-permute-start.6 = (f32[16,256]{1,0:T(8,128)S(1)}, f32[16,256]{1,0:T(8,128)S(1)}, u32[]{:S(2)}, u32[]{:S(2)}) collective-permute-start(f32[16,256]{1,0:T(8,128)S(1)} %get-tuple-element.39.sent_2), channel_id=1, source_target_pairs={{0,272},{1,273},{2,274},{3,275},{4,276},{5,277},{6,278},{7,279},{8... | collective-permute-start | bytes 49160 | tf_op jit(solution)/shard_map/ppermute | solution.py:730
  41.6 0.0 collective-permute-done.5.got_1
  41.6 1.4 %collective-permute-done.6.got_2 = f32[16,256]{1,0:T(8,128)S(1)} collective-permute-done((f32[16,256]{1,0:T(8,128)S(1)}, f32[16,256]{1,0:T(8,128)S(1)}, u32[]{:S(2)}, u32[]{:S(2)}) %collective-permute-start.6) | collective-permute-done | bytes 16416 | tf_op jit(solution)/shard_map/ppermute | solution.py:730
  43.1 0.0 collective-permute-done.9.mean_2
  43.1 0.0 collective-permute-done.8.mean_1
  43.1 0.0 collective-permute-done.7.mean_0
  43.1 3.8 %last.1 = f32[4,192,384]{2,1,0:T(8,128)} custom-call(s32[16,16]{1,0:T(8,128)} %nest_patch.3, f32[16,640]{1,0:T(8,128)S(1)} %get-tuple-element.23.params, f32[4,192,384]{2,1,0:T(8,128)S(1)} %bitcast.9, bf16[4,192,384]{2,1,0:T(8,128)(2,1)S(1)} %bitcast.13, f32[4,192,384]{2,1,0:T(8,128)S(1)} %get-tuple-element.24.y, ...), custom_call_target="tpu_custom_call" | custom-call | tf_op jit(solution)/shard_map/last/pallas_call | solution.py:689
  (1 shorter events, 0.0 us)
Async XLA Ops:
  0.0 1.2 %copy-start.1 = (bf16[1,4,1,192,384]{4,3,2,1,0:T(8,128)(2,1)S(1)}, bf16[1,4,1,192,384]{4,3,2,1,0:T(8,128)(2,1)}, u32[]{:S(2)}) copy-start(bf16[1,4,1,192,384]{4,3,2,1,0:T(8,128)(2,1)} %param.6) | copy-start | bytes 1769476
  0.0 1.5 %copy-start = (f32[1,4,1,192,384]{4,3,2,1,0:T(8,128)S(1)}, f32[1,4,1,192,384]{4,3,2,1,0:T(8,128)}, u32[]{:S(2)}) copy-start(f32[1,4,1,192,384]{4,3,2,1,0:T(8,128)} %param.5) | copy-start | bytes 3538948
  2.3 40.8 %collective-permute-start.9 = (f32[4,64,128]{2,1,0:T(8,128)S(1)}, f32[4,64,128]{2,1,0:T(8,128)S(1)}, u32[]{:S(2)}, u32[]{:S(2)}) collective-permute-start(f32[4,64,128]{2,1,0:T(8,128)S(1)} %get-tuple-element.40), channel_id=1, source_target_pairs={{272,0},{273,1},{274,2},{275,3},{276,4},{277,5},{278,6},{279,7},{2... | collective-permute-start | bytes 393224 | tf_op jit(solution)/shard_map/ppermute | solution.py:730
  3.6 39.5 %collective-permute-start.8 = (f32[4,64,128]{2,1,0:T(8,128)S(1)}, f32[4,64,128]{2,1,0:T(8,128)S(1)}, u32[]{:S(2)}, u32[]{:S(2)}) collective-permute-start(f32[4,64,128]{2,1,0:T(8,128)S(1)} %get-tuple-element.40), channel_id=1, source_target_pairs={{256,0},{257,1},{258,2},{259,3},{260,4},{261,5},{262,6},{263,7},{2... | collective-permute-start | bytes 393224 | tf_op jit(solution)/shard_map/ppermute | solution.py:730
  4.9 38.2 %collective-permute-start.7 = (f32[4,64,128]{2,1,0:T(8,128)S(1)}, f32[4,64,128]{2,1,0:T(8,128)S(1)}, u32[]{:S(2)}, u32[]{:S(2)}) collective-permute-start(f32[4,64,128]{2,1,0:T(8,128)S(1)} %get-tuple-element.40), channel_id=1, source_target_pairs={{256,16},{257,17},{258,18},{259,19},{260,20},{261,21},{262,22},{26... | collective-permute-start | bytes 393224 | tf_op jit(solution)/shard_map/ppermute | solution.py:730
  6.2 13.4 %collective-permute-start = (f32[3,4,384]{2,1,0:T(4,128)S(1)}, f32[3,4,384]{2,1,0:T(4,128)S(1)}, u32[]{:S(2)}, u32[]{:S(2)}) collective-permute-start(f32[3,4,384]{2,1,0:T(4,128)S(1)} %get-tuple-element.28), channel_id=1, source_target_pairs={{0,16},{1,17},{2,18},{3,19},{4,20},{5,21},{6,22},{7,23},{8,24},{9,... | collective-permute-start | bytes 55304 | tf_op jit(solution)/shard_map/ppermute | solution.py:730
  12.3 9.0 %collective-permute-start.1 = (f32[3,4,384]{2,1,0:T(4,128)S(1)}, f32[3,4,384]{2,1,0:T(4,128)S(1)}, u32[]{:S(2)}, u32[]{:S(2)}) collective-permute-start(f32[3,4,384]{2,1,0:T(4,128)S(1)} %get-tuple-element.29), channel_id=1, source_target_pairs={{16,32},{17,33},{18,34},{19,35},{20,36},{21,37},{22,38},{23,39},{2... | collective-permute-start | bytes 55304 | tf_op jit(solution)/shard_map/ppermute | solution.py:730
  21.3 5.2 %collective-permute-start.2 = (f32[6,4,256]{2,1,0:T(4,128)S(1)}, f32[6,4,256]{2,1,0:T(4,128)S(1)}, u32[]{:S(2)}, u32[]{:S(2)}) collective-permute-start(f32[6,4,256]{2,1,0:T(4,128)S(1)} %get-tuple-element.34), channel_id=1, source_target_pairs={{0,1},{1,0},{2,3},{3,2},{4,5},{5,4},{6,7},{7,6},{8,9},{9,8},{10,11... | collective-permute-start | bytes 73736 | tf_op jit(solution)/shard_map/ppermute | solution.py:730
  23.2 6.4 %collective-permute-start.3 = (f32[6,4,256]{2,1,0:T(4,128)S(1)}, f32[6,4,256]{2,1,0:T(4,128)S(1)}, u32[]{:S(2)}, u32[]{:S(2)}) collective-permute-start(f32[6,4,256]{2,1,0:T(4,128)S(1)} %get-tuple-element.35), channel_id=1, source_target_pairs={{1,2},{2,1},{3,4},{4,3},{5,6},{6,5},{7,8},{8,7},{9,10},{10,9},{11,... | collective-permute-start | bytes 73736 | tf_op jit(solution)/shard_map/ppermute | solution.py:730
  30.2 2.7 %collective-permute-start.4 = (f32[16,256]{1,0:T(8,128)S(1)}, f32[16,256]{1,0:T(8,128)S(1)}, u32[]{:S(2)}, u32[]{:S(2)}) collective-permute-start(f32[16,256]{1,0:T(8,128)S(1)} %get-tuple-element.37.sent_0), channel_id=1, source_target_pairs={{16,256},{17,257},{18,258},{19,259},{20,260},{21,261},{22,262},{23... | collective-permute-start | bytes 49160 | tf_op jit(solution)/shard_map/ppermute | solution.py:730
  31.5 10.1 %collective-permute-start.5 = (f32[16,256]{1,0:T(8,128)S(1)}, f32[16,256]{1,0:T(8,128)S(1)}, u32[]{:S(2)}, u32[]{:S(2)}) collective-permute-start(f32[16,256]{1,0:T(8,128)S(1)} %get-tuple-element.38.sent_1), channel_id=1, source_target_pairs={{0,256},{1,257},{2,258},{3,259},{4,260},{5,261},{6,262},{7,263},{8... | collective-permute-start | bytes 49160 | tf_op jit(solution)/shard_map/ppermute | solution.py:730
  32.9 10.1 %collective-permute-start.6 = (f32[16,256]{1,0:T(8,128)S(1)}, f32[16,256]{1,0:T(8,128)S(1)}, u32[]{:S(2)}, u32[]{:S(2)}) collective-permute-start(f32[16,256]{1,0:T(8,128)S(1)} %get-tuple-element.39.sent_2), channel_id=1, source_target_pairs={{0,272},{1,273},{2,274},{3,275},{4,276},{5,277},{6,278},{7,279},{8... | collective-permute-start | bytes 49160 | tf_op jit(solution)/shard_map/ppermute | solution.py:730

commit v5 on v4

--- a/solution.py
+++ b/solution.py
@@ -310,7 +310,7 @@
     )(*near(params, x, drive))
 
 
-def bank_kernel(x, drive, rows, cols):
+def bank_kernel(params, x, drive, north, south, rows, cols, y):
     @pl.when(position()[0] == 0)
     def _():
         cols[...] = jnp.zeros(cols.shape, F32)
@@ -327,17 +327,26 @@
                 cols[i, f : f + 1, 0:H] = from_x[i : i + 1]
             for i in range(4):
                 cols[8 + i, f : f + 1, 0:H] = from_drive[i : i + 1]
-
-
-def banks(x, drive):
+            coefs = closed(params[f : f + 1, 0:W], params)
+            get = between(north[0, f : f + 1, :], x.at[f], south[0, f : f + 1, :])
+            for r in range(0, H, CHUNK):
+                end = r + CHUNK
+                y[f, r:end, :] = step_rows(get, r, coefs, drive[f, r:end, :].astype(F32))
+
+
+def banks(params, x, drive, north, south):
     return pl.pallas_call(
         bank_kernel,
-        in_specs=[VMEM] * 2,
-        out_specs=[VMEM] * 2,
-        out_shape=[pltpu.VMEM((14, V, W), F32), pltpu.VMEM((12, V, 256), F32)],
+        in_specs=[VMEM] * 5,
+        out_specs=[VMEM] * 3,
+        out_shape=[
+            pltpu.VMEM((14, V, W), F32),
+            pltpu.VMEM((12, V, 256), F32),
+            pltpu.VMEM((V, H, W), F32),
+        ],
         compiler_params=SMALL,
         name="banks",
-    )(*near(x, drive))
+    )(*near(params, x, drive, north, south))
 
 
 def pack_kernel(ends, from_one, from_two, one, two, north, south):
@@ -586,7 +595,7 @@
 
 
 def last_kernel(
-    nest_patch, params, x, drive, y, tent_row, tent_col, north, south, beyond,
+    nest_patch, params, stepped, y, tent_row, tent_col, beyond,
     sent_0, sent_1, sent_2, got_0, got_1, got_2, mean_0, mean_1, mean_2, out, tile, entries, sems,
 ):
     section, row, column = position()
@@ -597,6 +606,12 @@
 
     def send(f):
         return pltpu.make_async_copy(tile.at[f], out.at[f], sems.at[f])
+
+    def with_sides(base, f, both):
+        left, right = f * 128, (V + f) * 128
+        tile[f, :, 0:128] = base[f, :, 0:128] + both[:, left : left + 128]
+        tile[f, :, 128 : W - 128] = base[f, :, 128 : W - 128]
+        tile[f, :, W - 128 : W] = base[f, :, W - 128 : W] + both[:, right : right + 128]
 
     @pl.when(parent)
     def _():
@@ -607,17 +622,7 @@
         outer = jnp.where(iota((1, n), 1) < V, aw, ae)
         both = spread(dot_nt(eye, beyond[:, 0:H]) * outer)
         for f in range(V):
-            coefs = closed(params[f : f + 1, 0:W], params)
-            get = between(north[0, f : f + 1, :], x.at[f], south[0, f : f + 1, :])
-            left, right = f * 128, (V + f) * 128
-            for r in range(0, H, CHUNK):
-                end = r + CHUNK
-                value = step_rows(get, r, coefs, drive[f, r:end, :].astype(F32))
-                tile[f, r:end, 0:128] = value[:, 0:128] + both[r:end, left : left + 128]
-                tile[f, r:end, 128 : W - 128] = value[:, 128 : W - 128]
-                tile[f, r:end, W - 128 : W] = (
-                    value[:, W - 128 : W] + both[r:end, right : right + 128]
-                )
+            with_sides(stepped, f, both)
         old = jnp.concatenate([s[0:n, :] for s in sent], axis=0)
         new = jnp.concatenate([s[n : 2 * n, :] for s in sent], axis=0)
         row_effect, col_effect = edge_effect(old, new, params, row_tent(), col_tent())
@@ -667,10 +672,7 @@
             )
         )
         for f in range(V):
-            left, right = f * 128, (V + f) * 128
-            tile[f, :, 0:128] = y[f, :, 0:128] + both[:, left : left + 128]
-            tile[f, :, 128 : W - 128] = y[f, :, 128 : W - 128]
-            tile[f, :, W - 128 : W] = y[f, :, W - 128 : W] + both[:, right : right + 128]
+            with_sides(y, f, both)
             for depth in range(3):
                 bottom = H - 1 - depth
                 tile[f, depth : depth + 1, :] = (
@@ -688,7 +690,7 @@
 def last(nest_patch, *arrays):
     return pl.pallas_call(
         last_kernel,
-        in_specs=[ANY] + [VMEM] * 18,
+        in_specs=[ANY] + [VMEM] * 15,
         out_specs=ANY,
         out_shape=jax.ShapeDtypeStruct((V, H, W), F32),
         scratch_shapes=[
@@ -740,13 +742,13 @@
     cols_one, cols_two, north, south = pack(ends, rows_one, rows_two)
     cols_one = shift(cols_one, 0, lambda r, c: (0, r, partner(c, 0)))
     cols_two = shift(cols_two, 0, lambda r, c: (0, r, partner(c, 1)))
-    rows, cols = banks(x, drive)
+    rows, cols, stepped = banks(params, x, drive, north, south)
     *sent, beyond = rims(
         sizes[1:], params, rows, cols, ends, north, south, cols_one, cols_two
     )
     got = [shift(sent[m], 0, lambda r, c, m=m: (1, r + m - 1, c)) for m in range(3)]
     out = last(
-        nest_patch, params, x, drive, y, *tents, north, south, beyond, *sent, *got, *means
+        nest_patch, params, stepped, y, *tents, beyond, *sent, *got, *means
     )
     return out.reshape(fields.shape)
 

time: 47.2 us -> 46.4 us (0.983)
  transfers between devices with their start and end apart: 10 -> 10, of which waited for: 4 -> 4; matrix products, arithmetic and copies ran while one was open for 0% -> 0% of each run, Pallas kernels for 3% -> 4%
where the time goes in v5:
time: 46.4 us; the launch traced here: 46 us
  starting transfers between devices  32.9 us (71%)
  Pallas kernels  6.56 us (14%)
  waiting for transfers between devices  6.06 us (13%)
    ppermute x10, starting transfers between devices, shift(): return lax.ppermute(value, AXES, routes(sizes, source, move))  32.9 us
    ppermute x10, waiting for transfers between devices, shift(): return lax.ppermute(value, AXES, routes(sizes, source, move))  6.06 us
    pallas_call x1, Pallas kernels, last(): pl.pallas_call(last_kernel, in_specs=[ANY] + [VMEM] * 15, out_specs=ANY,...  2.97 us
    pallas_call x1, Pallas kernels, edge(): pl.pallas_call(edge_kernel, in_specs=[ANY] * 5, out_specs=[VMEM] * 3, out...  1.16 us
    pallas_call x1, Pallas kernels, banks(): pl.pallas_call(bank_kernel, in_specs=[VMEM] * 5, out_specs=[VMEM] * 3, ou...  1.09 us
  transfers between devices with their start and end apart: 10, of which 4 were waited for; matrix products, arithmetic and copies ran while one was open for 0% of the time, Pallas kernels for 4%

profile of v5, /device:TPU:34, one launch (start us, length us, event | category | flops | bytes accessed | tf_op | source)
XLA Modules:
  0.0 46.0 jit_solution(5764411857705559286)
XLA Ops:
  0.0 0.0 copy-start.1
  0.0 0.0 copy-start
  0.0 1.2 %edge.1 = (f32[3,4,384]{2,1,0:T(4,128)S(1)}, f32[3,4,384]{2,1,0:T(4,128)S(1)}, f32[16,640]{1,0:T(8,128)S(1)}) custom-call(f32[4,192,384]{2,1,0:T(8,128)} %bitcast.6, bf16[4,192,384]{2,1,0:T(8,128)(2,1)} %bitcast.9, f32[2]{0:T(128)} %bitcast.12, f32[4]{0:T(128)} %diffusion.1, s32[16,16]{1,0:T(8,128)} %nest_patch.3), custom_call_target="tpu_custom_call" | custom-call | tf_op jit(solution)/shard_map/edge/pallas_call | solution.py:187
  1.2 0.0 copy-done.1
  1.2 0.4 copy-done
  1.6 0.7 %nests.1 = (f32[4,192,384]{2,1,0:T(8,128)S(1)}, f32[4,64,128]{2,1,0:T(8,128)S(1)}, f32[6,4,256]{2,1,0:T(4,128)S(1)}, bf16[256,384]{1,0:T(8,128)(2,1)S(1)}, bf16[192,256]{1,0:T(8,128)(2,1)S(1)}) custom-call(f32[16,640]{1,0:T(8,128)S(1)} %get-tuple-element.24.params, f32[4,192,384]{2,1,0:T(8,128)S(1)} %bitcast.7, bf16[4,192,384]{2,1,0:T(8,128)(2,1)S(1)} %bitcast.10), custom_call_target="tpu_custom_call" | custom-call | tf_op jit(solution)/shard_map/nests/pallas_call | solution.py:291
  2.3 1.3 %collective-permute-start.9 = (f32[4,64,128]{2,1,0:T(8,128)S(1)}, f32[4,64,128]{2,1,0:T(8,128)S(1)}, u32[]{:S(2)}, u32[]{:S(2)}) collective-permute-start(f32[4,64,128]{2,1,0:T(8,128)S(1)} %get-tuple-element.42), channel_id=1, source_target_pairs={{272,0},{273,1},{274,2},{275,3},{276,4},{277,5},{278,6},{279,7},{2... | collective-permute-start | bytes 393224 | tf_op jit(solution)/shard_map/ppermute | solution.py:732
  3.6 1.3 %collective-permute-start.8 = (f32[4,64,128]{2,1,0:T(8,128)S(1)}, f32[4,64,128]{2,1,0:T(8,128)S(1)}, u32[]{:S(2)}, u32[]{:S(2)}) collective-permute-start(f32[4,64,128]{2,1,0:T(8,128)S(1)} %get-tuple-element.42), channel_id=1, source_target_pairs={{256,0},{257,1},{258,2},{259,3},{260,4},{261,5},{262,6},{263,7},{2... | collective-permute-start | bytes 393224 | tf_op jit(solution)/shard_map/ppermute | solution.py:732
  4.9 1.3 %collective-permute-start.7 = (f32[4,64,128]{2,1,0:T(8,128)S(1)}, f32[4,64,128]{2,1,0:T(8,128)S(1)}, u32[]{:S(2)}, u32[]{:S(2)}) collective-permute-start(f32[4,64,128]{2,1,0:T(8,128)S(1)} %get-tuple-element.42), channel_id=1, source_target_pairs={{256,16},{257,17},{258,18},{259,19},{260,20},{261,21},{262,22},{26... | collective-permute-start | bytes 393224 | tf_op jit(solution)/shard_map/ppermute | solution.py:732
  6.2 6.1 %collective-permute-start = (f32[3,4,384]{2,1,0:T(4,128)S(1)}, f32[3,4,384]{2,1,0:T(4,128)S(1)}, u32[]{:S(2)}, u32[]{:S(2)}) collective-permute-start(f32[3,4,384]{2,1,0:T(4,128)S(1)} %get-tuple-element.26), channel_id=1, source_target_pairs={{0,16},{1,17},{2,18},{3,19},{4,20},{5,21},{6,22},{7,23},{8,24},{9,... | collective-permute-start | bytes 55304 | tf_op jit(solution)/shard_map/ppermute | solution.py:732
  12.3 7.3 %collective-permute-start.1 = (f32[3,4,384]{2,1,0:T(4,128)S(1)}, f32[3,4,384]{2,1,0:T(4,128)S(1)}, u32[]{:S(2)}, u32[]{:S(2)}) collective-permute-start(f32[3,4,384]{2,1,0:T(4,128)S(1)} %get-tuple-element.27), channel_id=1, source_target_pairs={{16,32},{17,33},{18,34},{19,35},{20,36},{21,37},{22,38},{23,39},{2... | collective-permute-start | bytes 55304 | tf_op jit(solution)/shard_map/ppermute | solution.py:732
  19.5 0.0 collective-permute-done.from_one
  19.6 1.7 %collective-permute-done.1.from_two = f32[3,4,384]{2,1,0:T(4,128)S(1)} collective-permute-done((f32[3,4,384]{2,1,0:T(4,128)S(1)}, f32[3,4,384]{2,1,0:T(4,128)S(1)}, u32[]{:S(2)}, u32[]{:S(2)}) %collective-permute-start.1) | collective-permute-done | bytes 18464 | tf_op jit(solution)/shard_map/ppermute | solution.py:732
  21.3 1.9 %collective-permute-start.2 = (f32[6,4,256]{2,1,0:T(4,128)S(1)}, f32[6,4,256]{2,1,0:T(4,128)S(1)}, u32[]{:S(2)}, u32[]{:S(2)}) collective-permute-start(f32[6,4,256]{2,1,0:T(4,128)S(1)} %get-tuple-element.36), channel_id=1, source_target_pairs={{0,1},{1,0},{2,3},{3,2},{4,5},{5,4},{6,7},{7,6},{8,9},{9,8},{10,11... | collective-permute-start | bytes 73736 | tf_op jit(solution)/shard_map/ppermute | solution.py:732
  23.2 2.5 %collective-permute-start.3 = (f32[6,4,256]{2,1,0:T(4,128)S(1)}, f32[6,4,256]{2,1,0:T(4,128)S(1)}, u32[]{:S(2)}, u32[]{:S(2)}) collective-permute-start(f32[6,4,256]{2,1,0:T(4,128)S(1)} %get-tuple-element.37), channel_id=1, source_target_pairs={{1,2},{2,1},{3,4},{4,3},{5,6},{6,5},{7,8},{8,7},{9,10},{10,9},{11,... | collective-permute-start | bytes 73736 | tf_op jit(solution)/shard_map/ppermute | solution.py:732
  25.7 1.1 %banks.1 = (f32[14,4,384]{2,1,0:T(4,128)S(1)}, f32[12,4,256]{2,1,0:T(4,128)S(1)}, f32[4,192,384]{2,1,0:T(8,128)S(1)}) custom-call(f32[16,640]{1,0:T(8,128)S(1)} %get-tuple-element.24.params, f32[4,192,384]{2,1,0:T(8,128)S(1)} %bitcast.8, bf16[4,192,384]{2,1,0:T(8,128)(2,1)S(1)} %bitcast.11, f32[3,4,384]{2,1,0:T(4,128)S(1)} %get-tuple-element.28.north.refs_3_, ...), custom_call_target="tpu_custom_call" | custom-call | tf_op jit(solution)/shard_map/banks/pallas_call | solution.py:338
  26.8 0.0 collective-permute-done.2.refs_5_
  26.8 2.8 %collective-permute-done.3.refs_6_ = f32[6,4,256]{2,1,0:T(4,128)S(1)} collective-permute-done((f32[6,4,256]{2,1,0:T(4,128)S(1)}, f32[6,4,256]{2,1,0:T(4,128)S(1)}, u32[]{:S(2)}, u32[]{:S(2)}) %collective-permute-start.3) | collective-permute-done | bytes 24608 | tf_op jit(solution)/shard_map/ppermute | solution.py:732
  29.6 0.6 %rims.1 = (f32[16,256]{1,0:T(8,128)S(1)}, f32[16,256]{1,0:T(8,128)S(1)}, f32[16,256]{1,0:T(8,128)S(1)}, f32[8,256]{1,0:T(8,128)S(1)}) custom-call(f32[16,640]{1,0:T(8,128)S(1)} %get-tuple-element.24.params, f32[14,4,384]{2,1,0:T(4,128)S(1)} %get-tuple-element.34.refs_0_, f32[12,4,256]{2,1,0:T(4,128)S(1)} %get-tuple-element.35.refs_1_, ...), custom_call_target="tpu_custom_call" | custom-call | tf_op jit(solution)/shard_map/rims/pallas_call | solution.py:530
  30.2 1.3 %collective-permute-start.4 = (f32[16,256]{1,0:T(8,128)S(1)}, f32[16,256]{1,0:T(8,128)S(1)}, u32[]{:S(2)}, u32[]{:S(2)}) collective-permute-start(f32[16,256]{1,0:T(8,128)S(1)} %get-tuple-element.39.sent_0), channel_id=1, source_target_pairs={{16,256},{17,257},{18,258},{19,259},{20,260},{21,261},{22,262},{23... | collective-permute-start | bytes 49160 | tf_op jit(solution)/shard_map/ppermute | solution.py:732
  31.5 1.3 %collective-permute-start.5 = (f32[16,256]{1,0:T(8,128)S(1)}, f32[16,256]{1,0:T(8,128)S(1)}, u32[]{:S(2)}, u32[]{:S(2)}) collective-permute-start(f32[16,256]{1,0:T(8,128)S(1)} %get-tuple-element.40.sent_1), channel_id=1, source_target_pairs={{0,256},{1,257},{2,258},{3,259},{4,260},{5,261},{6,262},{7,263},{8... | collective-permute-start | bytes 49160 | tf_op jit(solution)/shard_map/ppermute | solution.py:732
  32.8 0.1 collective-permute-done.4.got_0
  32.9 8.7 %collective-permute-start.6 = (f32[16,256]{1,0:T(8,128)S(1)}, f32[16,256]{1,0:T(8,128)S(1)}, u32[]{:S(2)}, u32[]{:S(2)}) collective-permute-start(f32[16,256]{1,0:T(8,128)S(1)} %get-tuple-element.41.sent_2), channel_id=1, source_target_pairs={{0,272},{1,273},{2,274},{3,275},{4,276},{5,277},{6,278},{7,279},{8... | collective-permute-start | bytes 49160 | tf_op jit(solution)/shard_map/ppermute | solution.py:732
  41.6 0.0 collective-permute-done.5.got_1
  41.6 1.4 %collective-permute-done.6.got_2 = f32[16,256]{1,0:T(8,128)S(1)} collective-permute-done((f32[16,256]{1,0:T(8,128)S(1)}, f32[16,256]{1,0:T(8,128)S(1)}, u32[]{:S(2)}, u32[]{:S(2)}) %collective-permute-start.6) | collective-permute-done | bytes 16416 | tf_op jit(solution)/shard_map/ppermute | solution.py:732
  43.1 0.0 collective-permute-done.9.mean_2
  43.1 0.0 collective-permute-done.8.mean_1
  43.1 0.0 collective-permute-done.7.mean_0
  43.1 3.0 %last.1 = f32[4,192,384]{2,1,0:T(8,128)} custom-call(s32[16,16]{1,0:T(8,128)} %nest_patch.3, f32[16,640]{1,0:T(8,128)S(1)} %get-tuple-element.24.params, f32[4,192,384]{2,1,0:T(8,128)S(1)} %get-tuple-element.30.stepped, f32[4,192,384]{2,1,0:T(8,128)S(1)} %get-tuple-element.31.y, bf16[256,384]{1,0:T(8,128)(2,1)S(1)} %get-tuple-element.32.tent_row, ...), custom_call_target="tpu_custom_call" | custom-call | tf_op jit(solution)/shard_map/last/pallas_call | solution.py:691
  (1 shorter events, 0.0 us)
Async XLA Ops:
  0.0 1.2 %copy-start.1 = (bf16[1,4,1,192,384]{4,3,2,1,0:T(8,128)(2,1)S(1)}, bf16[1,4,1,192,384]{4,3,2,1,0:T(8,128)(2,1)}, u32[]{:S(2)}) copy-start(bf16[1,4,1,192,384]{4,3,2,1,0:T(8,128)(2,1)} %param.6) | copy-start | bytes 1769476
  0.0 1.5 %copy-start = (f32[1,4,1,192,384]{4,3,2,1,0:T(8,128)S(1)}, f32[1,4,1,192,384]{4,3,2,1,0:T(8,128)}, u32[]{:S(2)}) copy-start(f32[1,4,1,192,384]{4,3,2,1,0:T(8,128)} %param.5) | copy-start | bytes 3538948
  2.3 40.8 %collective-permute-start.9 = (f32[4,64,128]{2,1,0:T(8,128)S(1)}, f32[4,64,128]{2,1,0:T(8,128)S(1)}, u32[]{:S(2)}, u32[]{:S(2)}) collective-permute-start(f32[4,64,128]{2,1,0:T(8,128)S(1)} %get-tuple-element.42), channel_id=1, source_target_pairs={{272,0},{273,1},{274,2},{275,3},{276,4},{277,5},{278,6},{279,7},{2... | collective-permute-start | bytes 393224 | tf_op jit(solution)/shard_map/ppermute | solution.py:732
  3.6 39.5 %collective-permute-start.8 = (f32[4,64,128]{2,1,0:T(8,128)S(1)}, f32[4,64,128]{2,1,0:T(8,128)S(1)}, u32[]{:S(2)}, u32[]{:S(2)}) collective-permute-start(f32[4,64,128]{2,1,0:T(8,128)S(1)} %get-tuple-element.42), channel_id=1, source_target_pairs={{256,0},{257,1},{258,2},{259,3},{260,4},{261,5},{262,6},{263,7},{2... | collective-permute-start | bytes 393224 | tf_op jit(solution)/shard_map/ppermute | solution.py:732
  4.9 38.2 %collective-permute-start.7 = (f32[4,64,128]{2,1,0:T(8,128)S(1)}, f32[4,64,128]{2,1,0:T(8,128)S(1)}, u32[]{:S(2)}, u32[]{:S(2)}) collective-permute-start(f32[4,64,128]{2,1,0:T(8,128)S(1)} %get-tuple-element.42), channel_id=1, source_target_pairs={{256,16},{257,17},{258,18},{259,19},{260,20},{261,21},{262,22},{26... | collective-permute-start | bytes 393224 | tf_op jit(solution)/shard_map/ppermute | solution.py:732
  6.2 13.4 %collective-permute-start = (f32[3,4,384]{2,1,0:T(4,128)S(1)}, f32[3,4,384]{2,1,0:T(4,128)S(1)}, u32[]{:S(2)}, u32[]{:S(2)}) collective-permute-start(f32[3,4,384]{2,1,0:T(4,128)S(1)} %get-tuple-element.26), channel_id=1, source_target_pairs={{0,16},{1,17},{2,18},{3,19},{4,20},{5,21},{6,22},{7,23},{8,24},{9,... | collective-permute-start | bytes 55304 | tf_op jit(solution)/shard_map/ppermute | solution.py:732
  12.3 9.0 %collective-permute-start.1 = (f32[3,4,384]{2,1,0:T(4,128)S(1)}, f32[3,4,384]{2,1,0:T(4,128)S(1)}, u32[]{:S(2)}, u32[]{:S(2)}) collective-permute-start(f32[3,4,384]{2,1,0:T(4,128)S(1)} %get-tuple-element.27), channel_id=1, source_target_pairs={{16,32},{17,33},{18,34},{19,35},{20,36},{21,37},{22,38},{23,39},{2... | collective-permute-start | bytes 55304 | tf_op jit(solution)/shard_map/ppermute | solution.py:732
  21.3 5.5 %collective-permute-start.2 = (f32[6,4,256]{2,1,0:T(4,128)S(1)}, f32[6,4,256]{2,1,0:T(4,128)S(1)}, u32[]{:S(2)}, u32[]{:S(2)}) collective-permute-start(f32[6,4,256]{2,1,0:T(4,128)S(1)} %get-tuple-element.36), channel_id=1, source_target_pairs={{0,1},{1,0},{2,3},{3,2},{4,5},{5,4},{6,7},{7,6},{8,9},{9,8},{10,11... | collective-permute-start | bytes 73736 | tf_op jit(solution)/shard_map/ppermute | solution.py:732
  23.2 6.4 %collective-permute-start.3 = (f32[6,4,256]{2,1,0:T(4,128)S(1)}, f32[6,4,256]{2,1,0:T(4,128)S(1)}, u32[]{:S(2)}, u32[]{:S(2)}) collective-permute-start(f32[6,4,256]{2,1,0:T(4,128)S(1)} %get-tuple-element.37), channel_id=1, source_target_pairs={{1,2},{2,1},{3,4},{4,3},{5,6},{6,5},{7,8},{8,7},{9,10},{10,9},{11,... | collective-permute-start | bytes 73736 | tf_op jit(solution)/shard_map/ppermute | solution.py:732
  30.2 2.7 %collective-permute-start.4 = (f32[16,256]{1,0:T(8,128)S(1)}, f32[16,256]{1,0:T(8,128)S(1)}, u32[]{:S(2)}, u32[]{:S(2)}) collective-permute-start(f32[16,256]{1,0:T(8,128)S(1)} %get-tuple-element.39.sent_0), channel_id=1, source_target_pairs={{16,256},{17,257},{18,258},{19,259},{20,260},{21,261},{22,262},{23... | collective-permute-start | bytes 49160 | tf_op jit(solution)/shard_map/ppermute | solution.py:732
  31.5 10.1 %collective-permute-start.5 = (f32[16,256]{1,0:T(8,128)S(1)}, f32[16,256]{1,0:T(8,128)S(1)}, u32[]{:S(2)}, u32[]{:S(2)}) collective-permute-start(f32[16,256]{1,0:T(8,128)S(1)} %get-tuple-element.40.sent_1), channel_id=1, source_target_pairs={{0,256},{1,257},{2,258},{3,259},{4,260},{5,261},{6,262},{7,263},{8... | collective-permute-start | bytes 49160 | tf_op jit(solution)/shard_map/ppermute | solution.py:732
  32.9 10.1 %collective-permute-start.6 = (f32[16,256]{1,0:T(8,128)S(1)}, f32[16,256]{1,0:T(8,128)S(1)}, u32[]{:S(2)}, u32[]{:S(2)}) collective-permute-start(f32[16,256]{1,0:T(8,128)S(1)} %get-tuple-element.41.sent_2), channel_id=1, source_target_pairs={{0,272},{1,273},{2,274},{3,275},{4,276},{5,277},{6,278},{7,279},{8... | collective-permute-start | bytes 49160 | tf_op jit(solution)/shard_map/ppermute | solution.py:732

commit v6 on v5

--- a/solution.py
+++ b/solution.py
@@ -228,13 +228,16 @@
         x_west, x_east = select_rows((0, 1), 128), select_rows((none, none, none, 127, 126), 128)
         d_west = select_rows((none, none, 0), 128)
         d_east = select_rows((none, none, none, none, none, 127), 128)
+        picks = jnp.concatenate([x_west, x_west, x_east, x_east, d_west, d_east], axis=1)
         for f in range(V):
-            values = dot_nt(x_west, x[f, :, 0:128]) + dot_nt(x_east, x[f, :, W - 128 : W])
-            values = values + lax.dot_general(
-                d_west, drive[f, :, 0:128], NT, preferred_element_type=F32
-            )
-            values = values + lax.dot_general(
-                d_east, drive[f, :, W - 128 : W], NT, preferred_element_type=F32
+            parts = (
+                *split2(x[f, :, 0:128]),
+                *split2(x[f, :, W - 128 : W]),
+                drive[f, :, 0:128],
+                drive[f, :, W - 128 : W],
+            )
+            values = lax.dot_general(
+                picks, jnp.concatenate(parts, axis=1), NT, preferred_element_type=F32
             )
             for i in range(6):
                 ends[i, f : f + 1, 0:H] = values[i : i + 1]
@@ -356,15 +359,22 @@
         north[...] = up[...]
         south[...] = down[...]
 
+    lane = iota((V, 128), 1)
+
     def fill(to_west, to_east):
-        for out, at, lo in ((to_west, 0, 0), (to_east, 3, W - 128)):
-            out[0:3] = ends[at : at + 3]
-            out[3, :, 0:128] = north[0, :, lo : lo + 128]
-            out[3, :, 128:256] = north[1, :, lo : lo + 128]
-            out[4, :, 0:128] = north[2, :, lo : lo + 128]
-            out[4, :, 128:256] = south[2, :, lo : lo + 128]
-            out[5, :, 0:128] = south[0, :, lo : lo + 128]
-            out[5, :, 128:256] = south[1, :, lo : lo + 128]
+        for i in range(3):
+            to_west[i, :, 0:128] = ends[i, :, 0:128]
+            above = pltpu.roll(north[i, :, 0:128], H - 128, 1)
+            below = pltpu.roll(south[i, :, 0:128], H - 126, 1)
+            to_west[i, :, 128:256] = jnp.where(
+                lane < H - 128, ends[i, :, 128:256], jnp.where(lane < H - 126, above, below)
+            )
+            to_east[i, :, 0:128] = ends[3 + i, :, 0:128]
+            above = north[i, :, W - 128 : W]
+            below = pltpu.roll(south[i, :, W - 128 : W], 126, 1)
+            to_east[i, :, 128:256] = jnp.where(
+                lane < H - 128, ends[3 + i, :, 128:256], jnp.where(lane >= 126, above, below)
+            )
 
     @pl.when(section == 0)
     def _():
@@ -373,7 +383,7 @@
 
 
 def pack(ends, from_one, from_two):
-    flank, row = pltpu.VMEM((6, V, 256), F32), pltpu.VMEM((3, V, W), F32)
+    flank, row = pltpu.VMEM((3, V, 256), F32), pltpu.VMEM((3, V, W), F32)
     return pl.pallas_call(
         pack_kernel,
         in_specs=[VMEM] * 3,
@@ -435,12 +445,16 @@
             )
             return value * keep * exists
 
-        north_1 = join(west[3, :, 0:128], north[0], east[3, :, 0:128])
-        north_2 = join(west[3, :, 128:256], north[1], east[3, :, 128:256])
-        north_f = join(west[4, :, 0:128], north[2], east[4, :, 0:128])
-        south_1 = join(west[5, :, 0:128], south[0], east[5, :, 0:128])
-        south_2 = join(west[5, :, 128:256], south[1], east[5, :, 128:256])
-        south_f = join(west[4, :, 128:256], south[2], east[4, :, 128:256])
+        def beyond_rows(values, to_west, to_east):
+            out = []
+            for i in range(3):
+                before = pltpu.roll(west[i, :, 128:256], to_west, 1)
+                after = pltpu.roll(east[i, :, 128:256], to_east, 1)
+                out.append(join(before, values[i], after))
+            return out
+
+        north_1, north_2, north_f = beyond_rows(north, 0, 256 - H)
+        south_1, south_2, south_f = beyond_rows(south, 2, 254 - H)
         top = with_sides(rows[0], lanes(near_w, 0), lanes(near_e, 0))
         bottom = with_sides(rows[9], lanes(near_w, H - 1), lanes(near_e, H - 1))
         new_north = halo_row(north_1, north_2, north_f, top, an, as_, has_n)
@@ -532,7 +546,7 @@
         in_specs=[VMEM] * 8,
         out_specs=[VMEM] * 4,
         out_shape=[pltpu.VMEM((4 * V, 256), F32)] * 3 + [pltpu.VMEM((2 * V, 256), F32)],
-        scratch_shapes=[pltpu.VMEM((6, V, 256), F32)] * 2,
+        scratch_shapes=[pltpu.VMEM((3, V, 256), F32)] * 2,
         compiler_params=SMALL,
         name="rims",
     )(*near(*arrays))
@@ -621,8 +635,6 @@
         eye = jnp.where(iota((H, H), 0) == iota((H, H), 1), 1.0, 0.0).astype(BF16)
         outer = jnp.where(iota((1, n), 1) < V, aw, ae)
         both = spread(dot_nt(eye, beyond[:, 0:H]) * outer)
-        for f in range(V):
-            with_sides(stepped, f, both)
         old = jnp.concatenate([s[0:n, :] for s in sent], axis=0)
         new = jnp.concatenate([s[n : 2 * n, :] for s in sent], axis=0)
         row_effect, col_effect = edge_effect(old, new, params, row_tent(), col_tent())
@@ -632,28 +644,36 @@
         by_col = dot_left(thirds, sum(col_effect)) * (1.0 / 9.0)
         line = iota((PH, PW), 0)
         fetch.wait()
+        patches = []
         for member in range(3):
             nest = row + member - 1
             entry = role_entry(entries, row, column, member, count)
             slot = lax.rem(entry, 9)
-
-            @pl.when((nest >= 0) & (nest < count) & (lax.div(entry, 9) == row))
-            def _(member=member, slot=slot):
-                at_row = pl.multiple_of(lax.div(slot, 3) * PH, PH)
-                at_col = pl.multiple_of(lax.rem(slot, 3) * PW, PW)
-                mine = (iota(by_col.shape, 1) >> 3) == member
-                beside = spread(jnp.where(mine, by_col, 0.0), member * n)
-                for f in range(V):
-                    left, right, up = f * 128, (V + f) * 128, member * n + f
-                    tile[f, pl.ds(at_row, PH), pl.ds(at_col, PW)] = (
-                        means[member][f]
-                        + jnp.where(line == 0, by_row[up : up + 1], 0.0)
-                        + jnp.where(line == PH - 1, by_row[up + V : up + V + 1], 0.0)
-                        + beside[:, left : left + 128]
-                        + beside[:, right : right + 128]
-                    )
-
+            mine = (iota(by_col.shape, 1) >> 3) == member
+            patches.append(
+                (
+                    (nest >= 0) & (nest < count) & (lax.div(entry, 9) == row),
+                    pl.multiple_of(lax.div(slot, 3) * PH, PH),
+                    pl.multiple_of(lax.rem(slot, 3) * PW, PW),
+                    spread(jnp.where(mine, by_col, 0.0), member * n),
+                )
+            )
         for f in range(V):
+            with_sides(stepped, f, both)
+            for member, (valid, at_row, at_col, beside) in enumerate(patches):
+                left, right, up = f * 128, (V + f) * 128, member * n + f
+                patch = (
+                    means[member][f]
+                    + jnp.where(line == 0, by_row[up : up + 1], 0.0)
+                    + jnp.where(line == PH - 1, by_row[up + V : up + V + 1], 0.0)
+                    + beside[:, left : left + 128]
+                    + beside[:, right : right + 128]
+                )
+
+                @pl.when(valid)
+                def _(at_row=at_row, at_col=at_col, patch=patch):
+                    tile[f, pl.ds(at_row, PH), pl.ds(at_col, PW)] = patch
+
             send(f).start()
 
     @pl.when(jnp.logical_not(parent))

time: 46.4 us -> 45.6 us (0.983)
  the two profiles are of different devices: /device:TPU:34 before, /device:TPU:32 now
where the time goes in v6:
time: 45.6 us; the launch traced here: 45.3 us
  starting transfers between devices  32.1 us (70%)
  waiting for transfers between devices  6.8 us (15%)
  Pallas kernels  5.92 us (13%)
    ppermute x10, starting transfers between devices, shift(): return lax.ppermute(value, AXES, routes(sizes, source, move))  32.1 us
    ppermute x10, waiting for transfers between devices, shift(): return lax.ppermute(value, AXES, routes(sizes, source, move))  6.8 us
    pallas_call x1, Pallas kernels, last(): pl.pallas_call(last_kernel, in_specs=[ANY] + [VMEM] * 15, out_specs=ANY,...  2.54 us
    pallas_call x1, Pallas kernels, edge(): pl.pallas_call(edge_kernel, in_specs=[ANY] * 5, out_specs=[VMEM] * 3, out...  1.16 us
    pallas_call x1, Pallas kernels, banks(): pl.pallas_call(bank_kernel, in_specs=[VMEM] * 5, out_specs=[VMEM] * 3, ou...  1.03 us
  transfers between devices with their start and end apart: 10, of which 3 were waited for; matrix products, arithmetic and copies ran while one was open for 0% of the time, Pallas kernels for 4%

profile of v6, /device:TPU:32, one launch (start us, length us, event | category | flops | bytes accessed | tf_op | source)
XLA Modules:
  0.0 45.3 jit_solution(16772881425638659180)
XLA Ops:
  0.0 0.0 copy-start.1
  0.0 0.0 copy-start
  0.0 1.2 %edge.1 = (f32[3,4,384]{2,1,0:T(4,128)S(1)}, f32[3,4,384]{2,1,0:T(4,128)S(1)}, f32[16,640]{1,0:T(8,128)S(1)}) custom-call(f32[4,192,384]{2,1,0:T(8,128)} %bitcast.6, bf16[4,192,384]{2,1,0:T(8,128)(2,1)} %bitcast.9, f32[2]{0:T(128)} %bitcast.12, f32[4]{0:T(128)} %diffusion.1, s32[16,16]{1,0:T(8,128)} %nest_patch.3), custom_call_target="tpu_custom_call" | custom-call | tf_op jit(solution)/shard_map/edge/pallas_call | solution.py:187
  1.2 0.0 copy-done.1
  1.2 0.4 copy-done
  1.6 0.4 nests.1
  2.0 1.3 %collective-permute-start.9 = (f32[4,64,128]{2,1,0:T(8,128)S(1)}, f32[4,64,128]{2,1,0:T(8,128)S(1)}, u32[]{:S(2)}, u32[]{:S(2)}) collective-permute-start(f32[4,64,128]{2,1,0:T(8,128)S(1)} %get-tuple-element.42), channel_id=1, source_target_pairs={{272,0},{273,1},{274,2},{275,3},{276,4},{277,5},{278,6},{279,7},{2... | collective-permute-start | bytes 393224 | tf_op jit(solution)/shard_map/ppermute | solution.py:752
  3.3 1.3 %collective-permute-start.8 = (f32[4,64,128]{2,1,0:T(8,128)S(1)}, f32[4,64,128]{2,1,0:T(8,128)S(1)}, u32[]{:S(2)}, u32[]{:S(2)}) collective-permute-start(f32[4,64,128]{2,1,0:T(8,128)S(1)} %get-tuple-element.42), channel_id=1, source_target_pairs={{256,0},{257,1},{258,2},{259,3},{260,4},{261,5},{262,6},{263,7},{2... | collective-permute-start | bytes 393224 | tf_op jit(solution)/shard_map/ppermute | solution.py:752
  4.6 0.7 %collective-permute-start.7 = (f32[4,64,128]{2,1,0:T(8,128)S(1)}, f32[4,64,128]{2,1,0:T(8,128)S(1)}, u32[]{:S(2)}, u32[]{:S(2)}) collective-permute-start(f32[4,64,128]{2,1,0:T(8,128)S(1)} %get-tuple-element.42), channel_id=1, source_target_pairs={{256,16},{257,17},{258,18},{259,19},{260,20},{261,21},{262,22},{26... | collective-permute-start | bytes 393224 | tf_op jit(solution)/shard_map/ppermute | solution.py:752
  5.2 6.7 %collective-permute-start = (f32[3,4,384]{2,1,0:T(4,128)S(1)}, f32[3,4,384]{2,1,0:T(4,128)S(1)}, u32[]{:S(2)}, u32[]{:S(2)}) collective-permute-start(f32[3,4,384]{2,1,0:T(4,128)S(1)} %get-tuple-element.26), channel_id=1, source_target_pairs={{0,16},{1,17},{2,18},{3,19},{4,20},{5,21},{6,22},{7,23},{8,24},{9,... | collective-permute-start | bytes 55304 | tf_op jit(solution)/shard_map/ppermute | solution.py:752
  12.0 0.7 %collective-permute-start.1 = (f32[3,4,384]{2,1,0:T(4,128)S(1)}, f32[3,4,384]{2,1,0:T(4,128)S(1)}, u32[]{:S(2)}, u32[]{:S(2)}) collective-permute-start(f32[3,4,384]{2,1,0:T(4,128)S(1)} %get-tuple-element.27), channel_id=1, source_target_pairs={{16,32},{17,33},{18,34},{19,35},{20,36},{21,37},{22,38},{23,39},{2... | collective-permute-start | bytes 55304 | tf_op jit(solution)/shard_map/ppermute | solution.py:752
  12.6 2.7 %collective-permute-done.from_one = f32[3,4,384]{2,1,0:T(4,128)S(1)} collective-permute-done((f32[3,4,384]{2,1,0:T(4,128)S(1)}, f32[3,4,384]{2,1,0:T(4,128)S(1)}, u32[]{:S(2)}, u32[]{:S(2)}) %collective-permute-start) | collective-permute-done | bytes 18464 | tf_op jit(solution)/shard_map/ppermute | solution.py:752
  15.3 0.0 collective-permute-done.1.from_two
  15.3 0.1 pack.1
  15.4 1.9 %collective-permute-start.2 = (f32[3,4,256]{2,1,0:T(4,128)S(1)}, f32[3,4,256]{2,1,0:T(4,128)S(1)}, u32[]{:S(2)}, u32[]{:S(2)}) collective-permute-start(f32[3,4,256]{2,1,0:T(4,128)S(1)} %get-tuple-element.36), channel_id=1, source_target_pairs={{0,1},{1,0},{2,3},{3,2},{4,5},{5,4},{6,7},{7,6},{8,9},{9,8},{10,11... | collective-permute-start | bytes 36872 | tf_op jit(solution)/shard_map/ppermute | solution.py:752
  17.3 2.5 %collective-permute-start.3 = (f32[3,4,256]{2,1,0:T(4,128)S(1)}, f32[3,4,256]{2,1,0:T(4,128)S(1)}, u32[]{:S(2)}, u32[]{:S(2)}) collective-permute-start(f32[3,4,256]{2,1,0:T(4,128)S(1)} %get-tuple-element.37), channel_id=1, source_target_pairs={{1,2},{2,1},{3,4},{4,3},{5,6},{6,5},{7,8},{8,7},{9,10},{10,9},{11,... | collective-permute-start | bytes 36872 | tf_op jit(solution)/shard_map/ppermute | solution.py:752
  19.8 1.0 %banks.1 = (f32[14,4,384]{2,1,0:T(4,128)S(1)}, f32[12,4,256]{2,1,0:T(4,128)S(1)}, f32[4,192,384]{2,1,0:T(8,128)S(1)}) custom-call(f32[16,640]{1,0:T(8,128)S(1)} %get-tuple-element.24.params, f32[4,192,384]{2,1,0:T(8,128)S(1)} %bitcast.8, bf16[4,192,384]{2,1,0:T(8,128)(2,1)S(1)} %bitcast.11, f32[3,4,384]{2,1,0:T(4,128)S(1)} %get-tuple-element.28.north.refs_3_, ...), custom_call_target="tpu_custom_call" | custom-call | tf_op jit(solution)/shard_map/banks/pallas_call | solution.py:341
  20.8 0.0 collective-permute-done.2.refs_5_
  20.8 2.7 %collective-permute-done.3.refs_6_ = f32[3,4,256]{2,1,0:T(4,128)S(1)} collective-permute-done((f32[3,4,256]{2,1,0:T(4,128)S(1)}, f32[3,4,256]{2,1,0:T(4,128)S(1)}, u32[]{:S(2)}, u32[]{:S(2)}) %collective-permute-start.3) | collective-permute-done | bytes 12320 | tf_op jit(solution)/shard_map/ppermute | solution.py:752
  23.5 0.7 %rims.1 = (f32[16,256]{1,0:T(8,128)S(1)}, f32[16,256]{1,0:T(8,128)S(1)}, f32[16,256]{1,0:T(8,128)S(1)}, f32[8,256]{1,0:T(8,128)S(1)}) custom-call(f32[16,640]{1,0:T(8,128)S(1)} %get-tuple-element.24.params, f32[14,4,384]{2,1,0:T(4,128)S(1)} %get-tuple-element.34.refs_0_, f32[12,4,256]{2,1,0:T(4,128)S(1)} %get-tuple-element.35.refs_1_, ...), custom_call_target="tpu_custom_call" | custom-call | tf_op jit(solution)/shard_map/rims/pallas_call | solution.py:544
  24.2 0.7 %collective-permute-start.4 = (f32[16,256]{1,0:T(8,128)S(1)}, f32[16,256]{1,0:T(8,128)S(1)}, u32[]{:S(2)}, u32[]{:S(2)}) collective-permute-start(f32[16,256]{1,0:T(8,128)S(1)} %get-tuple-element.39.sent_0), channel_id=1, source_target_pairs={{16,256},{17,257},{18,258},{19,259},{20,260},{21,261},{22,262},{23... | collective-permute-start | bytes 49160 | tf_op jit(solution)/shard_map/ppermute | solution.py:752
  24.9 1.3 %collective-permute-start.5 = (f32[16,256]{1,0:T(8,128)S(1)}, f32[16,256]{1,0:T(8,128)S(1)}, u32[]{:S(2)}, u32[]{:S(2)}) collective-permute-start(f32[16,256]{1,0:T(8,128)S(1)} %get-tuple-element.40.sent_1), channel_id=1, source_target_pairs={{0,256},{1,257},{2,258},{3,259},{4,260},{5,261},{6,262},{7,263},{8... | collective-permute-start | bytes 49160 | tf_op jit(solution)/shard_map/ppermute | solution.py:752
  26.2 0.0 collective-permute-done.4.got_0
  26.2 15.1 %collective-permute-start.6 = (f32[16,256]{1,0:T(8,128)S(1)}, f32[16,256]{1,0:T(8,128)S(1)}, u32[]{:S(2)}, u32[]{:S(2)}) collective-permute-start(f32[16,256]{1,0:T(8,128)S(1)} %get-tuple-element.41.sent_2), channel_id=1, source_target_pairs={{0,272},{1,273},{2,274},{3,275},{4,276},{5,277},{6,278},{7,279},{8... | collective-permute-start | bytes 49160 | tf_op jit(solution)/shard_map/ppermute | solution.py:752
  41.3 0.0 collective-permute-done.5.got_1
  41.3 1.4 %collective-permute-done.6.got_2 = f32[16,256]{1,0:T(8,128)S(1)} collective-permute-done((f32[16,256]{1,0:T(8,128)S(1)}, f32[16,256]{1,0:T(8,128)S(1)}, u32[]{:S(2)}, u32[]{:S(2)}) %collective-permute-start.6) | collective-permute-done | bytes 16416 | tf_op jit(solution)/shard_map/ppermute | solution.py:752
  42.8 0.0 collective-permute-done.9.mean_2
  42.8 0.0 collective-permute-done.8.mean_1
  42.8 0.0 collective-permute-done.7.mean_0
  42.8 2.5 %last.1 = f32[4,192,384]{2,1,0:T(8,128)} custom-call(s32[16,16]{1,0:T(8,128)} %nest_patch.3, f32[16,640]{1,0:T(8,128)S(1)} %get-tuple-element.24.params, f32[4,192,384]{2,1,0:T(8,128)S(1)} %get-tuple-element.30.stepped, f32[4,192,384]{2,1,0:T(8,128)S(1)} %get-tuple-element.31.y, bf16[256,384]{1,0:T(8,128)(2,1)S(1)} %get-tuple-element.32.tent_row, ...), custom_call_target="tpu_custom_call" | custom-call | tf_op jit(solution)/shard_map/last/pallas_call | solution.py:711
Async XLA Ops:
  0.0 1.2 %copy-start.1 = (bf16[1,4,1,192,384]{4,3,2,1,0:T(8,128)(2,1)S(1)}, bf16[1,4,1,192,384]{4,3,2,1,0:T(8,128)(2,1)}, u32[]{:S(2)}) copy-start(bf16[1,4,1,192,384]{4,3,2,1,0:T(8,128)(2,1)} %param.6) | copy-start | bytes 1769476
  0.0 1.5 %copy-start = (f32[1,4,1,192,384]{4,3,2,1,0:T(8,128)S(1)}, f32[1,4,1,192,384]{4,3,2,1,0:T(8,128)}, u32[]{:S(2)}) copy-start(f32[1,4,1,192,384]{4,3,2,1,0:T(8,128)} %param.5) | copy-start | bytes 3538948
  2.0 40.8 %collective-permute-start.9 = (f32[4,64,128]{2,1,0:T(8,128)S(1)}, f32[4,64,128]{2,1,0:T(8,128)S(1)}, u32[]{:S(2)}, u32[]{:S(2)}) collective-permute-start(f32[4,64,128]{2,1,0:T(8,128)S(1)} %get-tuple-element.42), channel_id=1, source_target_pairs={{272,0},{273,1},{274,2},{275,3},{276,4},{277,5},{278,6},{279,7},{2... | collective-permute-start | bytes 393224 | tf_op jit(solution)/shard_map/ppermute | solution.py:752
  3.3 39.5 %collective-permute-start.8 = (f32[4,64,128]{2,1,0:T(8,128)S(1)}, f32[4,64,128]{2,1,0:T(8,128)S(1)}, u32[]{:S(2)}, u32[]{:S(2)}) collective-permute-start(f32[4,64,128]{2,1,0:T(8,128)S(1)} %get-tuple-element.42), channel_id=1, source_target_pairs={{256,0},{257,1},{258,2},{259,3},{260,4},{261,5},{262,6},{263,7},{2... | collective-permute-start | bytes 393224 | tf_op jit(solution)/shard_map/ppermute | solution.py:752
  4.6 38.2 %collective-permute-start.7 = (f32[4,64,128]{2,1,0:T(8,128)S(1)}, f32[4,64,128]{2,1,0:T(8,128)S(1)}, u32[]{:S(2)}, u32[]{:S(2)}) collective-permute-start(f32[4,64,128]{2,1,0:T(8,128)S(1)} %get-tuple-element.42), channel_id=1, source_target_pairs={{256,16},{257,17},{258,18},{259,19},{260,20},{261,21},{262,22},{26... | collective-permute-start | bytes 393224 | tf_op jit(solution)/shard_map/ppermute | solution.py:752
  5.2 10.0 %collective-permute-start = (f32[3,4,384]{2,1,0:T(4,128)S(1)}, f32[3,4,384]{2,1,0:T(4,128)S(1)}, u32[]{:S(2)}, u32[]{:S(2)}) collective-permute-start(f32[3,4,384]{2,1,0:T(4,128)S(1)} %get-tuple-element.26), channel_id=1, source_target_pairs={{0,16},{1,17},{2,18},{3,19},{4,20},{5,21},{6,22},{7,23},{8,24},{9,... | collective-permute-start | bytes 55304 | tf_op jit(solution)/shard_map/ppermute | solution.py:752
  12.0 3.3 %collective-permute-start.1 = (f32[3,4,384]{2,1,0:T(4,128)S(1)}, f32[3,4,384]{2,1,0:T(4,128)S(1)}, u32[]{:S(2)}, u32[]{:S(2)}) collective-permute-start(f32[3,4,384]{2,1,0:T(4,128)S(1)} %get-tuple-element.27), channel_id=1, source_target_pairs={{16,32},{17,33},{18,34},{19,35},{20,36},{21,37},{22,38},{23,39},{2... | collective-permute-start | bytes 55304 | tf_op jit(solution)/shard_map/ppermute | solution.py:752
  15.4 5.4 %collective-permute-start.2 = (f32[3,4,256]{2,1,0:T(4,128)S(1)}, f32[3,4,256]{2,1,0:T(4,128)S(1)}, u32[]{:S(2)}, u32[]{:S(2)}) collective-permute-start(f32[3,4,256]{2,1,0:T(4,128)S(1)} %get-tuple-element.36), channel_id=1, source_target_pairs={{0,1},{1,0},{2,3},{3,2},{4,5},{5,4},{6,7},{7,6},{8,9},{9,8},{10,11... | collective-permute-start | bytes 36872 | tf_op jit(solution)/shard_map/ppermute | solution.py:752
  17.3 6.2 %collective-permute-start.3 = (f32[3,4,256]{2,1,0:T(4,128)S(1)}, f32[3,4,256]{2,1,0:T(4,128)S(1)}, u32[]{:S(2)}, u32[]{:S(2)}) collective-permute-start(f32[3,4,256]{2,1,0:T(4,128)S(1)} %get-tuple-element.37), channel_id=1, source_target_pairs={{1,2},{2,1},{3,4},{4,3},{5,6},{6,5},{7,8},{8,7},{9,10},{10,9},{11,... | collective-permute-start | bytes 36872 | tf_op jit(solution)/shard_map/ppermute | solution.py:752
  24.2 2.0 %collective-permute-start.4 = (f32[16,256]{1,0:T(8,128)S(1)}, f32[16,256]{1,0:T(8,128)S(1)}, u32[]{:S(2)}, u32[]{:S(2)}) collective-permute-start(f32[16,256]{1,0:T(8,128)S(1)} %get-tuple-element.39.sent_0), channel_id=1, source_target_pairs={{16,256},{17,257},{18,258},{19,259},{20,260},{21,261},{22,262},{23... | collective-permute-start | bytes 49160 | tf_op jit(solution)/shard_map/ppermute | solution.py:752
  24.9 16.4 %collective-permute-start.5 = (f32[16,256]{1,0:T(8,128)S(1)}, f32[16,256]{1,0:T(8,128)S(1)}, u32[]{:S(2)}, u32[]{:S(2)}) collective-permute-start(f32[16,256]{1,0:T(8,128)S(1)} %get-tuple-element.40.sent_1), channel_id=1, source_target_pairs={{0,256},{1,257},{2,258},{3,259},{4,260},{5,261},{6,262},{7,263},{8... | collective-permute-start | bytes 49160 | tf_op jit(solution)/shard_map/ppermute | solution.py:752
  26.2 16.6 %collective-permute-start.6 = (f32[16,256]{1,0:T(8,128)S(1)}, f32[16,256]{1,0:T(8,128)S(1)}, u32[]{:S(2)}, u32[]{:S(2)}) collective-permute-start(f32[16,256]{1,0:T(8,128)S(1)} %get-tuple-element.41.sent_2), channel_id=1, source_target_pairs={{0,272},{1,273},{2,274},{3,275},{4,276},{5,277},{6,278},{7,279},{8... | collective-permute-start | bytes 49160 | tf_op jit(solution)/shard_map/ppermute | solution.py:752

commit v7 on v6

--- a/solution.py
+++ b/solution.py
@@ -608,26 +608,26 @@
     return dot_right(values, jnp.where((lane == target) & valid, 1.0, 0.0).astype(BF16))
 
 
-def last_kernel(
-    nest_patch, params, stepped, y, tent_row, tent_col, beyond,
-    sent_0, sent_1, sent_2, got_0, got_1, got_2, mean_0, mean_1, mean_2, out, tile, entries, sems,
+def put_sides(tile, base, f, both):
+    left, right = f * 128, (V + f) * 128
+    tile[f, :, 0:128] = base[f, :, 0:128] + both[:, left : left + 128]
+    tile[f, :, 128 : W - 128] = base[f, :, 128 : W - 128]
+    tile[f, :, W - 128 : W] = base[f, :, W - 128 : W] + both[:, right : right + 128]
+
+
+def parents_kernel(
+    nest_patch, params, stepped, beyond, sent_0, sent_1, sent_2, mean_0, mean_1, mean_2,
+    out, tile, entries, sems,
 ):
     section, row, column = position()
     count = nest_patch.shape[0]
-    parent = section == 0
-    sent, got, means = (sent_0, sent_1, sent_2), (got_0, got_1, got_2), (mean_0, mean_1, mean_2)
+    sent, means = (sent_0, sent_1, sent_2), (mean_0, mean_1, mean_2)
     n = 2 * V
 
     def send(f):
         return pltpu.make_async_copy(tile.at[f], out.at[f], sems.at[f])
 
-    def with_sides(base, f, both):
-        left, right = f * 128, (V + f) * 128
-        tile[f, :, 0:128] = base[f, :, 0:128] + both[:, left : left + 128]
-        tile[f, :, 128 : W - 128] = base[f, :, 128 : W - 128]
-        tile[f, :, W - 128 : W] = base[f, :, W - 128 : W] + both[:, right : right + 128]
-
-    @pl.when(parent)
+    @pl.when(section == 0)
     def _():
         fetch = pltpu.make_async_copy(nest_patch, entries, sems.at[V])
         fetch.start()
@@ -659,7 +659,7 @@
                 )
             )
         for f in range(V):
-            with_sides(stepped, f, both)
+            put_sides(tile, stepped, f, both)
             for member, (valid, at_row, at_col, beside) in enumerate(patches):
                 left, right, up = f * 128, (V + f) * 128, member * n + f
                 patch = (
@@ -676,7 +676,35 @@
 
             send(f).start()
 
-    @pl.when(jnp.logical_not(parent))
+        for f in range(V):
+            send(f).wait()
+
+
+def parents(nest_patch, *arrays):
+    return pl.pallas_call(
+        parents_kernel,
+        in_specs=[ANY] + [VMEM] * 9,
+        out_specs=ANY,
+        out_shape=jax.ShapeDtypeStruct((V, H, W), F32),
+        scratch_shapes=[
+            pltpu.VMEM((V, H, W), F32),
+            pltpu.SMEM(nest_patch.shape, jnp.int32),
+            pltpu.SemaphoreType.DMA((V + 1,)),
+        ],
+        compiler_params=SMALL,
+        name="parents",
+    )(*far(nest_patch), *near(*arrays))
+
+
+def last_kernel(done, params, y, tent_row, tent_col, got_0, got_1, got_2, out, tile, sems):
+    del done
+    got = (got_0, got_1, got_2)
+    n = 2 * V
+
+    def send(f):
+        return pltpu.make_async_copy(tile.at[f], out.at[f], sems.at[f])
+
+    @pl.when(position()[0] != 0)
     def _():
         member = params[MEMBER : MEMBER + 1, 0:256]
         u = jnp.where(
@@ -692,7 +720,7 @@
             )
         )
         for f in range(V):
-            with_sides(y, f, both)
+            put_sides(tile, y, f, both)
             for depth in range(3):
                 bottom = H - 1 - depth
                 tile[f, depth : depth + 1, :] = (
@@ -703,24 +731,21 @@
                 )
             send(f).start()
 
-    for f in range(V):
-        send(f).wait()
-
-
-def last(nest_patch, *arrays):
+        for f in range(V):
+            send(f).wait()
+
+
+def last(done, *arrays):
     return pl.pallas_call(
         last_kernel,
-        in_specs=[ANY] + [VMEM] * 15,
+        in_specs=[ANY] + [VMEM] * 7,
         out_specs=ANY,
         out_shape=jax.ShapeDtypeStruct((V, H, W), F32),
-        scratch_shapes=[
-            pltpu.VMEM((V, H, W), F32),
-            pltpu.SMEM(nest_patch.shape, jnp.int32),
-            pltpu.SemaphoreType.DMA((V + 1,)),
-        ],
+        input_output_aliases={0: 0},
+        scratch_shapes=[pltpu.VMEM((V, H, W), F32), pltpu.SemaphoreType.DMA((V,))],
         compiler_params=SMALL,
         name="last",
-    )(*far(nest_patch), *near(*arrays))
+    )(done, *near(*arrays))
 
 
 def routes(sizes, source, move):
@@ -767,9 +792,8 @@
         sizes[1:], params, rows, cols, ends, north, south, cols_one, cols_two
     )
     got = [shift(sent[m], 0, lambda r, c, m=m: (1, r + m - 1, c)) for m in range(3)]
-    out = last(
-        nest_patch, params, stepped, y, *tents, beyond, *sent, *got, *means
-    )
+    done = parents(nest_patch, params, stepped, beyond, *sent, *means)
+    out = last(done, params, y, *tents, *got)
     return out.reshape(fields.shape)
 
 

time: 45.6 us -> 42.2 us (0.925)
  the two profiles are of different devices: /device:TPU:32 before, /device:TPU:102 now
where the time goes in v7:
time: 42.2 us; the launch traced here: 41.8 us
  waiting for transfers between devices  18.3 us (43%)
  starting transfers between devices  16.4 us (39%)
  Pallas kernels  6.52 us (15%)
    ppermute x10, waiting for transfers between devices, shift(): return lax.ppermute(value, AXES, routes(sizes, source, move))  18.3 us
    ppermute x10, starting transfers between devices, shift(): return lax.ppermute(value, AXES, routes(sizes, source, move))  16.4 us
    pallas_call x1, Pallas kernels, nests(): pl.pallas_call(nests_kernel, in_specs=[VMEM] * 3, out_specs=[VMEM] * 5, o...  3.41 us
    pallas_call x1, Pallas kernels, last(): pl.pallas_call(last_kernel, in_specs=[ANY] + [VMEM] * 7, out_specs=ANY, o...  1.83 us
    pallas_call x1, Pallas kernels, edge(): pl.pallas_call(edge_kernel, in_specs=[ANY] * 5, out_specs=[VMEM] * 3, out...  1.16 us
  transfers between devices with their start and end apart: 10, of which 3 were waited for; matrix products, arithmetic and copies ran while one was open for 0% of the time, Pallas kernels for 0%

profile of v7, /device:TPU:102, one launch (start us, length us, event | category | flops | bytes accessed | tf_op | source)
XLA Modules:
  0.0 41.8 jit_solution(9593746507123425825)
XLA Ops:
  0.0 0.0 copy-start.1
  0.0 0.0 copy-start
  0.0 1.2 %edge.1 = (f32[3,4,384]{2,1,0:T(4,128)S(1)}, f32[3,4,384]{2,1,0:T(4,128)S(1)}, f32[16,640]{1,0:T(8,128)S(1)}) custom-call(f32[4,192,384]{2,1,0:T(8,128)} %bitcast.6, bf16[4,192,384]{2,1,0:T(8,128)(2,1)} %bitcast.9, f32[2]{0:T(128)} %bitcast.12, f32[4]{0:T(128)} %diffusion.1, s32[16,16]{1,0:T(8,128)} %nest_patch.3), custom_call_target="tpu_custom_call" | custom-call | tf_op jit(solution)/shard_map/edge/pallas_call | solution.py:187
  1.2 0.0 copy-done.1
  1.2 0.4 copy-done
  1.6 3.4 %nests.1 = (f32[4,192,384]{2,1,0:T(8,128)S(1)}, f32[4,64,128]{2,1,0:T(8,128)S(1)}, f32[6,4,256]{2,1,0:T(4,128)S(1)}, bf16[256,384]{1,0:T(8,128)(2,1)S(1)}, bf16[192,256]{1,0:T(8,128)(2,1)S(1)}) custom-call(f32[16,640]{1,0:T(8,128)S(1)} %get-tuple-element.24.params, f32[4,192,384]{2,1,0:T(8,128)S(1)} %bitcast.7, bf16[4,192,384]{2,1,0:T(8,128)(2,1)S(1)} %bitcast.10), custom_call_target="tpu_custom_call" | custom-call | tf_op jit(solution)/shard_map/nests/pallas_call | solution.py:294
  5.0 7.3 %collective-permute-start.6 = (f32[4,64,128]{2,1,0:T(8,128)S(1)}, f32[4,64,128]{2,1,0:T(8,128)S(1)}, u32[]{:S(2)}, u32[]{:S(2)}) collective-permute-start(f32[4,64,128]{2,1,0:T(8,128)S(1)} %get-tuple-element.39), channel_id=1, source_target_pairs={{272,0},{273,1},{274,2},{275,3},{276,4},{277,5},{278,6},{279,7},{2... | collective-permute-start | bytes 393224 | tf_op jit(solution)/shard_map/ppermute | solution.py:777
  12.3 1.3 %collective-permute-start.5 = (f32[4,64,128]{2,1,0:T(8,128)S(1)}, f32[4,64,128]{2,1,0:T(8,128)S(1)}, u32[]{:S(2)}, u32[]{:S(2)}) collective-permute-start(f32[4,64,128]{2,1,0:T(8,128)S(1)} %get-tuple-element.39), channel_id=1, source_target_pairs={{256,0},{257,1},{258,2},{259,3},{260,4},{261,5},{262,6},{263,7},{2... | collective-permute-start | bytes 393224 | tf_op jit(solution)/shard_map/ppermute | solution.py:777
  13.6 1.3 %collective-permute-start.4 = (f32[4,64,128]{2,1,0:T(8,128)S(1)}, f32[4,64,128]{2,1,0:T(8,128)S(1)}, u32[]{:S(2)}, u32[]{:S(2)}) collective-permute-start(f32[4,64,128]{2,1,0:T(8,128)S(1)} %get-tuple-element.39), channel_id=1, source_target_pairs={{256,16},{257,17},{258,18},{259,19},{260,20},{261,21},{262,22},{26... | collective-permute-start | bytes 393224 | tf_op jit(solution)/shard_map/ppermute | solution.py:777
  14.9 0.7 %collective-permute-start = (f32[3,4,384]{2,1,0:T(4,128)S(1)}, f32[3,4,384]{2,1,0:T(4,128)S(1)}, u32[]{:S(2)}, u32[]{:S(2)}) collective-permute-start(f32[3,4,384]{2,1,0:T(4,128)S(1)} %get-tuple-element.26), channel_id=1, source_target_pairs={{0,16},{1,17},{2,18},{3,19},{4,20},{5,21},{6,22},{7,23},{8,24},{9,... | collective-permute-start | bytes 55304 | tf_op jit(solution)/shard_map/ppermute | solution.py:777
  15.6 0.7 %collective-permute-start.1 = (f32[3,4,384]{2,1,0:T(4,128)S(1)}, f32[3,4,384]{2,1,0:T(4,128)S(1)}, u32[]{:S(2)}, u32[]{:S(2)}) collective-permute-start(f32[3,4,384]{2,1,0:T(4,128)S(1)} %get-tuple-element.27), channel_id=1, source_target_pairs={{16,32},{17,33},{18,34},{19,35},{20,36},{21,37},{22,38},{23,39},{2... | collective-permute-start | bytes 55304 | tf_op jit(solution)/shard_map/ppermute | solution.py:777
  16.2 0.0 collective-permute-done.from_one
  16.2 0.0 collective-permute-done.1.from_two
  16.3 0.7 %collective-permute-start.2 = (f32[3,4,256]{2,1,0:T(4,128)S(1)}, f32[3,4,256]{2,1,0:T(4,128)S(1)}, u32[]{:S(2)}, u32[]{:S(2)}) collective-permute-start(f32[3,4,256]{2,1,0:T(4,128)S(1)} %get-tuple-element.33), channel_id=1, source_target_pairs={{0,1},{1,0},{2,3},{3,2},{4,5},{5,4},{6,7},{7,6},{8,9},{9,8},{10,11... | collective-permute-start | bytes 36872 | tf_op jit(solution)/shard_map/ppermute | solution.py:777
  16.9 0.7 %collective-permute-start.3 = (f32[3,4,256]{2,1,0:T(4,128)S(1)}, f32[3,4,256]{2,1,0:T(4,128)S(1)}, u32[]{:S(2)}, u32[]{:S(2)}) collective-permute-start(f32[3,4,256]{2,1,0:T(4,128)S(1)} %get-tuple-element.34), channel_id=1, source_target_pairs={{1,2},{2,1},{3,4},{4,3},{5,6},{6,5},{7,8},{8,7},{9,10},{10,9},{11,... | collective-permute-start | bytes 36872 | tf_op jit(solution)/shard_map/ppermute | solution.py:777
  17.6 0.0 collective-permute-done.2.refs_5_
  17.6 0.0 collective-permute-done.3.refs_6_
  17.7 1.3 %collective-permute-start.7 = (f32[16,256]{1,0:T(8,128)S(1)}, f32[16,256]{1,0:T(8,128)S(1)}, u32[]{:S(2)}, u32[]{:S(2)}) collective-permute-start(f32[16,256]{1,0:T(8,128)S(1)} %get-tuple-element.36.sent_0), channel_id=1, source_target_pairs={{16,256},{17,257},{18,258},{19,259},{20,260},{21,261},{22,262},{23... | collective-permute-start | bytes 49160 | tf_op jit(solution)/shard_map/ppermute | solution.py:777
  19.0 1.3 %collective-permute-start.8 = (f32[16,256]{1,0:T(8,128)S(1)}, f32[16,256]{1,0:T(8,128)S(1)}, u32[]{:S(2)}, u32[]{:S(2)}) collective-permute-start(f32[16,256]{1,0:T(8,128)S(1)} %get-tuple-element.37.sent_1), channel_id=1, source_target_pairs={{0,256},{1,257},{2,258},{3,259},{4,260},{5,261},{6,262},{7,263},{8... | collective-permute-start | bytes 49160 | tf_op jit(solution)/shard_map/ppermute | solution.py:777
  20.3 0.0 collective-permute-done.6.mean_2
  20.3 1.3 %collective-permute-start.9 = (f32[16,256]{1,0:T(8,128)S(1)}, f32[16,256]{1,0:T(8,128)S(1)}, u32[]{:S(2)}, u32[]{:S(2)}) collective-permute-start(f32[16,256]{1,0:T(8,128)S(1)} %get-tuple-element.38.sent_2), channel_id=1, source_target_pairs={{0,272},{1,273},{2,274},{3,275},{4,276},{5,277},{6,278},{7,279},{8... | collective-permute-start | bytes 49160 | tf_op jit(solution)/shard_map/ppermute | solution.py:777
  21.6 0.0 collective-permute-done.5.mean_1
  21.6 0.0 collective-permute-done.4.mean_0
  21.6 0.1 parents.1.done
  21.7 11.4 %collective-permute-done.7.got_0 = f32[16,256]{1,0:T(8,128)S(1)} collective-permute-done((f32[16,256]{1,0:T(8,128)S(1)}, f32[16,256]{1,0:T(8,128)S(1)}, u32[]{:S(2)}, u32[]{:S(2)}) %collective-permute-start.7) | collective-permute-done | bytes 16416 | tf_op jit(solution)/shard_map/ppermute | solution.py:777
  33.1 1.1 %collective-permute-done.8.got_1 = f32[16,256]{1,0:T(8,128)S(1)} collective-permute-done((f32[16,256]{1,0:T(8,128)S(1)}, f32[16,256]{1,0:T(8,128)S(1)}, u32[]{:S(2)}, u32[]{:S(2)}) %collective-permute-start.8) | collective-permute-done | bytes 16416 | tf_op jit(solution)/shard_map/ppermute | solution.py:777
  34.2 5.9 %collective-permute-done.9.got_2 = f32[16,256]{1,0:T(8,128)S(1)} collective-permute-done((f32[16,256]{1,0:T(8,128)S(1)}, f32[16,256]{1,0:T(8,128)S(1)}, u32[]{:S(2)}, u32[]{:S(2)}) %collective-permute-start.9) | collective-permute-done | bytes 16416 | tf_op jit(solution)/shard_map/ppermute | solution.py:777
  40.0 1.8 %last.1 = f32[4,192,384]{2,1,0:T(8,128)} custom-call(f32[4,192,384]{2,1,0:T(8,128)} %parents.1.done, f32[16,640]{1,0:T(8,128)S(1)} %get-tuple-element.24.params, f32[4,192,384]{2,1,0:T(8,128)S(1)} %get-tuple-element.40.y, bf16[256,384]{1,0:T(8,128)(2,1)S(1)} %get-tuple-element.41.tent_row, ...), custom_call_target="tpu_custom_call", output_to_operand_aliasing={{}: (0, {})} | custom-call | tf_op jit(solution)/shard_map/last/pallas_call | solution.py:739
  (3 shorter events, 0.1 us)
Async XLA Ops:
  0.0 1.2 %copy-start.1 = (bf16[1,4,1,192,384]{4,3,2,1,0:T(8,128)(2,1)S(1)}, bf16[1,4,1,192,384]{4,3,2,1,0:T(8,128)(2,1)}, u32[]{:S(2)}) copy-start(bf16[1,4,1,192,384]{4,3,2,1,0:T(8,128)(2,1)} %param.6) | copy-start | bytes 1769476
  0.0 1.5 %copy-start = (f32[1,4,1,192,384]{4,3,2,1,0:T(8,128)S(1)}, f32[1,4,1,192,384]{4,3,2,1,0:T(8,128)}, u32[]{:S(2)}) copy-start(f32[1,4,1,192,384]{4,3,2,1,0:T(8,128)} %param.5) | copy-start | bytes 3538948
  5.0 15.3 %collective-permute-start.6 = (f32[4,64,128]{2,1,0:T(8,128)S(1)}, f32[4,64,128]{2,1,0:T(8,128)S(1)}, u32[]{:S(2)}, u32[]{:S(2)}) collective-permute-start(f32[4,64,128]{2,1,0:T(8,128)S(1)} %get-tuple-element.39), channel_id=1, source_target_pairs={{272,0},{273,1},{274,2},{275,3},{276,4},{277,5},{278,6},{279,7},{2... | collective-permute-start | bytes 393224 | tf_op jit(solution)/shard_map/ppermute | solution.py:777
  12.3 9.3 %collective-permute-start.5 = (f32[4,64,128]{2,1,0:T(8,128)S(1)}, f32[4,64,128]{2,1,0:T(8,128)S(1)}, u32[]{:S(2)}, u32[]{:S(2)}) collective-permute-start(f32[4,64,128]{2,1,0:T(8,128)S(1)} %get-tuple-element.39), channel_id=1, source_target_pairs={{256,0},{257,1},{258,2},{259,3},{260,4},{261,5},{262,6},{263,7},{2... | collective-permute-start | bytes 393224 | tf_op jit(solution)/shard_map/ppermute | solution.py:777
  13.6 8.0 %collective-permute-start.4 = (f32[4,64,128]{2,1,0:T(8,128)S(1)}, f32[4,64,128]{2,1,0:T(8,128)S(1)}, u32[]{:S(2)}, u32[]{:S(2)}) collective-permute-start(f32[4,64,128]{2,1,0:T(8,128)S(1)} %get-tuple-element.39), channel_id=1, source_target_pairs={{256,16},{257,17},{258,18},{259,19},{260,20},{261,21},{262,22},{26... | collective-permute-start | bytes 393224 | tf_op jit(solution)/shard_map/ppermute | solution.py:777
  14.9 1.3 %collective-permute-start = (f32[3,4,384]{2,1,0:T(4,128)S(1)}, f32[3,4,384]{2,1,0:T(4,128)S(1)}, u32[]{:S(2)}, u32[]{:S(2)}) collective-permute-start(f32[3,4,384]{2,1,0:T(4,128)S(1)} %get-tuple-element.26), channel_id=1, source_target_pairs={{0,16},{1,17},{2,18},{3,19},{4,20},{5,21},{6,22},{7,23},{8,24},{9,... | collective-permute-start | bytes 55304 | tf_op jit(solution)/shard_map/ppermute | solution.py:777
  15.6 0.7 %collective-permute-start.1 = (f32[3,4,384]{2,1,0:T(4,128)S(1)}, f32[3,4,384]{2,1,0:T(4,128)S(1)}, u32[]{:S(2)}, u32[]{:S(2)}) collective-permute-start(f32[3,4,384]{2,1,0:T(4,128)S(1)} %get-tuple-element.27), channel_id=1, source_target_pairs={{16,32},{17,33},{18,34},{19,35},{20,36},{21,37},{22,38},{23,39},{2... | collective-permute-start | bytes 55304 | tf_op jit(solution)/shard_map/ppermute | solution.py:777
  16.3 1.4 %collective-permute-start.2 = (f32[3,4,256]{2,1,0:T(4,128)S(1)}, f32[3,4,256]{2,1,0:T(4,128)S(1)}, u32[]{:S(2)}, u32[]{:S(2)}) collective-permute-start(f32[3,4,256]{2,1,0:T(4,128)S(1)} %get-tuple-element.33), channel_id=1, source_target_pairs={{0,1},{1,0},{2,3},{3,2},{4,5},{5,4},{6,7},{7,6},{8,9},{9,8},{10,11... | collective-permute-start | bytes 36872 | tf_op jit(solution)/shard_map/ppermute | solution.py:777
  16.9 0.7 %collective-permute-start.3 = (f32[3,4,256]{2,1,0:T(4,128)S(1)}, f32[3,4,256]{2,1,0:T(4,128)S(1)}, u32[]{:S(2)}, u32[]{:S(2)}) collective-permute-start(f32[3,4,256]{2,1,0:T(4,128)S(1)} %get-tuple-element.34), channel_id=1, source_target_pairs={{1,2},{2,1},{3,4},{4,3},{5,6},{6,5},{7,8},{8,7},{9,10},{10,9},{11,... | collective-permute-start | bytes 36872 | tf_op jit(solution)/shard_map/ppermute | solution.py:777
  17.7 15.4 %collective-permute-start.7 = (f32[16,256]{1,0:T(8,128)S(1)}, f32[16,256]{1,0:T(8,128)S(1)}, u32[]{:S(2)}, u32[]{:S(2)}) collective-permute-start(f32[16,256]{1,0:T(8,128)S(1)} %get-tuple-element.36.sent_0), channel_id=1, source_target_pairs={{16,256},{17,257},{18,258},{19,259},{20,260},{21,261},{22,262},{23... | collective-permute-start | bytes 49160 | tf_op jit(solution)/shard_map/ppermute | solution.py:777
  19.0 15.2 %collective-permute-start.8 = (f32[16,256]{1,0:T(8,128)S(1)}, f32[16,256]{1,0:T(8,128)S(1)}, u32[]{:S(2)}, u32[]{:S(2)}) collective-permute-start(f32[16,256]{1,0:T(8,128)S(1)} %get-tuple-element.37.sent_1), channel_id=1, source_target_pairs={{0,256},{1,257},{2,258},{3,259},{4,260},{5,261},{6,262},{7,263},{8... | collective-permute-start | bytes 49160 | tf_op jit(solution)/shard_map/ppermute | solution.py:777
  20.3 19.7 %collective-permute-start.9 = (f32[16,256]{1,0:T(8,128)S(1)}, f32[16,256]{1,0:T(8,128)S(1)}, u32[]{:S(2)}, u32[]{:S(2)}) collective-permute-start(f32[16,256]{1,0:T(8,128)S(1)} %get-tuple-element.38.sent_2), channel_id=1, source_target_pairs={{0,272},{1,273},{2,274},{3,275},{4,276},{5,277},{6,278},{7,279},{8... | collective-permute-start | bytes 49160 | tf_op jit(solution)/shard_map/ppermute | solution.py:777

commit v8 on v7

--- a/solution.py
+++ b/solution.py
@@ -599,13 +599,12 @@
     return third_0, third_1, third_2
 
 
-def spread(values, first=0):
+def spread(values):
     shape = (values.shape[1], 2 * V * 128)
-    index, lane = iota(shape, 0) - first, iota(shape, 1)
+    index, lane = iota(shape, 0), iota(shape, 1)
     block, depth = index & (2 * V - 1), index >> 3
     target = block * 128 + jnp.where(block < V, depth, 127 - depth)
-    valid = (index >= 0) & (depth < 3)
-    return dot_right(values, jnp.where((lane == target) & valid, 1.0, 0.0).astype(BF16))
+    return dot_right(values, jnp.where(lane == target, 1.0, 0.0).astype(BF16))
 
 
 def put_sides(tile, base, f, both):
@@ -642,32 +641,30 @@
         thirds = iota((PH, H), 1) - 3 * iota((PH, H), 0)
         thirds = jnp.where((thirds >= 0) & (thirds <= 2), 1.0, 0.0).astype(BF16)
         by_col = dot_left(thirds, sum(col_effect)) * (1.0 / 9.0)
-        line = iota((PH, PW), 0)
+        line, lane = iota((PH, PW), 0), iota((PH, PW), 1)
         fetch.wait()
         patches = []
         for member in range(3):
             nest = row + member - 1
             entry = role_entry(entries, row, column, member, count)
             slot = lax.rem(entry, 9)
-            mine = (iota(by_col.shape, 1) >> 3) == member
             patches.append(
                 (
                     (nest >= 0) & (nest < count) & (lax.div(entry, 9) == row),
                     pl.multiple_of(lax.div(slot, 3) * PH, PH),
                     pl.multiple_of(lax.rem(slot, 3) * PW, PW),
-                    spread(jnp.where(mine, by_col, 0.0), member * n),
                 )
             )
         for f in range(V):
             put_sides(tile, stepped, f, both)
-            for member, (valid, at_row, at_col, beside) in enumerate(patches):
-                left, right, up = f * 128, (V + f) * 128, member * n + f
+            for member, (valid, at_row, at_col) in enumerate(patches):
+                up = member * n + f
                 patch = (
                     means[member][f]
                     + jnp.where(line == 0, by_row[up : up + 1], 0.0)
                     + jnp.where(line == PH - 1, by_row[up + V : up + V + 1], 0.0)
-                    + beside[:, left : left + 128]
-                    + beside[:, right : right + 128]
+                    + jnp.where(lane == 0, by_col[:, up : up + 1], 0.0)
+                    + jnp.where(lane == PW - 1, by_col[:, up + V : up + V + 1], 0.0)
                 )
 
                 @pl.when(valid)

time: 42.2 us -> 42.2 us (level)
  no operation moved by 1% of the time
where the time goes in v8:
time: 42.2 us; the launch traced here: 41.8 us
  waiting for transfers between devices  18.3 us (43%)
  starting transfers between devices  16.4 us (39%)
  Pallas kernels  6.52 us (15%)
    ppermute x10, waiting for transfers between devices, shift(): return lax.ppermute(value, AXES, routes(sizes, source, move))  18.3 us
    ppermute x10, starting transfers between devices, shift(): return lax.ppermute(value, AXES, routes(sizes, source, move))  16.4 us
    pallas_call x1, Pallas kernels, nests(): pl.pallas_call(nests_kernel, in_specs=[VMEM] * 3, out_specs=[VMEM] * 5, o...  3.41 us
    pallas_call x1, Pallas kernels, last(): pl.pallas_call(last_kernel, in_specs=[ANY] + [VMEM] * 7, out_specs=ANY, o...  1.83 us
    pallas_call x1, Pallas kernels, edge(): pl.pallas_call(edge_kernel, in_specs=[ANY] * 5, out_specs=[VMEM] * 3, out...  1.16 us
  transfers between devices with their start and end apart: 10, of which 3 were waited for; matrix products, arithmetic and copies ran while one was open for 0% of the time, Pallas kernels for 0%

profile of v8, /device:TPU:102, one launch (start us, length us, event | category | flops | bytes accessed | tf_op | source)
XLA Modules:
  0.0 41.8 jit_solution(13153329811747399884)
XLA Ops:
  0.0 0.0 copy-start.1
  0.0 0.0 copy-start
  0.0 1.2 %edge.1 = (f32[3,4,384]{2,1,0:T(4,128)S(1)}, f32[3,4,384]{2,1,0:T(4,128)S(1)}, f32[16,640]{1,0:T(8,128)S(1)}) custom-call(f32[4,192,384]{2,1,0:T(8,128)} %bitcast.6, bf16[4,192,384]{2,1,0:T(8,128)(2,1)} %bitcast.9, f32[2]{0:T(128)} %bitcast.12, f32[4]{0:T(128)} %diffusion.1, s32[16,16]{1,0:T(8,128)} %nest_patch.3), custom_call_target="tpu_custom_call" | custom-call | tf_op jit(solution)/shard_map/edge/pallas_call | solution.py:187
  1.2 0.0 copy-done.1
  1.2 0.4 copy-done
  1.6 3.4 %nests.1 = (f32[4,192,384]{2,1,0:T(8,128)S(1)}, f32[4,64,128]{2,1,0:T(8,128)S(1)}, f32[6,4,256]{2,1,0:T(4,128)S(1)}, bf16[256,384]{1,0:T(8,128)(2,1)S(1)}, bf16[192,256]{1,0:T(8,128)(2,1)S(1)}) custom-call(f32[16,640]{1,0:T(8,128)S(1)} %get-tuple-element.24.params, f32[4,192,384]{2,1,0:T(8,128)S(1)} %bitcast.7, bf16[4,192,384]{2,1,0:T(8,128)(2,1)S(1)} %bitcast.10), custom_call_target="tpu_custom_call" | custom-call | tf_op jit(solution)/shard_map/nests/pallas_call | solution.py:294
  5.0 7.3 %collective-permute-start.6 = (f32[4,64,128]{2,1,0:T(8,128)S(1)}, f32[4,64,128]{2,1,0:T(8,128)S(1)}, u32[]{:S(2)}, u32[]{:S(2)}) collective-permute-start(f32[4,64,128]{2,1,0:T(8,128)S(1)} %get-tuple-element.39), channel_id=1, source_target_pairs={{272,0},{273,1},{274,2},{275,3},{276,4},{277,5},{278,6},{279,7},{2... | collective-permute-start | bytes 393224 | tf_op jit(solution)/shard_map/ppermute | solution.py:774
  12.3 1.3 %collective-permute-start.5 = (f32[4,64,128]{2,1,0:T(8,128)S(1)}, f32[4,64,128]{2,1,0:T(8,128)S(1)}, u32[]{:S(2)}, u32[]{:S(2)}) collective-permute-start(f32[4,64,128]{2,1,0:T(8,128)S(1)} %get-tuple-element.39), channel_id=1, source_target_pairs={{256,0},{257,1},{258,2},{259,3},{260,4},{261,5},{262,6},{263,7},{2... | collective-permute-start | bytes 393224 | tf_op jit(solution)/shard_map/ppermute | solution.py:774
  13.6 1.3 %collective-permute-start.4 = (f32[4,64,128]{2,1,0:T(8,128)S(1)}, f32[4,64,128]{2,1,0:T(8,128)S(1)}, u32[]{:S(2)}, u32[]{:S(2)}) collective-permute-start(f32[4,64,128]{2,1,0:T(8,128)S(1)} %get-tuple-element.39), channel_id=1, source_target_pairs={{256,16},{257,17},{258,18},{259,19},{260,20},{261,21},{262,22},{26... | collective-permute-start | bytes 393224 | tf_op jit(solution)/shard_map/ppermute | solution.py:774
  14.9 0.7 %collective-permute-start = (f32[3,4,384]{2,1,0:T(4,128)S(1)}, f32[3,4,384]{2,1,0:T(4,128)S(1)}, u32[]{:S(2)}, u32[]{:S(2)}) collective-permute-start(f32[3,4,384]{2,1,0:T(4,128)S(1)} %get-tuple-element.26), channel_id=1, source_target_pairs={{0,16},{1,17},{2,18},{3,19},{4,20},{5,21},{6,22},{7,23},{8,24},{9,... | collective-permute-start | bytes 55304 | tf_op jit(solution)/shard_map/ppermute | solution.py:774
  15.6 0.7 %collective-permute-start.1 = (f32[3,4,384]{2,1,0:T(4,128)S(1)}, f32[3,4,384]{2,1,0:T(4,128)S(1)}, u32[]{:S(2)}, u32[]{:S(2)}) collective-permute-start(f32[3,4,384]{2,1,0:T(4,128)S(1)} %get-tuple-element.27), channel_id=1, source_target_pairs={{16,32},{17,33},{18,34},{19,35},{20,36},{21,37},{22,38},{23,39},{2... | collective-permute-start | bytes 55304 | tf_op jit(solution)/shard_map/ppermute | solution.py:774
  16.2 0.0 collective-permute-done.from_one
  16.2 0.0 collective-permute-done.1.from_two
  16.3 0.7 %collective-permute-start.2 = (f32[3,4,256]{2,1,0:T(4,128)S(1)}, f32[3,4,256]{2,1,0:T(4,128)S(1)}, u32[]{:S(2)}, u32[]{:S(2)}) collective-permute-start(f32[3,4,256]{2,1,0:T(4,128)S(1)} %get-tuple-element.33), channel_id=1, source_target_pairs={{0,1},{1,0},{2,3},{3,2},{4,5},{5,4},{6,7},{7,6},{8,9},{9,8},{10,11... | collective-permute-start | bytes 36872 | tf_op jit(solution)/shard_map/ppermute | solution.py:774
  16.9 0.7 %collective-permute-start.3 = (f32[3,4,256]{2,1,0:T(4,128)S(1)}, f32[3,4,256]{2,1,0:T(4,128)S(1)}, u32[]{:S(2)}, u32[]{:S(2)}) collective-permute-start(f32[3,4,256]{2,1,0:T(4,128)S(1)} %get-tuple-element.34), channel_id=1, source_target_pairs={{1,2},{2,1},{3,4},{4,3},{5,6},{6,5},{7,8},{8,7},{9,10},{10,9},{11,... | collective-permute-start | bytes 36872 | tf_op jit(solution)/shard_map/ppermute | solution.py:774
  17.6 0.0 collective-permute-done.2.refs_5_
  17.6 0.0 collective-permute-done.3.refs_6_
  17.7 1.3 %collective-permute-start.7 = (f32[16,256]{1,0:T(8,128)S(1)}, f32[16,256]{1,0:T(8,128)S(1)}, u32[]{:S(2)}, u32[]{:S(2)}) collective-permute-start(f32[16,256]{1,0:T(8,128)S(1)} %get-tuple-element.36.sent_0), channel_id=1, source_target_pairs={{16,256},{17,257},{18,258},{19,259},{20,260},{21,261},{22,262},{23... | collective-permute-start | bytes 49160 | tf_op jit(solution)/shard_map/ppermute | solution.py:774
  19.0 1.3 %collective-permute-start.8 = (f32[16,256]{1,0:T(8,128)S(1)}, f32[16,256]{1,0:T(8,128)S(1)}, u32[]{:S(2)}, u32[]{:S(2)}) collective-permute-start(f32[16,256]{1,0:T(8,128)S(1)} %get-tuple-element.37.sent_1), channel_id=1, source_target_pairs={{0,256},{1,257},{2,258},{3,259},{4,260},{5,261},{6,262},{7,263},{8... | collective-permute-start | bytes 49160 | tf_op jit(solution)/shard_map/ppermute | solution.py:774
  20.3 0.0 collective-permute-done.6.mean_2
  20.3 1.3 %collective-permute-start.9 = (f32[16,256]{1,0:T(8,128)S(1)}, f32[16,256]{1,0:T(8,128)S(1)}, u32[]{:S(2)}, u32[]{:S(2)}) collective-permute-start(f32[16,256]{1,0:T(8,128)S(1)} %get-tuple-element.38.sent_2), channel_id=1, source_target_pairs={{0,272},{1,273},{2,274},{3,275},{4,276},{5,277},{6,278},{7,279},{8... | collective-permute-start | bytes 49160 | tf_op jit(solution)/shard_map/ppermute | solution.py:774
  21.6 0.0 collective-permute-done.5.mean_1
  21.6 0.0 collective-permute-done.4.mean_0
  21.6 0.1 parents.1.done
  21.7 11.4 %collective-permute-done.7.got_0 = f32[16,256]{1,0:T(8,128)S(1)} collective-permute-done((f32[16,256]{1,0:T(8,128)S(1)}, f32[16,256]{1,0:T(8,128)S(1)}, u32[]{:S(2)}, u32[]{:S(2)}) %collective-permute-start.7) | collective-permute-done | bytes 16416 | tf_op jit(solution)/shard_map/ppermute | solution.py:774
  33.1 1.1 %collective-permute-done.8.got_1 = f32[16,256]{1,0:T(8,128)S(1)} collective-permute-done((f32[16,256]{1,0:T(8,128)S(1)}, f32[16,256]{1,0:T(8,128)S(1)}, u32[]{:S(2)}, u32[]{:S(2)}) %collective-permute-start.8) | collective-permute-done | bytes 16416 | tf_op jit(solution)/shard_map/ppermute | solution.py:774
  34.2 5.9 %collective-permute-done.9.got_2 = f32[16,256]{1,0:T(8,128)S(1)} collective-permute-done((f32[16,256]{1,0:T(8,128)S(1)}, f32[16,256]{1,0:T(8,128)S(1)}, u32[]{:S(2)}, u32[]{:S(2)}) %collective-permute-start.9) | collective-permute-done | bytes 16416 | tf_op jit(solution)/shard_map/ppermute | solution.py:774
  40.0 1.8 %last.1 = f32[4,192,384]{2,1,0:T(8,128)} custom-call(f32[4,192,384]{2,1,0:T(8,128)} %parents.1.done, f32[16,640]{1,0:T(8,128)S(1)} %get-tuple-element.24.params, f32[4,192,384]{2,1,0:T(8,128)S(1)} %get-tuple-element.40.y, bf16[256,384]{1,0:T(8,128)(2,1)S(1)} %get-tuple-element.41.tent_row, ...), custom_call_target="tpu_custom_call", output_to_operand_aliasing={{}: (0, {})} | custom-call | tf_op jit(solution)/shard_map/last/pallas_call | solution.py:736
  (3 shorter events, 0.1 us)
Async XLA Ops:
  0.0 1.2 %copy-start.1 = (bf16[1,4,1,192,384]{4,3,2,1,0:T(8,128)(2,1)S(1)}, bf16[1,4,1,192,384]{4,3,2,1,0:T(8,128)(2,1)}, u32[]{:S(2)}) copy-start(bf16[1,4,1,192,384]{4,3,2,1,0:T(8,128)(2,1)} %param.6) | copy-start | bytes 1769476
  0.0 1.5 %copy-start = (f32[1,4,1,192,384]{4,3,2,1,0:T(8,128)S(1)}, f32[1,4,1,192,384]{4,3,2,1,0:T(8,128)}, u32[]{:S(2)}) copy-start(f32[1,4,1,192,384]{4,3,2,1,0:T(8,128)} %param.5) | copy-start | bytes 3538948
  5.0 15.3 %collective-permute-start.6 = (f32[4,64,128]{2,1,0:T(8,128)S(1)}, f32[4,64,128]{2,1,0:T(8,128)S(1)}, u32[]{:S(2)}, u32[]{:S(2)}) collective-permute-start(f32[4,64,128]{2,1,0:T(8,128)S(1)} %get-tuple-element.39), channel_id=1, source_target_pairs={{272,0},{273,1},{274,2},{275,3},{276,4},{277,5},{278,6},{279,7},{2... | collective-permute-start | bytes 393224 | tf_op jit(solution)/shard_map/ppermute | solution.py:774
  12.3 9.3 %collective-permute-start.5 = (f32[4,64,128]{2,1,0:T(8,128)S(1)}, f32[4,64,128]{2,1,0:T(8,128)S(1)}, u32[]{:S(2)}, u32[]{:S(2)}) collective-permute-start(f32[4,64,128]{2,1,0:T(8,128)S(1)} %get-tuple-element.39), channel_id=1, source_target_pairs={{256,0},{257,1},{258,2},{259,3},{260,4},{261,5},{262,6},{263,7},{2... | collective-permute-start | bytes 393224 | tf_op jit(solution)/shard_map/ppermute | solution.py:774
  13.6 8.0 %collective-permute-start.4 = (f32[4,64,128]{2,1,0:T(8,128)S(1)}, f32[4,64,128]{2,1,0:T(8,128)S(1)}, u32[]{:S(2)}, u32[]{:S(2)}) collective-permute-start(f32[4,64,128]{2,1,0:T(8,128)S(1)} %get-tuple-element.39), channel_id=1, source_target_pairs={{256,16},{257,17},{258,18},{259,19},{260,20},{261,21},{262,22},{26... | collective-permute-start | bytes 393224 | tf_op jit(solution)/shard_map/ppermute | solution.py:774
  14.9 1.3 %collective-permute-start = (f32[3,4,384]{2,1,0:T(4,128)S(1)}, f32[3,4,384]{2,1,0:T(4,128)S(1)}, u32[]{:S(2)}, u32[]{:S(2)}) collective-permute-start(f32[3,4,384]{2,1,0:T(4,128)S(1)} %get-tuple-element.26), channel_id=1, source_target_pairs={{0,16},{1,17},{2,18},{3,19},{4,20},{5,21},{6,22},{7,23},{8,24},{9,... | collective-permute-start | bytes 55304 | tf_op jit(solution)/shard_map/ppermute | solution.py:774
  15.6 0.7 %collective-permute-start.1 = (f32[3,4,384]{2,1,0:T(4,128)S(1)}, f32[3,4,384]{2,1,0:T(4,128)S(1)}, u32[]{:S(2)}, u32[]{:S(2)}) collective-permute-start(f32[3,4,384]{2,1,0:T(4,128)S(1)} %get-tuple-element.27), channel_id=1, source_target_pairs={{16,32},{17,33},{18,34},{19,35},{20,36},{21,37},{22,38},{23,39},{2... | collective-permute-start | bytes 55304 | tf_op jit(solution)/shard_map/ppermute | solution.py:774
  16.3 1.4 %collective-permute-start.2 = (f32[3,4,256]{2,1,0:T(4,128)S(1)}, f32[3,4,256]{2,1,0:T(4,128)S(1)}, u32[]{:S(2)}, u32[]{:S(2)}) collective-permute-start(f32[3,4,256]{2,1,0:T(4,128)S(1)} %get-tuple-element.33), channel_id=1, source_target_pairs={{0,1},{1,0},{2,3},{3,2},{4,5},{5,4},{6,7},{7,6},{8,9},{9,8},{10,11... | collective-permute-start | bytes 36872 | tf_op jit(solution)/shard_map/ppermute | solution.py:774
  16.9 0.7 %collective-permute-start.3 = (f32[3,4,256]{2,1,0:T(4,128)S(1)}, f32[3,4,256]{2,1,0:T(4,128)S(1)}, u32[]{:S(2)}, u32[]{:S(2)}) collective-permute-start(f32[3,4,256]{2,1,0:T(4,128)S(1)} %get-tuple-element.34), channel_id=1, source_target_pairs={{1,2},{2,1},{3,4},{4,3},{5,6},{6,5},{7,8},{8,7},{9,10},{10,9},{11,... | collective-permute-start | bytes 36872 | tf_op jit(solution)/shard_map/ppermute | solution.py:774
  17.7 15.4 %collective-permute-start.7 = (f32[16,256]{1,0:T(8,128)S(1)}, f32[16,256]{1,0:T(8,128)S(1)}, u32[]{:S(2)}, u32[]{:S(2)}) collective-permute-start(f32[16,256]{1,0:T(8,128)S(1)} %get-tuple-element.36.sent_0), channel_id=1, source_target_pairs={{16,256},{17,257},{18,258},{19,259},{20,260},{21,261},{22,262},{23... | collective-permute-start | bytes 49160 | tf_op jit(solution)/shard_map/ppermute | solution.py:774
  19.0 15.2 %collective-permute-start.8 = (f32[16,256]{1,0:T(8,128)S(1)}, f32[16,256]{1,0:T(8,128)S(1)}, u32[]{:S(2)}, u32[]{:S(2)}) collective-permute-start(f32[16,256]{1,0:T(8,128)S(1)} %get-tuple-element.37.sent_1), channel_id=1, source_target_pairs={{0,256},{1,257},{2,258},{3,259},{4,260},{5,261},{6,262},{7,263},{8... | collective-permute-start | bytes 49160 | tf_op jit(solution)/shard_map/ppermute | solution.py:774
  20.3 19.7 %collective-permute-start.9 = (f32[16,256]{1,0:T(8,128)S(1)}, f32[16,256]{1,0:T(8,128)S(1)}, u32[]{:S(2)}, u32[]{:S(2)}) collective-permute-start(f32[16,256]{1,0:T(8,128)S(1)} %get-tuple-element.38.sent_2), channel_id=1, source_target_pairs={{0,272},{1,273},{2,274},{3,275},{4,276},{5,277},{6,278},{7,279},{8... | collective-permute-start | bytes 49160 | tf_op jit(solution)/shard_map/ppermute | solution.py:774

commit v9 on v8

--- a/solution.py
+++ b/solution.py
@@ -29,6 +29,7 @@
 VMEM = pl.BlockSpec(memory_space=pltpu.VMEM)
 ANY = pl.BlockSpec(memory_space=pl.ANY)
 SMALL = pltpu.CompilerParams(vmem_limit_bytes=16 << 20)
+PACKED = pltpu.CompilerParams(vmem_limit_bytes=16 << 20)
 
 
 def iota(shape, dim):
@@ -347,7 +348,7 @@
             pltpu.VMEM((12, V, 256), F32),
             pltpu.VMEM((V, H, W), F32),
         ],
-        compiler_params=SMALL,
+        compiler_params=PACKED,
         name="banks",
     )(*near(params, x, drive, north, south))
 
@@ -659,17 +660,16 @@
             put_sides(tile, stepped, f, both)
             for member, (valid, at_row, at_col) in enumerate(patches):
                 up = member * n + f
-                patch = (
-                    means[member][f]
-                    + jnp.where(line == 0, by_row[up : up + 1], 0.0)
-                    + jnp.where(line == PH - 1, by_row[up + V : up + V + 1], 0.0)
-                    + jnp.where(lane == 0, by_col[:, up : up + 1], 0.0)
-                    + jnp.where(lane == PW - 1, by_col[:, up + V : up + V + 1], 0.0)
-                )
 
                 @pl.when(valid)
-                def _(at_row=at_row, at_col=at_col, patch=patch):
-                    tile[f, pl.ds(at_row, PH), pl.ds(at_col, PW)] = patch
+                def _(member=member, f=f, up=up, at_row=at_row, at_col=at_col):
+                    tile[f, pl.ds(at_row, PH), pl.ds(at_col, PW)] = (
+                        means[member][f]
+                        + jnp.where(line == 0, by_row[up : up + 1], 0.0)
+                        + jnp.where(line == PH - 1, by_row[up + V : up + V + 1], 0.0)
+                        + jnp.where(lane == 0, by_col[:, up : up + 1], 0.0)
+                        + jnp.where(lane == PW - 1, by_col[:, up + V : up + V + 1], 0.0)
+                    )
 
             send(f).start()
 
@@ -740,7 +740,7 @@
         out_shape=jax.ShapeDtypeStruct((V, H, W), F32),
         input_output_aliases={0: 0},
         scratch_shapes=[pltpu.VMEM((V, H, W), F32), pltpu.SemaphoreType.DMA((V,))],
-        compiler_params=SMALL,
+        compiler_params=PACKED,
         name="last",
     )(done, *near(*arrays))
 

time: 42.2 us -> 42.2 us (level)
  no operation moved by 1% of the time
where the time goes in v9:
time: 42.2 us; the launch traced here: 41.8 us
  waiting for transfers between devices  18.3 us (43%)
  starting transfers between devices  16.4 us (39%)
  Pallas kernels  6.52 us (15%)
    ppermute x10, waiting for transfers between devices, shift(): return lax.ppermute(value, AXES, routes(sizes, source, move))  18.3 us
    ppermute x10, starting transfers between devices, shift(): return lax.ppermute(value, AXES, routes(sizes, source, move))  16.4 us
    pallas_call x1, Pallas kernels, nests(): pl.pallas_call(nests_kernel, in_specs=[VMEM] * 3, out_specs=[VMEM] * 5, o...  3.41 us
    pallas_call x1, Pallas kernels, last(): pl.pallas_call(last_kernel, in_specs=[ANY] + [VMEM] * 7, out_specs=ANY, o...  1.83 us
    pallas_call x1, Pallas kernels, edge(): pl.pallas_call(edge_kernel, in_specs=[ANY] * 5, out_specs=[VMEM] * 3, out...  1.16 us
  transfers between devices with their start and end apart: 10, of which 3 were waited for; matrix products, arithmetic and copies ran while one was open for 0% of the time, Pallas kernels for 0%

profile of v9, /device:TPU:102, one launch (start us, length us, event | category | flops | bytes accessed | tf_op | source)
XLA Modules:
  0.0 41.8 jit_solution(4458357709321149180)
XLA Ops:
  0.0 0.0 copy-start.1
  0.0 0.0 copy-start
  0.0 1.2 %edge.1 = (f32[3,4,384]{2,1,0:T(4,128)S(1)}, f32[3,4,384]{2,1,0:T(4,128)S(1)}, f32[16,640]{1,0:T(8,128)S(1)}) custom-call(f32[4,192,384]{2,1,0:T(8,128)} %bitcast.6, bf16[4,192,384]{2,1,0:T(8,128)(2,1)} %bitcast.9, f32[2]{0:T(128)} %bitcast.12, f32[4]{0:T(128)} %diffusion.1, s32[16,16]{1,0:T(8,128)} %nest_patch.3), custom_call_target="tpu_custom_call" | custom-call | tf_op jit(solution)/shard_map/edge/pallas_call | solution.py:188
  1.2 0.0 copy-done.1
  1.2 0.4 copy-done
  1.6 3.4 %nests.1 = (f32[4,192,384]{2,1,0:T(8,128)S(1)}, f32[4,64,128]{2,1,0:T(8,128)S(1)}, f32[6,4,256]{2,1,0:T(4,128)S(1)}, bf16[256,384]{1,0:T(8,128)(2,1)S(1)}, bf16[192,256]{1,0:T(8,128)(2,1)S(1)}) custom-call(f32[16,640]{1,0:T(8,128)S(1)} %get-tuple-element.24.params, f32[4,192,384]{2,1,0:T(8,128)S(1)} %bitcast.7, bf16[4,192,384]{2,1,0:T(8,128)(2,1)S(1)} %bitcast.10), custom_call_target="tpu_custom_call" | custom-call | tf_op jit(solution)/shard_map/nests/pallas_call | solution.py:295
  5.0 7.3 %collective-permute-start.6 = (f32[4,64,128]{2,1,0:T(8,128)S(1)}, f32[4,64,128]{2,1,0:T(8,128)S(1)}, u32[]{:S(2)}, u32[]{:S(2)}) collective-permute-start(f32[4,64,128]{2,1,0:T(8,128)S(1)} %get-tuple-element.39), channel_id=1, source_target_pairs={{272,0},{273,1},{274,2},{275,3},{276,4},{277,5},{278,6},{279,7},{2... | collective-permute-start | bytes 393224 | tf_op jit(solution)/shard_map/ppermute | solution.py:774
  12.3 1.3 %collective-permute-start.5 = (f32[4,64,128]{2,1,0:T(8,128)S(1)}, f32[4,64,128]{2,1,0:T(8,128)S(1)}, u32[]{:S(2)}, u32[]{:S(2)}) collective-permute-start(f32[4,64,128]{2,1,0:T(8,128)S(1)} %get-tuple-element.39), channel_id=1, source_target_pairs={{256,0},{257,1},{258,2},{259,3},{260,4},{261,5},{262,6},{263,7},{2... | collective-permute-start | bytes 393224 | tf_op jit(solution)/shard_map/ppermute | solution.py:774
  13.6 1.3 %collective-permute-start.4 = (f32[4,64,128]{2,1,0:T(8,128)S(1)}, f32[4,64,128]{2,1,0:T(8,128)S(1)}, u32[]{:S(2)}, u32[]{:S(2)}) collective-permute-start(f32[4,64,128]{2,1,0:T(8,128)S(1)} %get-tuple-element.39), channel_id=1, source_target_pairs={{256,16},{257,17},{258,18},{259,19},{260,20},{261,21},{262,22},{26... | collective-permute-start | bytes 393224 | tf_op jit(solution)/shard_map/ppermute | solution.py:774
  14.9 0.7 %collective-permute-start = (f32[3,4,384]{2,1,0:T(4,128)S(1)}, f32[3,4,384]{2,1,0:T(4,128)S(1)}, u32[]{:S(2)}, u32[]{:S(2)}) collective-permute-start(f32[3,4,384]{2,1,0:T(4,128)S(1)} %get-tuple-element.26), channel_id=1, source_target_pairs={{0,16},{1,17},{2,18},{3,19},{4,20},{5,21},{6,22},{7,23},{8,24},{9,... | collective-permute-start | bytes 55304 | tf_op jit(solution)/shard_map/ppermute | solution.py:774
  15.6 0.7 %collective-permute-start.1 = (f32[3,4,384]{2,1,0:T(4,128)S(1)}, f32[3,4,384]{2,1,0:T(4,128)S(1)}, u32[]{:S(2)}, u32[]{:S(2)}) collective-permute-start(f32[3,4,384]{2,1,0:T(4,128)S(1)} %get-tuple-element.27), channel_id=1, source_target_pairs={{16,32},{17,33},{18,34},{19,35},{20,36},{21,37},{22,38},{23,39},{2... | collective-permute-start | bytes 55304 | tf_op jit(solution)/shard_map/ppermute | solution.py:774
  16.2 0.0 collective-permute-done.from_one
  16.2 0.0 collective-permute-done.1.from_two
  16.3 0.7 %collective-permute-start.2 = (f32[3,4,256]{2,1,0:T(4,128)S(1)}, f32[3,4,256]{2,1,0:T(4,128)S(1)}, u32[]{:S(2)}, u32[]{:S(2)}) collective-permute-start(f32[3,4,256]{2,1,0:T(4,128)S(1)} %get-tuple-element.33), channel_id=1, source_target_pairs={{0,1},{1,0},{2,3},{3,2},{4,5},{5,4},{6,7},{7,6},{8,9},{9,8},{10,11... | collective-permute-start | bytes 36872 | tf_op jit(solution)/shard_map/ppermute | solution.py:774
  16.9 0.7 %collective-permute-start.3 = (f32[3,4,256]{2,1,0:T(4,128)S(1)}, f32[3,4,256]{2,1,0:T(4,128)S(1)}, u32[]{:S(2)}, u32[]{:S(2)}) collective-permute-start(f32[3,4,256]{2,1,0:T(4,128)S(1)} %get-tuple-element.34), channel_id=1, source_target_pairs={{1,2},{2,1},{3,4},{4,3},{5,6},{6,5},{7,8},{8,7},{9,10},{10,9},{11,... | collective-permute-start | bytes 36872 | tf_op jit(solution)/shard_map/ppermute | solution.py:774
  17.6 0.0 collective-permute-done.2.refs_5_
  17.6 0.0 collective-permute-done.3.refs_6_
  17.7 1.3 %collective-permute-start.7 = (f32[16,256]{1,0:T(8,128)S(1)}, f32[16,256]{1,0:T(8,128)S(1)}, u32[]{:S(2)}, u32[]{:S(2)}) collective-permute-start(f32[16,256]{1,0:T(8,128)S(1)} %get-tuple-element.36.sent_0), channel_id=1, source_target_pairs={{16,256},{17,257},{18,258},{19,259},{20,260},{21,261},{22,262},{23... | collective-permute-start | bytes 49160 | tf_op jit(solution)/shard_map/ppermute | solution.py:774
  19.0 1.3 %collective-permute-start.8 = (f32[16,256]{1,0:T(8,128)S(1)}, f32[16,256]{1,0:T(8,128)S(1)}, u32[]{:S(2)}, u32[]{:S(2)}) collective-permute-start(f32[16,256]{1,0:T(8,128)S(1)} %get-tuple-element.37.sent_1), channel_id=1, source_target_pairs={{0,256},{1,257},{2,258},{3,259},{4,260},{5,261},{6,262},{7,263},{8... | collective-permute-start | bytes 49160 | tf_op jit(solution)/shard_map/ppermute | solution.py:774
  20.3 0.0 collective-permute-done.6.mean_2
  20.3 1.3 %collective-permute-start.9 = (f32[16,256]{1,0:T(8,128)S(1)}, f32[16,256]{1,0:T(8,128)S(1)}, u32[]{:S(2)}, u32[]{:S(2)}) collective-permute-start(f32[16,256]{1,0:T(8,128)S(1)} %get-tuple-element.38.sent_2), channel_id=1, source_target_pairs={{0,272},{1,273},{2,274},{3,275},{4,276},{5,277},{6,278},{7,279},{8... | collective-permute-start | bytes 49160 | tf_op jit(solution)/shard_map/ppermute | solution.py:774
  21.6 0.0 collective-permute-done.5.mean_1
  21.6 0.0 collective-permute-done.4.mean_0
  21.6 0.1 parents.1.done
  21.7 11.4 %collective-permute-done.7.got_0 = f32[16,256]{1,0:T(8,128)S(1)} collective-permute-done((f32[16,256]{1,0:T(8,128)S(1)}, f32[16,256]{1,0:T(8,128)S(1)}, u32[]{:S(2)}, u32[]{:S(2)}) %collective-permute-start.7) | collective-permute-done | bytes 16416 | tf_op jit(solution)/shard_map/ppermute | solution.py:774
  33.1 1.1 %collective-permute-done.8.got_1 = f32[16,256]{1,0:T(8,128)S(1)} collective-permute-done((f32[16,256]{1,0:T(8,128)S(1)}, f32[16,256]{1,0:T(8,128)S(1)}, u32[]{:S(2)}, u32[]{:S(2)}) %collective-permute-start.8) | collective-permute-done | bytes 16416 | tf_op jit(solution)/shard_map/ppermute | solution.py:774
  34.2 5.9 %collective-permute-done.9.got_2 = f32[16,256]{1,0:T(8,128)S(1)} collective-permute-done((f32[16,256]{1,0:T(8,128)S(1)}, f32[16,256]{1,0:T(8,128)S(1)}, u32[]{:S(2)}, u32[]{:S(2)}) %collective-permute-start.9) | collective-permute-done | bytes 16416 | tf_op jit(solution)/shard_map/ppermute | solution.py:774
  40.0 1.8 %last.1 = f32[4,192,384]{2,1,0:T(8,128)} custom-call(f32[4,192,384]{2,1,0:T(8,128)} %parents.1.done, f32[16,640]{1,0:T(8,128)S(1)} %get-tuple-element.24.params, f32[4,192,384]{2,1,0:T(8,128)S(1)} %get-tuple-element.40.y, bf16[256,384]{1,0:T(8,128)(2,1)S(1)} %get-tuple-element.41.tent_row, ...), custom_call_target="tpu_custom_call", output_to_operand_aliasing={{}: (0, {})} | custom-call | tf_op jit(solution)/shard_map/last/pallas_call | solution.py:736
  (3 shorter events, 0.1 us)
Async XLA Ops:
  0.0 1.2 %copy-start.1 = (bf16[1,4,1,192,384]{4,3,2,1,0:T(8,128)(2,1)S(1)}, bf16[1,4,1,192,384]{4,3,2,1,0:T(8,128)(2,1)}, u32[]{:S(2)}) copy-start(bf16[1,4,1,192,384]{4,3,2,1,0:T(8,128)(2,1)} %param.6) | copy-start | bytes 1769476
  0.0 1.5 %copy-start = (f32[1,4,1,192,384]{4,3,2,1,0:T(8,128)S(1)}, f32[1,4,1,192,384]{4,3,2,1,0:T(8,128)}, u32[]{:S(2)}) copy-start(f32[1,4,1,192,384]{4,3,2,1,0:T(8,128)} %param.5) | copy-start | bytes 3538948
  5.0 15.3 %collective-permute-start.6 = (f32[4,64,128]{2,1,0:T(8,128)S(1)}, f32[4,64,128]{2,1,0:T(8,128)S(1)}, u32[]{:S(2)}, u32[]{:S(2)}) collective-permute-start(f32[4,64,128]{2,1,0:T(8,128)S(1)} %get-tuple-element.39), channel_id=1, source_target_pairs={{272,0},{273,1},{274,2},{275,3},{276,4},{277,5},{278,6},{279,7},{2... | collective-permute-start | bytes 393224 | tf_op jit(solution)/shard_map/ppermute | solution.py:774
  12.3 9.3 %collective-permute-start.5 = (f32[4,64,128]{2,1,0:T(8,128)S(1)}, f32[4,64,128]{2,1,0:T(8,128)S(1)}, u32[]{:S(2)}, u32[]{:S(2)}) collective-permute-start(f32[4,64,128]{2,1,0:T(8,128)S(1)} %get-tuple-element.39), channel_id=1, source_target_pairs={{256,0},{257,1},{258,2},{259,3},{260,4},{261,5},{262,6},{263,7},{2... | collective-permute-start | bytes 393224 | tf_op jit(solution)/shard_map/ppermute | solution.py:774
  13.6 8.0 %collective-permute-start.4 = (f32[4,64,128]{2,1,0:T(8,128)S(1)}, f32[4,64,128]{2,1,0:T(8,128)S(1)}, u32[]{:S(2)}, u32[]{:S(2)}) collective-permute-start(f32[4,64,128]{2,1,0:T(8,128)S(1)} %get-tuple-element.39), channel_id=1, source_target_pairs={{256,16},{257,17},{258,18},{259,19},{260,20},{261,21},{262,22},{26... | collective-permute-start | bytes 393224 | tf_op jit(solution)/shard_map/ppermute | solution.py:774
  14.9 1.3 %collective-permute-start = (f32[3,4,384]{2,1,0:T(4,128)S(1)}, f32[3,4,384]{2,1,0:T(4,128)S(1)}, u32[]{:S(2)}, u32[]{:S(2)}) collective-permute-start(f32[3,4,384]{2,1,0:T(4,128)S(1)} %get-tuple-element.26), channel_id=1, source_target_pairs={{0,16},{1,17},{2,18},{3,19},{4,20},{5,21},{6,22},{7,23},{8,24},{9,... | collective-permute-start | bytes 55304 | tf_op jit(solution)/shard_map/ppermute | solution.py:774
  15.6 0.7 %collective-permute-start.1 = (f32[3,4,384]{2,1,0:T(4,128)S(1)}, f32[3,4,384]{2,1,0:T(4,128)S(1)}, u32[]{:S(2)}, u32[]{:S(2)}) collective-permute-start(f32[3,4,384]{2,1,0:T(4,128)S(1)} %get-tuple-element.27), channel_id=1, source_target_pairs={{16,32},{17,33},{18,34},{19,35},{20,36},{21,37},{22,38},{23,39},{2... | collective-permute-start | bytes 55304 | tf_op jit(solution)/shard_map/ppermute | solution.py:774
  16.3 1.4 %collective-permute-start.2 = (f32[3,4,256]{2,1,0:T(4,128)S(1)}, f32[3,4,256]{2,1,0:T(4,128)S(1)}, u32[]{:S(2)}, u32[]{:S(2)}) collective-permute-start(f32[3,4,256]{2,1,0:T(4,128)S(1)} %get-tuple-element.33), channel_id=1, source_target_pairs={{0,1},{1,0},{2,3},{3,2},{4,5},{5,4},{6,7},{7,6},{8,9},{9,8},{10,11... | collective-permute-start | bytes 36872 | tf_op jit(solution)/shard_map/ppermute | solution.py:774
  16.9 0.7 %collective-permute-start.3 = (f32[3,4,256]{2,1,0:T(4,128)S(1)}, f32[3,4,256]{2,1,0:T(4,128)S(1)}, u32[]{:S(2)}, u32[]{:S(2)}) collective-permute-start(f32[3,4,256]{2,1,0:T(4,128)S(1)} %get-tuple-element.34), channel_id=1, source_target_pairs={{1,2},{2,1},{3,4},{4,3},{5,6},{6,5},{7,8},{8,7},{9,10},{10,9},{11,... | collective-permute-start | bytes 36872 | tf_op jit(solution)/shard_map/ppermute | solution.py:774
  17.7 15.4 %collective-permute-start.7 = (f32[16,256]{1,0:T(8,128)S(1)}, f32[16,256]{1,0:T(8,128)S(1)}, u32[]{:S(2)}, u32[]{:S(2)}) collective-permute-start(f32[16,256]{1,0:T(8,128)S(1)} %get-tuple-element.36.sent_0), channel_id=1, source_target_pairs={{16,256},{17,257},{18,258},{19,259},{20,260},{21,261},{22,262},{23... | collective-permute-start | bytes 49160 | tf_op jit(solution)/shard_map/ppermute | solution.py:774
  19.0 15.2 %collective-permute-start.8 = (f32[16,256]{1,0:T(8,128)S(1)}, f32[16,256]{1,0:T(8,128)S(1)}, u32[]{:S(2)}, u32[]{:S(2)}) collective-permute-start(f32[16,256]{1,0:T(8,128)S(1)} %get-tuple-element.37.sent_1), channel_id=1, source_target_pairs={{0,256},{1,257},{2,258},{3,259},{4,260},{5,261},{6,262},{7,263},{8... | collective-permute-start | bytes 49160 | tf_op jit(solution)/shard_map/ppermute | solution.py:774
  20.3 19.7 %collective-permute-start.9 = (f32[16,256]{1,0:T(8,128)S(1)}, f32[16,256]{1,0:T(8,128)S(1)}, u32[]{:S(2)}, u32[]{:S(2)}) collective-permute-start(f32[16,256]{1,0:T(8,128)S(1)} %get-tuple-element.38.sent_2), channel_id=1, source_target_pairs={{0,272},{1,273},{2,274},{3,275},{4,276},{5,277},{6,278},{7,279},{8... | collective-permute-start | bytes 49160 | tf_op jit(solution)/shard_map/ppermute | solution.py:774
